TPU v7x, 32 devices: a whole 2x2x4 slice. The times are simulated.
32 devices in a mesh: img: 4 (over z), cap: 8 (over y, x, core).
Axes of the slice: x: 2, y: 2, z: 4, core: 2. Of those that a mesh axis runs over, the one named last changes fastest.
Arguments:
- patches: bfloat16 [128, 256, 768], P(('img', 'cap')), may hold values from -32 to 32
- words: bfloat16 [128, 64, 768], P(('img', 'cap')), may hold values from -4.5 to 4.5
- natural_sharpness_exponent: float32 [1], replicated, may hold values from 2.3 to 3.9
- candidates: int32 [4, 8, 6], replicated, may hold values from -1 to 7, as said below
- counts: int32 [4, 8], replicated, may hold values from 3 to 6, as said below
Outputs:
- patch_grad: bfloat16 [128, 256, 768], P(('img', 'cap'))
- word_grad: bfloat16 [128, 64, 768], P(('img', 'cap'))
- loss: float32 [1], replicated
- temp_grad: float32 [1], replicated
Inputs may be any that keep to these rules, and one draw needn't show every extreme that they name: `candidates`: entry [a, b, 0] is b; entries 1 to counts[a, b] - 1 are distinct columns other than b; later entries are -1. `counts`: some image block has exactly 6 candidate blocks.
All inputs are finite; a program needn't handle non-finite values.
Results may differ from a plain program's by a relative error of at most 0.0085.
Values may be sent and summed in bfloat16 or wider, within the bound.
No kernel may reach another device: no remote copies, remote signals or barrier semaphores. Data moves between devices by JAX's collectives and lax.ppermute only.
A program may use at most 128 MiB of HBM per device.

v0:
```python
import jax
import jax.numpy as jnp
from jax import lax
from jax.sharding import PartitionSpec as P

D = 768
P_SIZE = 256
W = 64


sharpness = 4.0
loss_scale = 65536.0
far_below = -1e30


def similarity_table(patch_block, word_tile_block):
    product = jnp.einsum(
        "ipd,jwd->ijwp", patch_block, word_tile_block, preferred_element_type=jnp.float32
    )
    return product * D ** (-0.5)


def couple_similarity_lines(linear_shift_map):
    lifted = sharpness * linear_shift_map
    over_words = jax.nn.logsumexp(lifted, axis=2) / sharpness
    over_patches = jax.nn.logsumexp(lifted, axis=3) / sharpness
    return 0.5 * (jnp.mean(over_words, axis=2) + jnp.mean(over_patches, axis=2))


def token_weights(linear_shift_map, couple_derivative):
    lifted = sharpness * linear_shift_map
    share_words = jax.nn.softmax(lifted, axis=2)
    share_patches = jax.nn.softmax(lifted, axis=3)
    blended = 0.5 * (share_words / P_SIZE + share_patches / W)
    return (blended * (couple_derivative[:, :, None, None] * (loss_scale * D ** (-0.5)))).astype(
        jnp.bfloat16
    )


def body(patches, words, natural_sharpness_exponent, candidates, counts):
    cycle_size = lax.axis_size("cap")
    row_total = lax.axis_size("img")
    row_index = lax.axis_index("img")
    column_index = lax.axis_index("cap")
    per_device = patches.shape[0]
    slot_total = candidates.shape[2]
    images = per_device * row_total * cycle_size
    trained_softness = jnp.exp(natural_sharpness_exponent[0])
    row_cands = lax.dynamic_index_in_dim(candidates, row_index, 0, keepdims=False)
    row_counts = lax.dynamic_index_in_dim(counts, row_index, 0, keepdims=False)
    own_cands = lax.dynamic_index_in_dim(row_cands, column_index, 0, keepdims=False)
    own_count = lax.dynamic_index_in_dim(row_counts, column_index, 0, keepdims=False)
    slot_ids = jnp.arange(slot_total, dtype=jnp.int32)
    block_ids = jnp.arange(cycle_size, dtype=jnp.int32)
    own_live = slot_ids < own_count
    slot_hits = (own_cands[:, None] == block_ids[None, :]) & own_live[:, None]
    block_live = jnp.any(slot_hits, axis=0)
    identity_rows = jnp.eye(per_device, dtype=jnp.float32)
    all_words = lax.all_gather(words, "cap", axis=0, tiled=True)
    word_blocks = all_words.reshape(cycle_size, per_device, W, D)

    def forward_slot(slot_index, logit_table):
        column = jnp.maximum(own_cands[slot_index], 0)

        def score_block(current):
            word_tile_block = lax.dynamic_index_in_dim(word_blocks, column, 0, keepdims=False)
            element_amounts = trained_softness * couple_similarity_lines(
                similarity_table(patches, word_tile_block)
            )
            return lax.dynamic_update_index_in_dim(current, element_amounts, column, 1)

        return lax.cond(own_live[slot_index], score_block, lambda current: current, logit_table)

    logits = lax.fori_loop(
        0, slot_total, forward_slot, jnp.zeros((per_device, cycle_size, per_device), jnp.float32)
    )
    live_mask = block_live[None, :, None]
    masked = jnp.where(live_mask, logits, far_below)
    row_lse = jax.nn.logsumexp(masked, axis=(1, 2))
    column_peak = jnp.max(masked, axis=0)
    peak_all = lax.pmax(column_peak, "cap")
    column_mass = jnp.sum(jnp.where(live_mask, jnp.exp(masked - peak_all[None]), 0.0), axis=0)
    mass_all = lax.psum(column_mass, "cap")
    col_lse = peak_all + jnp.log(mass_all)
    positive = jnp.where(block_ids[None, :, None] == column_index, identity_rows[:, None, :], 0.0)
    couple_derivative = jnp.where(
        live_mask,
        0.5
        / images
        * (
            jnp.exp(masked - row_lse[:, None, None])
            + jnp.exp(masked - col_lse[None])
            - 2.0 * positive
        ),
        0.0,
    )
    own_lse = lax.dynamic_index_in_dim(col_lse, column_index, 0, keepdims=False)
    diagonal = jnp.sum(logits * positive)
    loss_part = 0.5 * (jnp.sum(row_lse) + jnp.sum(own_lse) - 2.0 * diagonal) / images
    temp_part = jnp.sum(couple_derivative * logits)
    loss_total, temp_total = lax.psum((loss_part, temp_part), ("img", "cap"))
    similarity_derivative = trained_softness * couple_derivative
    stored_init = None

    def patch_slot(slot_index, state):
        column = jnp.maximum(own_cands[slot_index], 0)

        def patch_compute(current):
            running, stored = current
            word_tile_block = lax.dynamic_index_in_dim(word_blocks, column, 0, keepdims=False)
            derivative_group_piece = lax.dynamic_index_in_dim(
                similarity_derivative, column, 1, keepdims=False
            )
            weights = token_weights(
                similarity_table(patches, word_tile_block), derivative_group_piece
            )
            running = running + jnp.einsum(
                "ijwp,jwd->ipd", weights, word_tile_block, preferred_element_type=jnp.float32
            )
            return (running, stored)

        return lax.cond(own_live[slot_index], patch_compute, lambda current: current, state)

    patch_total, unused_store = lax.fori_loop(
        0, slot_total, patch_slot, (jnp.zeros(patches.shape, jnp.float32), stored_init)
    )
    lse_rows = lax.all_gather(row_lse, "cap", axis=0, tiled=True)
    piece = lax.all_gather(patches, "cap", axis=0, tiled=True)
    number = piece.shape[0] // per_device

    def add_block(offset, running):
        source_cands = lax.dynamic_index_in_dim(row_cands, offset, 0, keepdims=False)
        source_count = lax.dynamic_index_in_dim(row_counts, offset, 0, keepdims=False)
        wanted = jnp.any((source_cands == column_index) & (slot_ids < source_count))

        def add_compute(partial_value):
            patch_block = lax.dynamic_slice_in_dim(piece, offset * per_device, per_device, 0)
            lse_block = lax.dynamic_slice_in_dim(lse_rows, offset * per_device, per_device, 0)
            linear_shift_map = similarity_table(patch_block, words)
            element_amounts = trained_softness * couple_similarity_lines(linear_shift_map)
            positive_rows = jnp.where(offset == column_index, identity_rows, 0.0)
            derivative_group_piece = trained_softness * (
                0.5
                / images
                * (
                    jnp.exp(element_amounts - lse_block[:, None])
                    + jnp.exp(element_amounts - own_lse[None, :])
                    - 2.0 * positive_rows
                )
            )
            weights = token_weights(linear_shift_map, derivative_group_piece)
            return partial_value + jnp.einsum(
                "ijwp,ipd->jwd", weights, patch_block, preferred_element_type=jnp.float32
            )

        return lax.cond(wanted, add_compute, lambda partial_value: partial_value, running)

    word_total = lax.fori_loop(0, number, add_block, jnp.zeros(words.shape, jnp.float32))
    return (
        patch_total.astype(jnp.bfloat16),
        word_total.astype(jnp.bfloat16),
        loss_total.reshape(1),
        temp_total.reshape(1),
    )


def solution(mesh):
    placed = (P(("img", "cap"), None, None), P(("img", "cap"), None, None), P(), P(), P())
    return jax.shard_map(
        body,
        mesh=mesh,
        in_specs=placed,
        out_specs=(P(("img", "cap"), None, None), P(("img", "cap"), None, None), P(), P()),
        check_vma=False,
    )
```

profile of v0, /device:TPU:17, one launch (start us, length us, event | category | flops | bytes accessed | tf_op | source)
XLA Modules:
  0.0 293.6 jit_solution(17989215401121480159)
XLA Ops:
  14.4 29.4 %all-gather.3.cloned.1.call-done = bf16[32,64,768]{2,1,0:T(8,128)(2,1)} async-done(((bf16[4,64,768]{2,1,0:T(8,128)(2,1)}), bf16[32,64,768]{2,1,0:T(8,128)(2,1)}) %all-gather.3.cloned.1.call-update) | async-done | bytes 3145744 | tf_op jit(solution)/shard_map/all_gather | solution.py:59
  43.7 35.0 %while.49 = (s32[]{:T(128)}, f32[4,8,4]{2,0,1:T(4,128)S(1)}, pred[6]{0:T(512)(128)(4,1)S(1)}, s32[6]{0:T(128)S(1)}, bf16[8,4,64,768]{3,2,1,0:T(8,128)(2,1)}, /*i...) while((s32[]{:T(128)}, f32[4,8,4]{2,0,1:T(4,128)S(1)}, pred[6]{0:T(512)(128)(4,1)S(1)}, ...), condition=%wide.region_10.11_spmd, body=%wide.region_1.10_spmd.sunk | while | flops 404518976 | bytes 4211844 | solution.py:74
  45.0 4.5 %conditional.7 = (f32[4,8,4]{2,0,1:T(4,128)S(1)}) conditional(s32[]{:T(128)} %bitcast.98, f32[4,8,4]{2,0,1:T(4,128)S(1)} %get-tuple-element.823, (s32[6]{0:T(128)S(1)}, s32[]{:T(128)}, bf16[8,4,64,768]{3,2,1,0:T(8,128)(2,1)}, bf16[4,256,768]{2,1,0:T(8,128)(2,1)}, f32[]{:T(128)}, /*index=5*/f32[4,8,4]{2,0,1:T(4,128)S(1)}) %tuple.130), branch_computations={%region_2.2_spmd, %region_3.9_spmd} | conditional | flops 404518976 | bytes 4211700 | solution.py:72
  46.2 2.2 fusion.100
  50.8 4.8 %conditional.7 = (f32[4,8,4]{2,0,1:T(4,128)S(1)}) conditional(s32[]{:T(128)} %bitcast.98, f32[4,8,4]{2,0,1:T(4,128)S(1)} %get-tuple-element.823, (s32[6]{0:T(128)S(1)}, s32[]{:T(128)}, bf16[8,4,64,768]{3,2,1,0:T(8,128)(2,1)}, bf16[4,256,768]{2,1,0:T(8,128)(2,1)}, f32[]{:T(128)}, /*index=5*/f32[4,8,4]{2,0,1:T(4,128)S(1)}) %tuple.130), branch_computations={%region_2.2_spmd, %region_3.9_spmd} | conditional | flops 404518976 | bytes 4211700 | solution.py:72
  52.0 2.5 fusion.100
  56.8 4.5 %conditional.7 = (f32[4,8,4]{2,0,1:T(4,128)S(1)}) conditional(s32[]{:T(128)} %bitcast.98, f32[4,8,4]{2,0,1:T(4,128)S(1)} %get-tuple-element.823, (s32[6]{0:T(128)S(1)}, s32[]{:T(128)}, bf16[8,4,64,768]{3,2,1,0:T(8,128)(2,1)}, bf16[4,256,768]{2,1,0:T(8,128)(2,1)}, f32[]{:T(128)}, /*index=5*/f32[4,8,4]{2,0,1:T(4,128)S(1)}) %tuple.130), branch_computations={%region_2.2_spmd, %region_3.9_spmd} | conditional | flops 404518976 | bytes 4211700 | solution.py:72
  58.1 2.2 fusion.100
  62.6 4.5 %conditional.7 = (f32[4,8,4]{2,0,1:T(4,128)S(1)}) conditional(s32[]{:T(128)} %bitcast.98, f32[4,8,4]{2,0,1:T(4,128)S(1)} %get-tuple-element.823, (s32[6]{0:T(128)S(1)}, s32[]{:T(128)}, bf16[8,4,64,768]{3,2,1,0:T(8,128)(2,1)}, bf16[4,256,768]{2,1,0:T(8,128)(2,1)}, f32[]{:T(128)}, /*index=5*/f32[4,8,4]{2,0,1:T(4,128)S(1)}) %tuple.130), branch_computations={%region_2.2_spmd, %region_3.9_spmd} | conditional | flops 404518976 | bytes 4211700 | solution.py:72
  63.9 2.2 fusion.100
  68.4 4.5 %conditional.7 = (f32[4,8,4]{2,0,1:T(4,128)S(1)}) conditional(s32[]{:T(128)} %bitcast.98, f32[4,8,4]{2,0,1:T(4,128)S(1)} %get-tuple-element.823, (s32[6]{0:T(128)S(1)}, s32[]{:T(128)}, bf16[8,4,64,768]{3,2,1,0:T(8,128)(2,1)}, bf16[4,256,768]{2,1,0:T(8,128)(2,1)}, f32[]{:T(128)}, /*index=5*/f32[4,8,4]{2,0,1:T(4,128)S(1)}) %tuple.130), branch_computations={%region_2.2_spmd, %region_3.9_spmd} | conditional | flops 404518976 | bytes 4211700 | solution.py:72
  69.7 2.2 fusion.100
  74.2 4.5 %conditional.7 = (f32[4,8,4]{2,0,1:T(4,128)S(1)}) conditional(s32[]{:T(128)} %bitcast.98, f32[4,8,4]{2,0,1:T(4,128)S(1)} %get-tuple-element.823, (s32[6]{0:T(128)S(1)}, s32[]{:T(128)}, bf16[8,4,64,768]{3,2,1,0:T(8,128)(2,1)}, bf16[4,256,768]{2,1,0:T(8,128)(2,1)}, f32[]{:T(128)}, /*index=5*/f32[4,8,4]{2,0,1:T(4,128)S(1)}) %tuple.130), branch_computations={%region_2.2_spmd, %region_3.9_spmd} | conditional | flops 404518976 | bytes 4211700 | solution.py:72
  75.5 2.2 fusion.100
  80.0 11.7 %pmax.7 = f32[8,4]{1,0:T(8,128)S(1)} all-reduce(f32[8,4]{1,0:T(8,128)S(1)} %get-tuple-element.605), channel_id=1, replica_groups=mesh['img'=4,'cap'=8] {'cap'}, use_global_device_ids=true, to_apply=%region_14.15 | all-reduce | flops 32 | bytes 256 | tf_op jit(solution)/shard_map/pmax | solution.py:81
  91.8 12.8 %all-reduce.2 = (f32[8,4]{1,0:T(8,128)S(1)}, f32[32]{0:T(128)S(1)}) all-reduce(f32[8,4]{1,0:T(8,128)S(1)} %select_reduce_fusion, f32[32]{0:T(128)S(1)} %dynamic-update-slice), channel_id=1, replica_groups=mesh['img'=4,'cap'=8] {'cap'}, use_global_device_ids=true, to_apply=%region_16.17 | all-reduce | flops 64 | bytes 512 | tf_op jit(solution)/shard_map/psum | solution.py:83
  107.9 40.2 %all-reduce.1 = (f32[1]{0:T(128)}, f32[1]{0:T(128)}) all-reduce(f32[1]{0:T(128)} %bitcast.29, f32[1]{0:T(128)} %bitcast.30), channel_id=1, replica_groups=mesh['img'=4,'cap'=8] {'img','cap'}, use_global_device_ids=true, to_apply=%region_41.42 | all-reduce | flops 2 | bytes 16 | tf_op jit(solution)/shard_map/psum | solution.py:101
  148.1 1.9 broadcast_in_dim.57
  150.1 63.3 %while.50 = (s32[]{:T(128)}, f32[4,256,768]{2,1,0:T(8,128)}, pred[6]{0:T(512)(128)(4,1)S(1)}, s32[6]{0:T(128)S(1)}, bf16[8,4,64,768]{3,2,1,0:T(8,128)(2,1)}, /*i...) while((s32[]{:T(128)}, f32[4,256,768]{2,1,0:T(8,128)}, ...), condition=%wide.region_24.25_spmd, body=%wide.region_17.24_spmd.sunk | while | flops 808725120 | bytes 14945716 | solution.py:124
  151.3 9.3 %conditional.8 = (f32[4,256,768]{2,1,0:T(8,128)}) conditional(s32[]{:T(128)} %bitcast.99, f32[4,256,768]{2,1,0:T(8,128)} %get-tuple-element.847, (s32[6]{0:T(128)S(1)}, s32[]{:T(128)}, bf16[8,4,64,768]{3,2,1,0:T(8,128)(2,1)}, bf16[4,256,768]{2,1,0:T(8,128)(2,1)S(1)}, f32[4,8,4]{2,0,1:T(4,128)S(1)}, /*index=5*/f32[4,256,768]{2,1,0:T(8,128)}) %tuple.132), branch_computations={%region_18.18_spmd, %region_19.23_spmd} | conditional | flops 808725120 | bytes 14945572 | solution.py:122
  155.6 5.1 %bitcast_add_fusion = f32[4,256,768]{2,1,0:T(8,128)} fusion(f32[4,256,768]{2,1,0:T(8,128)} %get-tuple-element.527, f32[4,4,64,256]{3,2,0,1:T(8,128)} %fusion.29, f32[4,4]{0,1:T(4,128)S(1)} %copy.21, bf16[8,4,64,768]{3,2,1,0:T(8,128)(2,1)} %get-tuple-element.528, s32[]{:T(128)} %bitcast.8, f32[4,4,64,256]{3,2,0,1:T(8,128)S(1)} %fusion.34), kind=kOutput, calls=%fused_computation.21 | convolution fusion | flops 405015040 | bytes 9832960 | tf_op jit(solution)/shard_map/while/body/eval_jaxpr/cond/branch_1_fun/ijwp,jwd->ipd/dot_general | solution.py:117
  161.9 9.3 %conditional.8 = (f32[4,256,768]{2,1,0:T(8,128)}) conditional(s32[]{:T(128)} %bitcast.99, f32[4,256,768]{2,1,0:T(8,128)} %get-tuple-element.847, (s32[6]{0:T(128)S(1)}, s32[]{:T(128)}, bf16[8,4,64,768]{3,2,1,0:T(8,128)(2,1)}, bf16[4,256,768]{2,1,0:T(8,128)(2,1)S(1)}, f32[4,8,4]{2,0,1:T(4,128)S(1)}, /*index=5*/f32[4,256,768]{2,1,0:T(8,128)}) %tuple.132), branch_computations={%region_18.18_spmd, %region_19.23_spmd} | conditional | flops 808725120 | bytes 14945572 | solution.py:122
  166.1 5.1 %bitcast_add_fusion = f32[4,256,768]{2,1,0:T(8,128)} fusion(f32[4,256,768]{2,1,0:T(8,128)} %get-tuple-element.527, f32[4,4,64,256]{3,2,0,1:T(8,128)} %fusion.29, f32[4,4]{0,1:T(4,128)S(1)} %copy.21, bf16[8,4,64,768]{3,2,1,0:T(8,128)(2,1)} %get-tuple-element.528, s32[]{:T(128)} %bitcast.8, f32[4,4,64,256]{3,2,0,1:T(8,128)S(1)} %fusion.34), kind=kOutput, calls=%fused_computation.21 | convolution fusion | flops 405015040 | bytes 9832960 | tf_op jit(solution)/shard_map/while/body/eval_jaxpr/cond/branch_1_fun/ijwp,jwd->ipd/dot_general | solution.py:117
  172.4 9.3 %conditional.8 = (f32[4,256,768]{2,1,0:T(8,128)}) conditional(s32[]{:T(128)} %bitcast.99, f32[4,256,768]{2,1,0:T(8,128)} %get-tuple-element.847, (s32[6]{0:T(128)S(1)}, s32[]{:T(128)}, bf16[8,4,64,768]{3,2,1,0:T(8,128)(2,1)}, bf16[4,256,768]{2,1,0:T(8,128)(2,1)S(1)}, f32[4,8,4]{2,0,1:T(4,128)S(1)}, /*index=5*/f32[4,256,768]{2,1,0:T(8,128)}) %tuple.132), branch_computations={%region_18.18_spmd, %region_19.23_spmd} | conditional | flops 808725120 | bytes 14945572 | solution.py:122
  176.7 5.1 %bitcast_add_fusion = f32[4,256,768]{2,1,0:T(8,128)} fusion(f32[4,256,768]{2,1,0:T(8,128)} %get-tuple-element.527, f32[4,4,64,256]{3,2,0,1:T(8,128)} %fusion.29, f32[4,4]{0,1:T(4,128)S(1)} %copy.21, bf16[8,4,64,768]{3,2,1,0:T(8,128)(2,1)} %get-tuple-element.528, s32[]{:T(128)} %bitcast.8, f32[4,4,64,256]{3,2,0,1:T(8,128)S(1)} %fusion.34), kind=kOutput, calls=%fused_computation.21 | convolution fusion | flops 405015040 | bytes 9832960 | tf_op jit(solution)/shard_map/while/body/eval_jaxpr/cond/branch_1_fun/ijwp,jwd->ipd/dot_general | solution.py:117
  183.0 9.3 %conditional.8 = (f32[4,256,768]{2,1,0:T(8,128)}) conditional(s32[]{:T(128)} %bitcast.99, f32[4,256,768]{2,1,0:T(8,128)} %get-tuple-element.847, (s32[6]{0:T(128)S(1)}, s32[]{:T(128)}, bf16[8,4,64,768]{3,2,1,0:T(8,128)(2,1)}, bf16[4,256,768]{2,1,0:T(8,128)(2,1)S(1)}, f32[4,8,4]{2,0,1:T(4,128)S(1)}, /*index=5*/f32[4,256,768]{2,1,0:T(8,128)}) %tuple.132), branch_computations={%region_18.18_spmd, %region_19.23_spmd} | conditional | flops 808725120 | bytes 14945572 | solution.py:122
  187.2 5.1 %bitcast_add_fusion = f32[4,256,768]{2,1,0:T(8,128)} fusion(f32[4,256,768]{2,1,0:T(8,128)} %get-tuple-element.527, f32[4,4,64,256]{3,2,0,1:T(8,128)} %fusion.29, f32[4,4]{0,1:T(4,128)S(1)} %copy.21, bf16[8,4,64,768]{3,2,1,0:T(8,128)(2,1)} %get-tuple-element.528, s32[]{:T(128)} %bitcast.8, f32[4,4,64,256]{3,2,0,1:T(8,128)S(1)} %fusion.34), kind=kOutput, calls=%fused_computation.21 | convolution fusion | flops 405015040 | bytes 9832960 | tf_op jit(solution)/shard_map/while/body/eval_jaxpr/cond/branch_1_fun/ijwp,jwd->ipd/dot_general | solution.py:117
  193.5 9.3 %conditional.8 = (f32[4,256,768]{2,1,0:T(8,128)}) conditional(s32[]{:T(128)} %bitcast.99, f32[4,256,768]{2,1,0:T(8,128)} %get-tuple-element.847, (s32[6]{0:T(128)S(1)}, s32[]{:T(128)}, bf16[8,4,64,768]{3,2,1,0:T(8,128)(2,1)}, bf16[4,256,768]{2,1,0:T(8,128)(2,1)S(1)}, f32[4,8,4]{2,0,1:T(4,128)S(1)}, /*index=5*/f32[4,256,768]{2,1,0:T(8,128)}) %tuple.132), branch_computations={%region_18.18_spmd, %region_19.23_spmd} | conditional | flops 808725120 | bytes 14945572 | solution.py:122
  197.8 5.1 %bitcast_add_fusion = f32[4,256,768]{2,1,0:T(8,128)} fusion(f32[4,256,768]{2,1,0:T(8,128)} %get-tuple-element.527, f32[4,4,64,256]{3,2,0,1:T(8,128)} %fusion.29, f32[4,4]{0,1:T(4,128)S(1)} %copy.21, bf16[8,4,64,768]{3,2,1,0:T(8,128)(2,1)} %get-tuple-element.528, s32[]{:T(128)} %bitcast.8, f32[4,4,64,256]{3,2,0,1:T(8,128)S(1)} %fusion.34), kind=kOutput, calls=%fused_computation.21 | convolution fusion | flops 405015040 | bytes 9832960 | tf_op jit(solution)/shard_map/while/body/eval_jaxpr/cond/branch_1_fun/ijwp,jwd->ipd/dot_general | solution.py:117
  204.1 9.3 %conditional.8 = (f32[4,256,768]{2,1,0:T(8,128)}) conditional(s32[]{:T(128)} %bitcast.99, f32[4,256,768]{2,1,0:T(8,128)} %get-tuple-element.847, (s32[6]{0:T(128)S(1)}, s32[]{:T(128)}, bf16[8,4,64,768]{3,2,1,0:T(8,128)(2,1)}, bf16[4,256,768]{2,1,0:T(8,128)(2,1)S(1)}, f32[4,8,4]{2,0,1:T(4,128)S(1)}, /*index=5*/f32[4,256,768]{2,1,0:T(8,128)}) %tuple.132), branch_computations={%region_18.18_spmd, %region_19.23_spmd} | conditional | flops 808725120 | bytes 14945572 | solution.py:122
  208.3 5.1 %bitcast_add_fusion = f32[4,256,768]{2,1,0:T(8,128)} fusion(f32[4,256,768]{2,1,0:T(8,128)} %get-tuple-element.527, f32[4,4,64,256]{3,2,0,1:T(8,128)} %fusion.29, f32[4,4]{0,1:T(4,128)S(1)} %copy.21, bf16[8,4,64,768]{3,2,1,0:T(8,128)(2,1)} %get-tuple-element.528, s32[]{:T(128)} %bitcast.8, f32[4,4,64,256]{3,2,0,1:T(8,128)S(1)} %fusion.34), kind=kOutput, calls=%fused_computation.21 | convolution fusion | flops 405015040 | bytes 9832960 | tf_op jit(solution)/shard_map/while/body/eval_jaxpr/cond/branch_1_fun/ijwp,jwd->ipd/dot_general | solution.py:117
  213.4 3.2 %convert_element_type.50 = bf16[4,256,768]{2,1,0:T(8,128)(2,1)} convert(f32[4,256,768]{2,1,0:T(8,128)} %get-tuple-element.571) | non-fusion elementwise | flops 786432 | bytes 4718592 | tf_op jit(solution)/shard_map/convert_element_type | solution.py:160
  216.7 69.3 %while.51 = (s32[]{:T(128)}, f32[4,64,768]{2,1,0:T(8,128)S(1)}, s32[8,6]{1,0:T(8,128)S(1)}, s32[]{:T(128)}, s32[8]{0:T(128)S(1)}, /*index=5*/bf16[32,256,768]{2,...) while((s32[]{:T(128)}, f32[4,64,768]{2,1,0:T(8,128)S(1)}, ...), condition=%wide.region_37.38_spmd.clone, body=%wide.region_25.37_spmd.clone.sunk | while | flops 809733696 | bytes 11568023 | solution.py:158
  219.2 9.8 %conditional.9 = (f32[4,64,768]{2,1,0:T(8,128)S(1)}) conditional(s32[]{:T(128)} %convert_element_type.74, f32[4,64,768]{2,1,0:T(8,128)S(1)} %get-tuple-element.874, (s32[]{:T(128)}, bf16[32,256,768]{2,1,0:T(8,128)(2,1)}, bf16[4,64,768]{2,1,0:T(8,128)(2,1)S(1)}, f32[]{:T(128)}, f32[32]{0:T(128)S(1)}, /*index=5*/f32[4]{0:T(128)S(1)}, s32[]{:T(128)}, ...), branch_computations={%region_27.27_spmd, %region_28.36_spmd} | conditional | flops 809733632 | bytes 11567724 | solution.py:156
  219.3 2.1 fusion.101
  224.0 5.0 %fusion.73 = f32[4,64,768]{2,1,0:T(8,128)S(1)} fusion(f32[4,64,768]{2,1,0:T(8,128)S(1)} %get-tuple-element.541, bf16[32,256,768]{2,1,0:T(8,128)(2,1)} %get-tuple-element.542, s32[]{:T(128)S(6)} %select_n.99, f32[4,4,64,256]{3,2,1,0:T(8,128)S(1)} %fusion.62, f32[4,4,64,256]{3,2,1,0:T(8,128)S(1)} %get-tuple-element.664, ...), kind=kOutput, calls=%fused_computation.67 | convolution fusion | flops 404423936 | bytes 5247044 | tf_op jit(solution)/shard_map/while/body/eval_jaxpr/cond/branch_1_fun/ijwp,ipd->jwd/dot_general | solution.py:152
  231.6 9.8 %conditional.9 = (f32[4,64,768]{2,1,0:T(8,128)S(1)}) conditional(s32[]{:T(128)} %convert_element_type.74, f32[4,64,768]{2,1,0:T(8,128)S(1)} %get-tuple-element.874, (s32[]{:T(128)}, bf16[32,256,768]{2,1,0:T(8,128)(2,1)}, bf16[4,64,768]{2,1,0:T(8,128)(2,1)S(1)}, f32[]{:T(128)}, f32[32]{0:T(128)S(1)}, /*index=5*/f32[4]{0:T(128)S(1)}, s32[]{:T(128)}, ...), branch_computations={%region_27.27_spmd, %region_28.36_spmd} | conditional | flops 809733632 | bytes 11567724 | solution.py:156
  231.6 2.1 fusion.101
  236.3 5.0 %fusion.73 = f32[4,64,768]{2,1,0:T(8,128)S(1)} fusion(f32[4,64,768]{2,1,0:T(8,128)S(1)} %get-tuple-element.541, bf16[32,256,768]{2,1,0:T(8,128)(2,1)} %get-tuple-element.542, s32[]{:T(128)S(6)} %select_n.99, f32[4,4,64,256]{3,2,1,0:T(8,128)S(1)} %fusion.62, f32[4,4,64,256]{3,2,1,0:T(8,128)S(1)} %get-tuple-element.664, ...), kind=kOutput, calls=%fused_computation.67 | convolution fusion | flops 404423936 | bytes 5247044 | tf_op jit(solution)/shard_map/while/body/eval_jaxpr/cond/branch_1_fun/ijwp,ipd->jwd/dot_general | solution.py:152
  246.4 9.8 %conditional.9 = (f32[4,64,768]{2,1,0:T(8,128)S(1)}) conditional(s32[]{:T(128)} %convert_element_type.74, f32[4,64,768]{2,1,0:T(8,128)S(1)} %get-tuple-element.874, (s32[]{:T(128)}, bf16[32,256,768]{2,1,0:T(8,128)(2,1)}, bf16[4,64,768]{2,1,0:T(8,128)(2,1)S(1)}, f32[]{:T(128)}, f32[32]{0:T(128)S(1)}, /*index=5*/f32[4]{0:T(128)S(1)}, s32[]{:T(128)}, ...), branch_computations={%region_27.27_spmd, %region_28.36_spmd} | conditional | flops 809733632 | bytes 11567724 | solution.py:156
  246.5 2.1 fusion.101
  251.2 5.0 %fusion.73 = f32[4,64,768]{2,1,0:T(8,128)S(1)} fusion(f32[4,64,768]{2,1,0:T(8,128)S(1)} %get-tuple-element.541, bf16[32,256,768]{2,1,0:T(8,128)(2,1)} %get-tuple-element.542, s32[]{:T(128)S(6)} %select_n.99, f32[4,4,64,256]{3,2,1,0:T(8,128)S(1)} %fusion.62, f32[4,4,64,256]{3,2,1,0:T(8,128)S(1)} %get-tuple-element.664, ...), kind=kOutput, calls=%fused_computation.67 | convolution fusion | flops 404423936 | bytes 5247044 | tf_op jit(solution)/shard_map/while/body/eval_jaxpr/cond/branch_1_fun/ijwp,ipd->jwd/dot_general | solution.py:152
  258.8 9.8 %conditional.9 = (f32[4,64,768]{2,1,0:T(8,128)S(1)}) conditional(s32[]{:T(128)} %convert_element_type.74, f32[4,64,768]{2,1,0:T(8,128)S(1)} %get-tuple-element.874, (s32[]{:T(128)}, bf16[32,256,768]{2,1,0:T(8,128)(2,1)}, bf16[4,64,768]{2,1,0:T(8,128)(2,1)S(1)}, f32[]{:T(128)}, f32[32]{0:T(128)S(1)}, /*index=5*/f32[4]{0:T(128)S(1)}, s32[]{:T(128)}, ...), branch_computations={%region_27.27_spmd, %region_28.36_spmd} | conditional | flops 809733632 | bytes 11567724 | solution.py:156
  258.8 2.1 fusion.101
  263.5 5.0 %fusion.73 = f32[4,64,768]{2,1,0:T(8,128)S(1)} fusion(f32[4,64,768]{2,1,0:T(8,128)S(1)} %get-tuple-element.541, bf16[32,256,768]{2,1,0:T(8,128)(2,1)} %get-tuple-element.542, s32[]{:T(128)S(6)} %select_n.99, f32[4,4,64,256]{3,2,1,0:T(8,128)S(1)} %fusion.62, f32[4,4,64,256]{3,2,1,0:T(8,128)S(1)} %get-tuple-element.664, ...), kind=kOutput, calls=%fused_computation.67 | convolution fusion | flops 404423936 | bytes 5247044 | tf_op jit(solution)/shard_map/while/body/eval_jaxpr/cond/branch_1_fun/ijwp,ipd->jwd/dot_general | solution.py:152
  273.6 9.8 %conditional.9 = (f32[4,64,768]{2,1,0:T(8,128)S(1)}) conditional(s32[]{:T(128)} %convert_element_type.74, f32[4,64,768]{2,1,0:T(8,128)S(1)} %get-tuple-element.874, (s32[]{:T(128)}, bf16[32,256,768]{2,1,0:T(8,128)(2,1)}, bf16[4,64,768]{2,1,0:T(8,128)(2,1)S(1)}, f32[]{:T(128)}, f32[32]{0:T(128)S(1)}, /*index=5*/f32[4]{0:T(128)S(1)}, s32[]{:T(128)}, ...), branch_computations={%region_27.27_spmd, %region_28.36_spmd} | conditional | flops 809733632 | bytes 11567724 | solution.py:156
  273.7 2.1 fusion.101
  278.4 5.0 %fusion.73 = f32[4,64,768]{2,1,0:T(8,128)S(1)} fusion(f32[4,64,768]{2,1,0:T(8,128)S(1)} %get-tuple-element.541, bf16[32,256,768]{2,1,0:T(8,128)(2,1)} %get-tuple-element.542, s32[]{:T(128)S(6)} %select_n.99, f32[4,4,64,256]{3,2,1,0:T(8,128)S(1)} %fusion.62, f32[4,4,64,256]{3,2,1,0:T(8,128)S(1)} %get-tuple-element.664, ...), kind=kOutput, calls=%fused_computation.67 | convolution fusion | flops 404423936 | bytes 5247044 | tf_op jit(solution)/shard_map/while/body/eval_jaxpr/cond/branch_1_fun/ijwp,ipd->jwd/dot_general | solution.py:152
  (198 shorter events, 75.8 us)
Async XLA Ops:
  7.2 2.2 copy-start
  7.2 36.6 %all-gather.3.cloned.1.call-start = ((), (), s32[]{:S(2)}) async-start(), calls=%async_computation | async-start | bytes 3538944 | tf_op jit(solution)/shard_map/all_gather | solution.py:59
  7.9 208.7 %all-gather.5.cloned.1.call-start = ((), (), s32[]{:S(2)}) async-start(), calls=%async_computation.1 | async-start | bytes 14155776 | tf_op jit(solution)/shard_map/all_gather | solution.py:128
  78.8 71.3 %copy-start.1 = (bf16[4,256,768]{2,1,0:T(8,128)(2,1)S(1)}, bf16[4,256,768]{2,1,0:T(8,128)(2,1)}, u32[]{:S(2)}) copy-start(bf16[4,256,768]{2,1,0:T(8,128)(2,1)} %get-tuple-element.902) | copy-start | bytes 4718596
  213.4 3.3 %copy-start.2 = (bf16[4,64,768]{2,1,0:T(8,128)(2,1)S(1)}, bf16[4,64,768]{2,1,0:T(8,128)(2,1)}, u32[]{:S(2)}) copy-start(bf16[4,64,768]{2,1,0:T(8,128)(2,1)} %param.18) | copy-start | bytes 1179652
Sparse Core Ops, SparseCore 0:
  9.9 33.7 all-gather.2
  45.6 72.9 all-gather.4
where the time goes:
time: 292 us; the launch traced here: 294 us
  matrix products  89.2 us (31%)
  blocking collectives  64.8 us (22%)
  other arithmetic  43.7 us (15%)
  waiting for transfers between devices  30.8 us (11%)
  local copies, waits for them, and re-layouts  26.2 us (9%)
  loops' own time  21.5 us (7%)
  between operations  17.4 us (6%)
    psum x1, blocking collectives, body(): loss_total, temp_total = lax.psum((loss_part, temp_part), ('img', 'cap'))  40.2 us
    dot_general x17, matrix products, similarity_table(): jnp.einsum('ipd,jwd->ijwp', patch_block, word_tile_block, preferred_eleme...  33.8 us
    dot_general x6, matrix products, patch_compute(): jnp.einsum('ijwp,jwd->ipd', weights, word_tile_block, preferred_element_t...  30.4 us
    all_gather x1, waiting for transfers between devices, body(): all_words = lax.all_gather(words, 'cap', axis=0, tiled=True)  29.4 us
    dot_general x5, matrix products, add_compute(): jnp.einsum('ijwp,ipd->jwd', weights, patch_block, preferred_element_type=...  25 us
    div x11, other arithmetic, token_weights(): share_words = jax.nn.softmax(lifted, axis=2)  15.5 us
    psum x1, blocking collectives, body(): mass_all = lax.psum(column_mass, 'cap')  12.8 us
    pmax x1, blocking collectives, body(): peak_all = lax.pmax(column_peak, 'cap')  11.7 us
  transfers between devices with their start and end apart: 2, of which 1 were waited for; matrix products, arithmetic and copies ran while one was open for 32% of the time, Pallas kernels for 0%

commit v1 on v0

v1 whole, which is shorter than its diff:
```python
import functools
import math

import jax
import jax.numpy as jnp
from jax import lax
from jax.experimental import pallas as pl
from jax.experimental.pallas import tpu as pltpu
from jax.sharding import PartitionSpec as P

sharpness = 4.0
loss_scale = 65536.0
far_below = -1e30
F32 = jnp.float32
BF16 = jnp.bfloat16
LANES = 128
ROWS = 8
VMEM_LIMIT = 56 << 20

NT = (((1,), (1,)), ((), ()))
NN = (((1,), (0,)), ((), ()))
TN = (((0,), (0,)), ((), ()))


def spec(space=pltpu.VMEM):
    return pl.BlockSpec(memory_space=space)


def block_is_live(cands, counts, row, block, column, slots):
    live = jnp.int32(0)
    for s in range(slots):
        hit = (cands[row, block, s] == column) & (s < counts[row, block])
        live = live | hit.astype(jnp.int32)
    return live > 0


def forward_kernel(offset, cands, counts, patches, words, prior, weights_out, scores_out, low, high):
    row = lax.axis_index("img")
    me = lax.axis_index("cap")
    column = me ^ offset
    per, patch, width = patches.shape
    tokens = words.shape[1]
    lines = per * tokens
    scale = sharpness * width**-0.5 * math.log2(math.e)
    scores_out[...] = prior[...]

    @pl.when(block_is_live(cands, counts, row, me, column, cands.shape[2]))
    def _():
        sub = lax.broadcasted_iota(jnp.int32, (ROWS, LANES), 0)
        lane = lax.broadcasted_iota(jnp.int32, (ROWS, LANES), 1)
        spot = lane == column * per + sub

        def place(i, over_words, over_patches):
            part = jnp.sum(over_words, axis=1, keepdims=True) * (1.0 / patch)
            part = part + over_patches * (1.0 / tokens)
            part = part * (0.5 * math.log(2.0) / sharpness)
            part = jnp.concatenate([part, jnp.zeros((ROWS - per, 1), F32)], axis=0)
            line = jnp.sum(jnp.where(spot & (sub < per), part, 0.0), axis=0, keepdims=True)
            return jnp.where(sub == i, line, 0.0)

        word_rows = words[...].reshape(lines, width)
        low[...] = jnp.full(low.shape, 1.0, F32)
        high[...] = jnp.full(high.shape, 1.0, F32)
        tile = jnp.zeros((ROWS, LANES), F32)
        for i in range(per):
            raw = lax.dot_general(word_rows, patches[i], NT, preferred_element_type=F32)
            mass = jnp.exp2(raw * scale)
            mass3 = mass.reshape(per, tokens, patch)
            word_sum = jnp.sum(mass3, axis=1)
            patch_sum = jnp.sum(mass, axis=1, keepdims=True)
            low[...] = jnp.minimum(low[...], jnp.min(word_sum, axis=0, keepdims=True))
            high[...] = jnp.maximum(high[...], jnp.max(word_sum, axis=0, keepdims=True))
            low[...] = jnp.minimum(low[...], jnp.min(patch_sum, axis=0, keepdims=True))
            high[...] = jnp.maximum(high[...], jnp.max(patch_sum, axis=0, keepdims=True))
            word_part = (0.5 / patch) / word_sum
            patch_part = (0.5 / tokens) / patch_sum
            blended = mass3 * (word_part[:, None, :] + patch_part.reshape(per, tokens, 1))
            weights_out[i] = blended.reshape(lines, patch).astype(BF16)
            patch_logs = jnp.sum(jnp.log2(patch_sum).reshape(per, tokens, 1), axis=1)
            tile = tile + place(i, jnp.log2(word_sum), patch_logs)
        scores_out[...] += tile
        safe = (jnp.min(low[...]) > 2.0**-90) & (jnp.max(high[...]) < 2.0**120)

        @pl.when(jnp.logical_not(safe))
        def _():
            scores_out[...] = prior[...]

            def image(i, carry):
                raw = lax.dot_general(word_rows, patches[i], NT, preferred_element_type=F32)
                lifted = raw * scale
                lifted3 = lifted.reshape(per, tokens, patch)
                word_top = jnp.max(lifted3, axis=1)
                patch_top = jnp.max(lifted, axis=1, keepdims=True)
                word_mass = jnp.exp2(lifted3 - word_top[:, None, :])
                patch_mass = jnp.exp2(lifted - patch_top).reshape(per, tokens, patch)
                word_sum = jnp.sum(word_mass, axis=1)
                patch_sum = jnp.sum(patch_mass, axis=2, keepdims=True)
                word_part = (0.5 / patch) / word_sum
                patch_part = (0.5 / tokens) / patch_sum
                blended = word_mass * word_part[:, None, :] + patch_mass * patch_part
                weights_out[i] = blended.reshape(lines, patch).astype(BF16)
                patch_logs = jnp.sum(
                    patch_top.reshape(per, tokens, 1) + jnp.log2(patch_sum), axis=1
                )
                scores_out[...] += place(i, word_top + jnp.log2(word_sum), patch_logs)
                return carry

            lax.fori_loop(0, per, image, 0)


def forward_call(offset, cands, counts, patches, words, prior):
    per, patch, width = patches.shape
    lines = per * words.shape[1]
    return pl.pallas_call(
        functools.partial(forward_kernel, offset),
        out_shape=(
            jax.ShapeDtypeStruct((per, lines, patch), BF16),
            jax.ShapeDtypeStruct((ROWS, LANES), F32),
        ),
        in_specs=[spec(pltpu.SMEM), spec(pltpu.SMEM), spec(), spec(), spec()],
        out_specs=(spec(), spec()),
        scratch_shapes=[pltpu.VMEM((1, patch), F32), pltpu.VMEM((1, patch), F32)],
        compiler_params=pltpu.CompilerParams(vmem_limit_bytes=VMEM_LIMIT),
        cost_estimate=pl.CostEstimate(
            flops=2 * per * lines * patch * width,
            bytes_accessed=2 * (per * patch * width + lines * width + per * lines * patch),
            transcendentals=per * lines * patch,
        ),
        name=f"forward_{offset}",
    )(cands, counts, patches, words, prior)


def stats_kernel(total, images, width, cands, counts, nse, *refs):
    tiles = refs[:total]
    coef_out, sums_out = refs[total:]
    row = lax.axis_index("img")
    me = lax.axis_index("cap")
    slots = cands.shape[2]
    per = images // (total * cands.shape[0])
    sub = lax.broadcasted_iota(jnp.int32, (ROWS, LANES), 0)
    lane = lax.broadcasted_iota(jnp.int32, (ROWS, LANES), 1)
    column = lane // per
    softness = jnp.exp(jnp.full((ROWS, LANES), nse[0], F32))
    kept, lives, marks = [], [], []
    peak = jnp.full((1, LANES), far_below, F32)
    for k in range(total):
        block = me ^ k
        live = jnp.zeros((ROWS, LANES), jnp.bool_)
        for s in range(slots):
            target = jnp.where(s < counts[row, block], cands[row, block, s], -1)
            live = live | (column == target)
        live = live & (sub < per)
        masked = jnp.where(live, tiles[k][...] * softness, far_below)
        kept.append(masked)
        lives.append(live)
        marks.append(live & (lane == block * per + sub))
        peak = jnp.maximum(peak, jnp.max(masked, axis=0, keepdims=True))
    mass = jnp.zeros((1, LANES), F32)
    for k in range(total):
        mass = mass + jnp.sum(
            jnp.where(lives[k], jnp.exp(kept[k] - peak), 0.0), axis=0, keepdims=True
        )
    col_ok = lane[:1] < total * per
    col_lse = jnp.where(col_ok, peak + jnp.log(jnp.where(col_ok, mass, 1.0)), 0.0)
    loss = jnp.zeros((ROWS, LANES), F32)
    temp = jnp.zeros((ROWS, LANES), F32)
    own = None
    for k in range(total):
        top = jnp.max(kept[k], axis=1, keepdims=True)
        part = jnp.sum(jnp.where(lives[k], jnp.exp(kept[k] - top), 0.0), axis=1, keepdims=True)
        row_lse = top + jnp.log(jnp.where(sub[:, :1] < per, part, 1.0))
        pull = jnp.where(
            lives[k],
            (0.5 / images)
            * (
                jnp.exp(kept[k] - row_lse)
                + jnp.exp(kept[k] - col_lse)
                - jnp.where(marks[k], 2.0, 0.0)
            ),
            0.0,
        )
        temp = temp + jnp.where(lives[k], pull * kept[k], 0.0)
        loss = loss + jnp.where((lane == 0) & (sub < per), row_lse, 0.0)
        loss = loss - jnp.where(marks[k], 2.0 * kept[k], 0.0)
        if k == 0:
            own = pull
    loss = loss + jnp.where(sub == 0, col_lse, 0.0)
    loss_total = jnp.sum(loss) * (0.5 / images)
    temp_total = jnp.sum(temp)
    sums_out[...] = jnp.where(sub == 0, loss_total, temp_total)
    factor = own * softness * (loss_scale * width**-0.5)
    for k in range(total):
        block = me ^ k
        spot = (lane == block * per + sub) & (sub < per)
        for i in range(per):
            line = jnp.broadcast_to(factor[i : i + 1], (ROWS, LANES))
            value = jnp.sum(jnp.where(spot, line, 0.0), axis=1, keepdims=True)
            coef_out[k, i] = jnp.broadcast_to(value, (ROWS, LANES))


def stats_call(images, width, cands, counts, nse, tiles, per):
    total = len(tiles)
    return pl.pallas_call(
        functools.partial(stats_kernel, total, images, width),
        out_shape=(
            jax.ShapeDtypeStruct((total, per, ROWS, LANES), F32),
            jax.ShapeDtypeStruct((ROWS, LANES), F32),
        ),
        in_specs=[spec(pltpu.SMEM)] * 3 + [spec()] * total,
        out_specs=(spec(), spec()),
        name="stats",
    )(cands, counts, nse, *tiles)


def scaled(weights, coef, i, per):
    lines, patch = weights.shape[1:]
    block = weights[i].astype(F32).reshape(per, lines // per, patch)
    factor = jnp.tile(coef[i, :per][:, None, :], (1, 1, patch // LANES))
    return (block * factor).reshape(lines, patch).astype(BF16)


def word_kernel(group, cands, counts, patches, coef, weights_a, weights_b, out_a, out_b):
    row = lax.axis_index("img")
    me = lax.axis_index("cap")
    per, patch, width = patches.shape
    for n, (weights, out) in enumerate(((weights_a, out_a), (weights_b, out_b))):
        offset = 2 * group + n
        live = block_is_live(cands, counts, row, me, me ^ offset, cands.shape[2])

        @pl.when(live)
        def _():
            total = jnp.zeros((weights.shape[1], width), F32)
            for i in range(per):
                total = total + lax.dot_general(
                    scaled(weights, coef.at[offset], i, per),
                    patches[i],
                    NN,
                    preferred_element_type=F32,
                )
            out[...] = total.reshape(out.shape).astype(out.dtype)

        @pl.when(jnp.logical_not(live))
        def _():
            out[...] = jnp.zeros(out.shape, out.dtype)


def word_call(group, cands, counts, patches, coef, weights_a, weights_b):
    per, patch, width = patches.shape
    lines = weights_a.shape[1]
    shape = (per, lines // per, width)
    return pl.pallas_call(
        functools.partial(word_kernel, group),
        out_shape=(jax.ShapeDtypeStruct(shape, F32), jax.ShapeDtypeStruct(shape, BF16)),
        in_specs=[spec(pltpu.SMEM)] * 2 + [spec()] * 4,
        out_specs=(spec(), spec()),
        compiler_params=pltpu.CompilerParams(vmem_limit_bytes=VMEM_LIMIT),
        cost_estimate=pl.CostEstimate(
            flops=4 * per * lines * patch * width,
            bytes_accessed=2 * per * patch * width + 4 * per * lines * patch + 6 * lines * width,
            transcendentals=0,
        ),
        name=f"word_{group}",
    )(cands, counts, patches, coef, weights_a, weights_b)


def patch_kernel(total, cands, counts, coef, *refs):
    weights, words, out, acc = refs[:total], refs[total : 2 * total], refs[-2], refs[-1]
    row = lax.axis_index("img")
    me = lax.axis_index("cap")
    per, patch, width = out.shape
    for k in range(total):

        def add(first):
            word_rows = words[k][...].reshape(weights[k].shape[1], width)
            for i in range(per):
                part = lax.dot_general(
                    scaled(weights[k], coef.at[k], i, per),
                    word_rows,
                    TN,
                    preferred_element_type=F32,
                )
                if first:
                    acc[i] = part
                else:
                    acc[i] += part

        if k == 0:
            add(True)
        else:
            live = block_is_live(cands, counts, row, me, me ^ k, cands.shape[2])
            pl.when(live)(functools.partial(add, False))
    out[...] = acc[...].astype(BF16)


def patch_call(cands, counts, coef, weights, words, shape):
    total = len(weights)
    per, patch, width = shape
    lines = weights[0].shape[1]
    return pl.pallas_call(
        functools.partial(patch_kernel, total),
        out_shape=jax.ShapeDtypeStruct(shape, BF16),
        in_specs=[spec(pltpu.SMEM)] * 2 + [spec()] * (1 + 2 * total),
        out_specs=spec(),
        scratch_shapes=[pltpu.VMEM(shape, F32)],
        compiler_params=pltpu.CompilerParams(vmem_limit_bytes=VMEM_LIMIT),
        cost_estimate=pl.CostEstimate(
            flops=2 * total * per * lines * patch * width,
            bytes_accessed=2 * total * (per * lines * patch + lines * width) + 2 * per * patch * width,
            transcendentals=0,
        ),
        name="patch",
    )(cands, counts, coef, *weights, *words)


def add_kernel(*refs):
    total = refs[0][...].astype(F32)
    for ref in refs[1:-1]:
        total = total + ref[...].astype(F32)
    refs[-1][...] = total.astype(refs[-1].dtype)


def add_call(name, dtype, *arrays):
    return pl.pallas_call(
        add_kernel,
        out_shape=jax.ShapeDtypeStruct(arrays[0].shape, dtype),
        in_specs=[spec()] * len(arrays),
        out_specs=spec(),
        name=name,
    )(*arrays)


def scalar_kernel(count, *refs):
    loss_out, temp_out = refs[count:]
    total = refs[0][...]
    for ref in refs[1:count]:
        total = total + ref[...]
    loss_out[0] = total[0, 0]
    temp_out[0] = total[1, 0]


def scalar_call(tiles):
    one = jax.ShapeDtypeStruct((1,), F32)
    return pl.pallas_call(
        functools.partial(scalar_kernel, len(tiles)),
        out_shape=(one, one),
        in_specs=[spec()] * len(tiles),
        out_specs=(spec(pltpu.SMEM), spec(pltpu.SMEM)),
        name="scalars",
    )(*tiles)


def body(patches, words, natural_sharpness_exponent, candidates, counts):
    total = lax.axis_size("cap")
    rows = lax.axis_size("img")
    per, patch, width = patches.shape
    images = per * total * rows
    groups = total // 2

    def hop(x, offset):
        return lax.ppermute(x, "cap", [(i, i ^ offset) for i in range(total)])

    words_at = [None] * total
    words_at[0] = words
    words_at[1] = hop(words, 1)
    for g in range(1, groups):
        words_at[2 * g] = hop(words, 2 * g)
    for g in range(1, groups):
        words_at[2 * g + 1] = hop(words_at[2 * g], 1)

    scores = jnp.zeros((ROWS, LANES), F32)
    weights = []
    for k in range(total):
        w, scores = forward_call(k, candidates, counts, patches, words_at[k], scores)
        weights.append(w)

    sibling = hop(scores, 1)
    pair = jnp.concatenate([scores, sibling], axis=0)
    tiles = [scores, sibling]
    for g in range(1, groups):
        other = hop(pair, 2 * g)
        tiles += [other[:ROWS], other[ROWS:]]
    coef, sums = stats_call(images, width, candidates, counts, natural_sharpness_exponent, tiles, per)

    sum_tiles = [sums]
    for k in range(1, rows):
        sum_tiles.append(lax.ppermute(sums, "img", [(i, (i + k) % rows) for i in range(rows)]))

    arrived = []
    kept = None
    for g in list(range(groups - 1, 0, -1)) + [0]:
        mine, theirs = word_call(
            g, candidates, counts, patches, coef, weights[2 * g], weights[2 * g + 1]
        )
        from_sibling = hop(theirs, 1)
        if g:
            joined = add_call(f"join_{g}", BF16, mine, from_sibling)
            arrived.append(hop(joined, 2 * g))
        else:
            kept = (mine, from_sibling)

    patch_grad = patch_call(candidates, counts, coef, weights, words_at, patches.shape)
    word_grad = add_call("finish", BF16, *kept, *arrived)
    loss, temp = scalar_call(sum_tiles)
    return patch_grad, word_grad, loss, temp


def solution(mesh):
    placed = (P(("img", "cap"), None, None), P(("img", "cap"), None, None), P(), P(), P())
    return jax.shard_map(
        body,
        mesh=mesh,
        in_specs=placed,
        out_specs=(P(("img", "cap"), None, None), P(("img", "cap"), None, None), P(), P()),
        check_vma=False,
    )
```

time: 292 us -> 129 us (0.44)
  the two profiles are of different devices: /device:TPU:17 before, /device:TPU:0 now
where the time goes in v1:
time: 129 us; the launch traced here: 128 us
  Pallas kernels  58.1 us (45%)
  starting transfers between devices  31 us (24%)
  waiting for transfers between devices  25.6 us (20%)
  local copies, waits for them, and re-layouts  11.4 us (9%)
  between operations  1.47 us (1%)
    pallas_call x8, Pallas kernels, forward_call(): pl.pallas_call(functools.partial(forward_kernel, offset), out_shape=(jax....  25.1 us
    ppermute x18, starting transfers between devices, hop(): return lax.ppermute(x, 'cap', [(i, i ^ offset) for i in range(total)])  22.8 us
    ppermute x18, waiting for transfers between devices, hop(): return lax.ppermute(x, 'cap', [(i, i ^ offset) for i in range(total)])  20.5 us
    pallas_call x4, Pallas kernels, word_call(): pl.pallas_call(functools.partial(word_kernel, group), out_shape=(jax.Shap...  13.9 us
    unnamed x40, local copies, waits for them, and re-layouts  9 us
    pallas_call x4, Pallas kernels, add_call(): pl.pallas_call(add_kernel, out_shape=jax.ShapeDtypeStruct(arrays[0].shape...  8.74 us
    ppermute x3, starting transfers between devices, body(): lax.ppermute(sums, 'img', [(i, (i + k) % rows) for i in range(rows)])  8.25 us
    pallas_call x1, Pallas kernels, patch_call(): pl.pallas_call(functools.partial(patch_kernel, total), out_shape=jax.Shap...  6.91 us
  transfers between devices with their start and end apart: 21, of which 7 were waited for; matrix products, arithmetic and copies ran while one was open for 3% of the time, Pallas kernels for 37%

profile of v1, /device:TPU:0, one launch (start us, length us, event | category | flops | bytes accessed | tf_op | source)
XLA Modules:
  0.0 127.6 jit_solution(13821747966876137497)
XLA Ops:
  0.6 3.0 %collective-permute-start.4 = (bf16[4,64,768]{2,1,0:T(8,128)(2,1)}, bf16[4,64,768]{2,1,0:T(8,128)(2,1)S(1)}, u32[]{:S(2)}, u32[]{:S(2)}) collective-permute-start(bf16[4,64,768]{2,1,0:T(8,128)(2,1)} %refs_8_.1), channel_id=1, source_target_pairs={{0,2},{1,3},{2,0},{3,1},{4,6},{5,7},{6,4},{7,5},{8,10},{9,11},{10,... | collective-permute-start | bytes 1179656 | tf_op jit(solution)/shard_map/ppermute | solution.py:360
  3.6 1.5 %collective-permute-start.2 = (bf16[4,64,768]{2,1,0:T(8,128)(2,1)}, bf16[4,64,768]{2,1,0:T(8,128)(2,1)S(1)}, u32[]{:S(2)}, u32[]{:S(2)}) collective-permute-start(bf16[4,64,768]{2,1,0:T(8,128)(2,1)} %refs_8_.1), channel_id=1, source_target_pairs={{0,4},{1,5},{2,6},{3,7},{4,0},{5,1},{6,2},{7,3},{8,12},{9,13},{10,... | collective-permute-start | bytes 1179656 | tf_op jit(solution)/shard_map/ppermute | solution.py:360
  5.2 8.6 %collective-permute-done.4.words.refs_10_ = bf16[4,64,768]{2,1,0:T(8,128)(2,1)S(1)} collective-permute-done((bf16[4,64,768]{2,1,0:T(8,128)(2,1)}, bf16[4,64,768]{2,1,0:T(8,128)(2,1)S(1)}, u32[]{:S(2)}, u32[]{:S(2)}) %collective-permute-start.4) | collective-permute-done | bytes 393248 | tf_op jit(solution)/shard_map/ppermute | solution.py:360
  13.8 9.1 %collective-permute-done.2.words.refs_12_ = bf16[4,64,768]{2,1,0:T(8,128)(2,1)S(1)} collective-permute-done((bf16[4,64,768]{2,1,0:T(8,128)(2,1)}, bf16[4,64,768]{2,1,0:T(8,128)(2,1)S(1)}, u32[]{:S(2)}, u32[]{:S(2)}) %collective-permute-start.2) | collective-permute-done | bytes 393248 | tf_op jit(solution)/shard_map/ppermute | solution.py:360
  23.4 1.4 %copy.18.cands = s32[4,8,6]{2,1,0:T(8,128)} copy(s32[4,8,6]{1,0,2:T(4,128)} %param.8) | data formatting | bytes 1536 | tf_op args[3]
  24.8 0.6 broadcast_in_dim.3.prior
  25.4 5.7 %forward_0.1 = (bf16[4,256,256]{2,1,0:T(8,128)(2,1)}, f32[8,128]{1,0:T(8,128)}) custom-call(s32[4,8,6]{2,1,0:T(8,128)} %copy.18.cands, s32[4,8]{1,0:T(4,128)} %counts.27, bf16[4,256,768]{2,1,0:T(8,128)(2,1)} %patches.23, bf16[4,64,768]{2,1,0:T(8,128)(2,1)} %refs_8_.1, f32[8,128]{1,0:T(8,128)} %broadcast_in_dim.3.prior), custom_call_target="tpu_custom_call" | custom-call | flops 402653184 | bytes 2490368 | tf_op jit(solution)/shard_map/forward_0/pallas_call | solution.py:114
  31.1 0.7 copy-done.3
  31.8 2.4 %forward_1.1 = (bf16[4,256,256]{2,1,0:T(8,128)(2,1)}, f32[8,128]{1,0:T(8,128)}) custom-call(s32[4,8,6]{2,1,0:T(8,128)} %copy.18.cands, s32[4,8]{1,0:T(4,128)} %counts.27, bf16[4,256,768]{2,1,0:T(8,128)(2,1)} %patches.23, bf16[4,64,768]{2,1,0:T(8,128)(2,1)} %copy-done.3, f32[8,128]{1,0:T(8,128)} %get-tuple-element.32.prior), custom_call_target="tpu_custom_call" | custom-call | flops 402653184 | bytes 2490368 | tf_op jit(solution)/shard_map/forward_1/pallas_call | solution.py:114
  34.2 3.3 %forward_2.1 = (bf16[4,256,256]{2,1,0:T(8,128)(2,1)}, f32[8,128]{1,0:T(8,128)}) custom-call(s32[4,8,6]{2,1,0:T(8,128)} %copy.18.cands, s32[4,8]{1,0:T(4,128)} %counts.27, bf16[4,256,768]{2,1,0:T(8,128)(2,1)} %patches.23, bf16[4,64,768]{2,1,0:T(8,128)(2,1)} %copy-done, f32[8,128]{1,0:T(8,128)} %get-tuple-element.33.prior), custom_call_target="tpu_custom_call" | custom-call | flops 402653184 | bytes 2490368 | tf_op jit(solution)/shard_map/forward_2/pallas_call | solution.py:114
  37.5 0.8 copy-done.4
  38.3 3.3 %forward_3.1 = (bf16[4,256,256]{2,1,0:T(8,128)(2,1)}, f32[8,128]{1,0:T(8,128)}) custom-call(s32[4,8,6]{2,1,0:T(8,128)} %copy.18.cands, s32[4,8]{1,0:T(4,128)} %counts.27, bf16[4,256,768]{2,1,0:T(8,128)(2,1)} %patches.23, bf16[4,64,768]{2,1,0:T(8,128)(2,1)} %copy-done.4, f32[8,128]{1,0:T(8,128)} %get-tuple-element.34.prior), custom_call_target="tpu_custom_call" | custom-call | flops 402653184 | bytes 2490368 | tf_op jit(solution)/shard_map/forward_3/pallas_call | solution.py:114
  41.6 2.4 %forward_4.1 = (bf16[4,256,256]{2,1,0:T(8,128)(2,1)}, f32[8,128]{1,0:T(8,128)}) custom-call(s32[4,8,6]{2,1,0:T(8,128)} %copy.18.cands, s32[4,8]{1,0:T(4,128)} %counts.27, bf16[4,256,768]{2,1,0:T(8,128)(2,1)} %patches.23, bf16[4,64,768]{2,1,0:T(8,128)(2,1)} %copy-done.1, f32[8,128]{1,0:T(8,128)} %get-tuple-element.35.prior), custom_call_target="tpu_custom_call" | custom-call | flops 402653184 | bytes 2490368 | tf_op jit(solution)/shard_map/forward_4/pallas_call | solution.py:114
  44.0 0.7 copy-done.5
  44.7 2.4 %forward_5.1 = (bf16[4,256,256]{2,1,0:T(8,128)(2,1)}, f32[8,128]{1,0:T(8,128)}) custom-call(s32[4,8,6]{2,1,0:T(8,128)} %copy.18.cands, s32[4,8]{1,0:T(4,128)} %counts.27, bf16[4,256,768]{2,1,0:T(8,128)(2,1)} %patches.23, bf16[4,64,768]{2,1,0:T(8,128)(2,1)} %copy-done.5, f32[8,128]{1,0:T(8,128)} %get-tuple-element.36.prior), custom_call_target="tpu_custom_call" | custom-call | flops 402653184 | bytes 2490368 | tf_op jit(solution)/shard_map/forward_5/pallas_call | solution.py:114
  47.1 3.3 %forward_6.1 = (bf16[4,256,256]{2,1,0:T(8,128)(2,1)}, f32[8,128]{1,0:T(8,128)}) custom-call(s32[4,8,6]{2,1,0:T(8,128)} %copy.18.cands, s32[4,8]{1,0:T(4,128)} %counts.27, bf16[4,256,768]{2,1,0:T(8,128)(2,1)} %patches.23, bf16[4,64,768]{2,1,0:T(8,128)(2,1)} %copy-done.2, f32[8,128]{1,0:T(8,128)} %get-tuple-element.37.prior), custom_call_target="tpu_custom_call" | custom-call | flops 402653184 | bytes 2490368 | tf_op jit(solution)/shard_map/forward_6/pallas_call | solution.py:114
  50.4 0.7 copy-done.6
  51.1 2.4 %forward_7.1 = (bf16[4,256,256]{2,1,0:T(8,128)(2,1)}, f32[8,128]{1,0:T(8,128)}) custom-call(s32[4,8,6]{2,1,0:T(8,128)} %copy.18.cands, s32[4,8]{1,0:T(4,128)} %counts.27, bf16[4,256,768]{2,1,0:T(8,128)(2,1)} %patches.23, bf16[4,64,768]{2,1,0:T(8,128)(2,1)} %copy-done.6, f32[8,128]{1,0:T(8,128)} %get-tuple-element.38.prior), custom_call_target="tpu_custom_call" | custom-call | flops 402653184 | bytes 2490368 | tf_op jit(solution)/shard_map/forward_7/pallas_call | solution.py:114
  53.5 4.1 %collective-permute-start.7 = (f32[8,128]{1,0:T(8,128)}, f32[8,128]{1,0:T(8,128)S(1)}, u32[]{:S(2)}, u32[]{:S(2)}) collective-permute-start(f32[8,128]{1,0:T(8,128)} %get-tuple-element.39.refs_0_), channel_id=1, source_target_pairs={{0,1},{1,0},{2,3},{3,2},{4,5},{5,4},{6,7},{7,6},{8,9},{9,8},{10,11... | collective-permute-start | bytes 12296 | tf_op jit(solution)/shard_map/ppermute | solution.py:360
  57.6 0.7 constant_dynamic-update-slice_fusion.1
  58.7 8.4 %collective-permute-start.10 = (f32[16,128]{1,0:T(8,128)S(1)}, f32[16,128]{1,0:T(8,128)S(1)}, u32[]{:S(2)}, u32[]{:S(2)}) collective-permute-start(f32[16,128]{1,0:T(8,128)S(1)} %constant_dynamic-update-slice_fusion), channel_id=1, source_target_pairs={{0,6},{1,7},{2,4},{3,5},{4,2},{5,3},{6,0},{7,1},{8,14},{9,15},{10,... | collective-permute-start | bytes 24584 | tf_op jit(solution)/shard_map/ppermute | solution.py:360
  68.8 0.6 fusion
  69.4 2.1 %collective-permute-done.9 = f32[16,128]{1,0:T(8,128)S(1)} collective-permute-done((f32[16,128]{1,0:T(8,128)S(1)}, f32[16,128]{1,0:T(8,128)S(1)}, u32[]{:S(2)}, u32[]{:S(2)}) %collective-permute-start.9) | collective-permute-done | bytes 8224 | tf_op jit(solution)/shard_map/ppermute | solution.py:360
  71.5 0.6 fusion.1
  72.1 0.6 fusion.2
  72.7 2.1 %stats.1 = (f32[8,4,8,128]{3,2,1,0:T(8,128)}, f32[8,128]{1,0:T(8,128)}) custom-call(s32[4,8,6]{2,1,0:T(8,128)} %copy.18.cands, s32[4,8]{1,0:T(4,128)} %counts.27, f32[1]{0:T(128)S(6)} %copy.24.nse, f32[8,128]{1,0:T(8,128)} %get-tuple-element.39.refs_0_, f32[8,128]{1,0:T(8,128)} %copy-done.14, f32[8,128]{1,0:T(8,128)} %get-tuple-element.65.refs_2_, ...), custom_call_target="tpu_custom_call" | custom-call | tf_op jit(solution)/shard_map/stats/pallas_call | solution.py:203
  74.8 3.4 %word_3.1 = (f32[4,64,768]{2,1,0:T(8,128)}, bf16[4,64,768]{2,1,0:T(8,128)(2,1)}) custom-call(s32[4,8,6]{2,1,0:T(8,128)} %copy.18.cands, s32[4,8]{1,0:T(4,128)} %counts.27, bf16[4,256,768]{2,1,0:T(8,128)(2,1)} %patches.23, f32[8,4,8,128]{3,2,1,0:T(8,128)} %get-tuple-element.40.coef, bf16[4,256,256]{2,1,0:T(8,128)(2,1)} %get-tuple-element.47.refs_6_.weights_a, ...), custom_call_target="tpu_custom_call" | custom-call | flops 805306368 | bytes 3801088 | tf_op jit(solution)/shard_map/word_3/pallas_call | solution.py:251
  78.2 3.1 %word_2.1 = (f32[4,64,768]{2,1,0:T(8,128)}, bf16[4,64,768]{2,1,0:T(8,128)(2,1)}) custom-call(s32[4,8,6]{2,1,0:T(8,128)} %copy.18.cands, s32[4,8]{1,0:T(4,128)} %counts.27, bf16[4,256,768]{2,1,0:T(8,128)(2,1)} %patches.23, f32[8,4,8,128]{3,2,1,0:T(8,128)} %get-tuple-element.40.coef, bf16[4,256,256]{2,1,0:T(8,128)(2,1)} %get-tuple-element.45.refs_4_.weights_a, ...), custom_call_target="tpu_custom_call" | custom-call | flops 805306368 | bytes 3801088 | tf_op jit(solution)/shard_map/word_2/pallas_call | solution.py:251
  81.9 4.0 %word_1.1 = (f32[4,64,768]{2,1,0:T(8,128)}, bf16[4,64,768]{2,1,0:T(8,128)(2,1)}) custom-call(s32[4,8,6]{2,1,0:T(8,128)} %copy.18.cands, s32[4,8]{1,0:T(4,128)} %counts.27, bf16[4,256,768]{2,1,0:T(8,128)(2,1)} %patches.23, f32[8,4,8,128]{3,2,1,0:T(8,128)} %get-tuple-element.40.coef, bf16[4,256,256]{2,1,0:T(8,128)(2,1)} %get-tuple-element.43.refs_2_.weights_a, ...), custom_call_target="tpu_custom_call" | custom-call | flops 805306368 | bytes 3801088 | tf_op jit(solution)/shard_map/word_1/pallas_call | solution.py:251
  85.9 3.4 %word_0.1 = (f32[4,64,768]{2,1,0:T(8,128)}, bf16[4,64,768]{2,1,0:T(8,128)(2,1)}) custom-call(s32[4,8,6]{2,1,0:T(8,128)} %copy.18.cands, s32[4,8]{1,0:T(4,128)} %counts.27, bf16[4,256,768]{2,1,0:T(8,128)(2,1)} %patches.23, f32[8,4,8,128]{3,2,1,0:T(8,128)} %get-tuple-element.40.coef, bf16[4,256,256]{2,1,0:T(8,128)(2,1)} %get-tuple-element.41.refs_0_.weights_a, ...), custom_call_target="tpu_custom_call" | custom-call | flops 805306368 | bytes 3801088 | tf_op jit(solution)/shard_map/word_0/pallas_call | solution.py:251
  89.8 0.7 copy-done.9
  90.6 2.0 %join_3.1 = bf16[4,64,768]{2,1,0:T(8,128)(2,1)} custom-call(f32[4,64,768]{2,1,0:T(8,128)} %get-tuple-element.51.refs_0_, bf16[4,64,768]{2,1,0:T(8,128)(2,1)} %copy-done.9), custom_call_target="tpu_custom_call" | custom-call | tf_op jit(solution)/shard_map/join_3/pallas_call | solution.py:323
  92.6 0.9 collective-permute-start.13
  93.6 0.7 copy-done.8
  94.3 2.1 %join_2.1 = bf16[4,64,768]{2,1,0:T(8,128)(2,1)} custom-call(f32[4,64,768]{2,1,0:T(8,128)} %get-tuple-element.53.refs_0_, bf16[4,64,768]{2,1,0:T(8,128)(2,1)} %copy-done.8), custom_call_target="tpu_custom_call" | custom-call | tf_op jit(solution)/shard_map/join_2/pallas_call | solution.py:323
  96.4 1.0 collective-permute-start.15
  97.4 0.7 copy-done.7
  98.2 2.1 %join_1.1 = bf16[4,64,768]{2,1,0:T(8,128)(2,1)} custom-call(f32[4,64,768]{2,1,0:T(8,128)} %get-tuple-element.55.refs_0_, bf16[4,64,768]{2,1,0:T(8,128)(2,1)} %copy-done.7), custom_call_target="tpu_custom_call" | custom-call | tf_op jit(solution)/shard_map/join_1/pallas_call | solution.py:323
  100.2 1.5 %collective-permute-start.17 = (bf16[4,64,768]{2,1,0:T(8,128)(2,1)}, bf16[4,64,768]{2,1,0:T(8,128)(2,1)S(1)}, u32[]{:S(2)}, u32[]{:S(2)}) collective-permute-start(bf16[4,64,768]{2,1,0:T(8,128)(2,1)} %join_1.1), channel_id=1, source_target_pairs={{0,2},{1,3},{2,0},{3,1},{4,6},{5,7},{6,4},{7,5},{8,10},{9,11},{10,... | collective-permute-start | bytes 1179656 | tf_op jit(solution)/shard_map/ppermute | solution.py:360
  101.7 3.3 %collective-permute-start.20 = (f32[8,128]{1,0:T(8,128)S(1)}, f32[8,128]{1,0:T(8,128)S(1)}, u32[]{:S(2)}, u32[]{:S(2)}) collective-permute-start(f32[8,128]{1,0:T(8,128)S(1)} %copy-done.15), channel_id=1, source_target_pairs={{0,24},{8,0},{16,8},{24,16},{1,25},{9,1},{17,9},{25,17},{2,26},{10... | collective-permute-start | bytes 12296 | tf_op jit(solution)/shard_map/ppermute | solution.py:386
  105.1 3.5 %collective-permute-done.20.refs_3_ = f32[8,128]{1,0:T(8,128)S(1)} collective-permute-done((f32[8,128]{1,0:T(8,128)S(1)}, f32[8,128]{1,0:T(8,128)S(1)}, u32[]{:S(2)}, u32[]{:S(2)}) %collective-permute-start.20) | collective-permute-done | bytes 4128 | tf_op jit(solution)/shard_map/ppermute | solution.py:386
  108.5 3.3 %collective-permute-start.19 = (f32[8,128]{1,0:T(8,128)S(1)}, f32[8,128]{1,0:T(8,128)S(1)}, u32[]{:S(2)}, u32[]{:S(2)}) collective-permute-start(f32[8,128]{1,0:T(8,128)S(1)} %copy-done.15), channel_id=1, source_target_pairs={{0,16},{8,24},{16,0},{24,8},{1,17},{9,25},{17,1},{25,9},{2,18},{10... | collective-permute-start | bytes 12296 | tf_op jit(solution)/shard_map/ppermute | solution.py:386
  111.9 1.6 %collective-permute-done.19.refs_2_ = f32[8,128]{1,0:T(8,128)S(1)} collective-permute-done((f32[8,128]{1,0:T(8,128)S(1)}, f32[8,128]{1,0:T(8,128)S(1)}, u32[]{:S(2)}, u32[]{:S(2)}) %collective-permute-start.19) | collective-permute-done | bytes 4128 | tf_op jit(solution)/shard_map/ppermute | solution.py:386
  113.4 1.6 %collective-permute-start.18 = (f32[8,128]{1,0:T(8,128)S(1)}, f32[8,128]{1,0:T(8,128)S(1)}, u32[]{:S(2)}, u32[]{:S(2)}) collective-permute-start(f32[8,128]{1,0:T(8,128)S(1)} %copy-done.15), channel_id=1, source_target_pairs={{0,8},{8,16},{16,24},{24,0},{1,9},{9,17},{17,25},{25,1},{2,10},{10... | collective-permute-start | bytes 12296 | tf_op jit(solution)/shard_map/ppermute | solution.py:386
  115.1 6.9 %patch.1 = bf16[4,256,768]{2,1,0:T(8,128)(2,1)} custom-call(s32[4,8,6]{2,1,0:T(8,128)} %copy.18.cands, s32[4,8]{1,0:T(4,128)} %counts.27, f32[8,4,8,128]{3,2,1,0:T(8,128)} %get-tuple-element.40.coef, bf16[4,256,256]{2,1,0:T(8,128)(2,1)} %get-tuple-element.41.refs_0_.weights_a, bf16[4,256,256]{2,1,0:T(8,128)(2,1)} %get-tuple-element.42.refs_1_.weights_b, ...), custom_call_target="tpu_custom_call" | custom-call | flops 3221225472 | bytes 8912896 | tf_op jit(solution)/shard_map/patch/pallas_call | solution.py:299
  122.6 1.3 %scalars.1 = (f32[1]{0:T(128)}, f32[1]{0:T(128)}) custom-call(f32[8,128]{1,0:T(8,128)} %get-tuple-element.57.refs_0_, f32[8,128]{1,0:T(8,128)} %copy-done.18, f32[8,128]{1,0:T(8,128)} %copy-done.17, f32[8,128]{1,0:T(8,128)} %copy-done.16), custom_call_target="tpu_custom_call" | custom-call | tf_op jit(solution)/shard_map/scalars/pallas_call | solution.py:343
  124.0 0.7 copy-done.10
  125.1 2.6 %finish.1 = bf16[4,64,768]{2,1,0:T(8,128)(2,1)} custom-call(f32[4,64,768]{2,1,0:T(8,128)} %get-tuple-element.49.refs_0_, bf16[4,64,768]{2,1,0:T(8,128)(2,1)} %copy-done.10, bf16[4,64,768]{2,1,0:T(8,128)(2,1)} %copy-done.11, bf16[4,64,768]{2,1,0:T(8,128)(2,1)} %copy-done.12, bf16[4,64,768]{2,1,0:T(8,128)(2,1)} %copy-done.13), custom_call_target="tpu_custom_call" | custom-call | tf_op jit(solution)/shard_map/finish/pallas_call | solution.py:323
  (58 shorter events, 3.9 us)
Async XLA Ops:
  0.6 13.2 %collective-permute-start.4 = (bf16[4,64,768]{2,1,0:T(8,128)(2,1)}, bf16[4,64,768]{2,1,0:T(8,128)(2,1)S(1)}, u32[]{:S(2)}, u32[]{:S(2)}) collective-permute-start(bf16[4,64,768]{2,1,0:T(8,128)(2,1)} %refs_8_.1), channel_id=1, source_target_pairs={{0,2},{1,3},{2,0},{3,1},{4,6},{5,7},{6,4},{7,5},{8,10},{9,11},{10,... | collective-permute-start | bytes 1179656 | tf_op jit(solution)/shard_map/ppermute | solution.py:360
  3.6 19.2 %collective-permute-start.2 = (bf16[4,64,768]{2,1,0:T(8,128)(2,1)}, bf16[4,64,768]{2,1,0:T(8,128)(2,1)S(1)}, u32[]{:S(2)}, u32[]{:S(2)}) collective-permute-start(bf16[4,64,768]{2,1,0:T(8,128)(2,1)} %refs_8_.1), channel_id=1, source_target_pairs={{0,4},{1,5},{2,6},{3,7},{4,0},{5,1},{6,2},{7,3},{8,12},{9,13},{10,... | collective-permute-start | bytes 1179656 | tf_op jit(solution)/shard_map/ppermute | solution.py:360
  5.2 17.7 %collective-permute-start = (bf16[4,64,768]{2,1,0:T(8,128)(2,1)}, bf16[4,64,768]{2,1,0:T(8,128)(2,1)S(1)}, u32[]{:S(2)}, u32[]{:S(2)}) collective-permute-start(bf16[4,64,768]{2,1,0:T(8,128)(2,1)} %refs_8_.1), channel_id=1, source_target_pairs={{0,6},{1,7},{2,4},{3,5},{4,2},{5,3},{6,0},{7,1},{8,14},{9,15},{10,... | collective-permute-start | bytes 1179656 | tf_op jit(solution)/shard_map/ppermute | solution.py:360
  5.2 25.9 %collective-permute-start.6 = (bf16[4,64,768]{2,1,0:T(8,128)(2,1)}, bf16[4,64,768]{2,1,0:T(8,128)(2,1)S(1)}, u32[]{:S(2)}, u32[]{:S(2)}) collective-permute-start(bf16[4,64,768]{2,1,0:T(8,128)(2,1)} %refs_8_.1), channel_id=1, source_target_pairs={{0,1},{1,0},{2,3},{3,2},{4,5},{5,4},{6,7},{7,6},{8,9},{9,8},{10,11... | collective-permute-start | bytes 1179656 | tf_op jit(solution)/shard_map/ppermute | solution.py:360
  13.8 20.4 %copy-start = (bf16[4,64,768]{2,1,0:T(8,128)(2,1)}, bf16[4,64,768]{2,1,0:T(8,128)(2,1)S(1)}, u32[]{:S(2)}) copy-start(bf16[4,64,768]{2,1,0:T(8,128)(2,1)S(1)} %collective-permute-done.4.words.refs_10_) | copy-start | bytes 1179652
  13.8 23.7 %collective-permute-start.5 = (bf16[4,64,768]{2,1,0:T(8,128)(2,1)S(1)}, bf16[4,64,768]{2,1,0:T(8,128)(2,1)S(1)}, u32[]{:S(2)}, u32[]{:S(2)}) collective-permute-start(bf16[4,64,768]{2,1,0:T(8,128)(2,1)S(1)} %collective-permute-done.4.words.refs_10_), channel_id=1, source_target_pairs={{0,1},{1,0},{2,3},{3,2},{4,5},{5,4},{6,7},{7,6},{8,9},{9,8},{10,11... | collective-permute-start | bytes 1179656 | tf_op jit(solution)/shard_map/ppermute | solution.py:360
  22.8 11.4 %copy-start.1 = (bf16[4,64,768]{2,1,0:T(8,128)(2,1)}, bf16[4,64,768]{2,1,0:T(8,128)(2,1)S(1)}, u32[]{:S(2)}) copy-start(bf16[4,64,768]{2,1,0:T(8,128)(2,1)S(1)} %collective-permute-done.2.words.refs_12_) | copy-start | bytes 1179652
  22.8 21.1 %collective-permute-start.3 = (bf16[4,64,768]{2,1,0:T(8,128)(2,1)S(1)}, bf16[4,64,768]{2,1,0:T(8,128)(2,1)S(1)}, u32[]{:S(2)}, u32[]{:S(2)}) collective-permute-start(bf16[4,64,768]{2,1,0:T(8,128)(2,1)S(1)} %collective-permute-done.2.words.refs_12_), channel_id=1, source_target_pairs={{0,1},{1,0},{2,3},{3,2},{4,5},{5,4},{6,7},{7,6},{8,9},{9,8},{10,11... | collective-permute-start | bytes 1179656 | tf_op jit(solution)/shard_map/ppermute | solution.py:360
  22.9 11.4 %copy-start.2 = (bf16[4,64,768]{2,1,0:T(8,128)(2,1)}, bf16[4,64,768]{2,1,0:T(8,128)(2,1)S(1)}, u32[]{:S(2)}) copy-start(bf16[4,64,768]{2,1,0:T(8,128)(2,1)S(1)} %collective-permute-done.words.refs_14_) | copy-start | bytes 1179652
  22.9 27.5 %collective-permute-start.1 = (bf16[4,64,768]{2,1,0:T(8,128)(2,1)S(1)}, bf16[4,64,768]{2,1,0:T(8,128)(2,1)S(1)}, u32[]{:S(2)}, u32[]{:S(2)}) collective-permute-start(bf16[4,64,768]{2,1,0:T(8,128)(2,1)S(1)} %collective-permute-done.words.refs_14_), channel_id=1, source_target_pairs={{0,1},{1,0},{2,3},{3,2},{4,5},{5,4},{6,7},{7,6},{8,9},{9,8},{10,11... | collective-permute-start | bytes 1179656 | tf_op jit(solution)/shard_map/ppermute | solution.py:360
  31.1 0.7 copy-start.3
  37.5 0.8 copy-start.4
  44.0 0.8 copy-start.5
  50.4 0.7 copy-start.6
  53.5 5.2 %collective-permute-start.7 = (f32[8,128]{1,0:T(8,128)}, f32[8,128]{1,0:T(8,128)S(1)}, u32[]{:S(2)}, u32[]{:S(2)}) collective-permute-start(f32[8,128]{1,0:T(8,128)} %get-tuple-element.39.refs_0_), channel_id=1, source_target_pairs={{0,1},{1,0},{2,3},{3,2},{4,5},{5,4},{6,7},{7,6},{8,9},{9,8},{10,11... | collective-permute-start | bytes 12296 | tf_op jit(solution)/shard_map/ppermute | solution.py:360
  58.7 14.0 %copy-start.14 = (f32[8,128]{1,0:T(8,128)}, f32[8,128]{1,0:T(8,128)S(1)}, u32[]{:S(2)}) copy-start(f32[8,128]{1,0:T(8,128)S(1)} %collective-permute-done.7.refs_1_) | copy-start | bytes 12292
  58.7 10.1 %collective-permute-start.10 = (f32[16,128]{1,0:T(8,128)S(1)}, f32[16,128]{1,0:T(8,128)S(1)}, u32[]{:S(2)}, u32[]{:S(2)}) collective-permute-start(f32[16,128]{1,0:T(8,128)S(1)} %constant_dynamic-update-slice_fusion), channel_id=1, source_target_pairs={{0,6},{1,7},{2,4},{3,5},{4,2},{5,3},{6,0},{7,1},{8,14},{9,15},{10,... | collective-permute-start | bytes 24584 | tf_op jit(solution)/shard_map/ppermute | solution.py:360
  67.8 3.7 %collective-permute-start.9 = (f32[16,128]{1,0:T(8,128)S(1)}, f32[16,128]{1,0:T(8,128)S(1)}, u32[]{:S(2)}, u32[]{:S(2)}) collective-permute-start(f32[16,128]{1,0:T(8,128)S(1)} %constant_dynamic-update-slice_fusion), channel_id=1, source_target_pairs={{0,4},{1,5},{2,6},{3,7},{4,0},{5,1},{6,2},{7,3},{8,12},{9,13},{10,... | collective-permute-start | bytes 24584 | tf_op jit(solution)/shard_map/ppermute | solution.py:360
  67.9 4.2 %collective-permute-start.8 = (f32[16,128]{1,0:T(8,128)S(1)}, f32[16,128]{1,0:T(8,128)S(1)}, u32[]{:S(2)}, u32[]{:S(2)}) collective-permute-start(f32[16,128]{1,0:T(8,128)S(1)} %constant_dynamic-update-slice_fusion), channel_id=1, source_target_pairs={{0,2},{1,3},{2,0},{3,1},{4,6},{5,7},{6,4},{7,5},{8,10},{9,11},{10,... | collective-permute-start | bytes 24584 | tf_op jit(solution)/shard_map/ppermute | solution.py:360
  78.2 11.6 %collective-permute-start.12 = (bf16[4,64,768]{2,1,0:T(8,128)(2,1)}, bf16[4,64,768]{2,1,0:T(8,128)(2,1)S(1)}, u32[]{:S(2)}, u32[]{:S(2)}) collective-permute-start(bf16[4,64,768]{2,1,0:T(8,128)(2,1)} %get-tuple-element.52), channel_id=1, source_target_pairs={{0,1},{1,0},{2,3},{3,2},{4,5},{5,4},{6,7},{7,6},{8,9},{9,8},{10,11... | collective-permute-start | bytes 1179656 | tf_op jit(solution)/shard_map/ppermute | solution.py:360
  81.4 12.2 %collective-permute-start.14 = (bf16[4,64,768]{2,1,0:T(8,128)(2,1)}, bf16[4,64,768]{2,1,0:T(8,128)(2,1)S(1)}, u32[]{:S(2)}, u32[]{:S(2)}) collective-permute-start(bf16[4,64,768]{2,1,0:T(8,128)(2,1)} %get-tuple-element.54), channel_id=1, source_target_pairs={{0,1},{1,0},{2,3},{3,2},{4,5},{5,4},{6,7},{7,6},{8,9},{9,8},{10,11... | collective-permute-start | bytes 1179656 | tf_op jit(solution)/shard_map/ppermute | solution.py:360
  85.9 11.5 %collective-permute-start.16 = (bf16[4,64,768]{2,1,0:T(8,128)(2,1)}, bf16[4,64,768]{2,1,0:T(8,128)(2,1)S(1)}, u32[]{:S(2)}, u32[]{:S(2)}) collective-permute-start(bf16[4,64,768]{2,1,0:T(8,128)(2,1)} %get-tuple-element.56), channel_id=1, source_target_pairs={{0,1},{1,0},{2,3},{3,2},{4,5},{5,4},{6,7},{7,6},{8,9},{9,8},{10,11... | collective-permute-start | bytes 1179656 | tf_op jit(solution)/shard_map/ppermute | solution.py:360
  89.3 34.6 %collective-permute-start.11 = (bf16[4,64,768]{2,1,0:T(8,128)(2,1)}, bf16[4,64,768]{2,1,0:T(8,128)(2,1)S(1)}, u32[]{:S(2)}, u32[]{:S(2)}) collective-permute-start(bf16[4,64,768]{2,1,0:T(8,128)(2,1)} %get-tuple-element.50), channel_id=1, source_target_pairs={{0,1},{1,0},{2,3},{3,2},{4,5},{5,4},{6,7},{7,6},{8,9},{9,8},{10,11... | collective-permute-start | bytes 1179656 | tf_op jit(solution)/shard_map/ppermute | solution.py:360
  89.8 0.8 copy-start.9
  92.6 31.3 %collective-permute-start.13 = (bf16[4,64,768]{2,1,0:T(8,128)(2,1)}, bf16[4,64,768]{2,1,0:T(8,128)(2,1)S(1)}, u32[]{:S(2)}, u32[]{:S(2)}) collective-permute-start(bf16[4,64,768]{2,1,0:T(8,128)(2,1)} %join_3.1), channel_id=1, source_target_pairs={{0,6},{1,7},{2,4},{3,5},{4,2},{5,3},{6,0},{7,1},{8,14},{9,15},{10,... | collective-permute-start | bytes 1179656 | tf_op jit(solution)/shard_map/ppermute | solution.py:360
  93.6 0.7 copy-start.8
  94.3 7.4 %copy-start.15 = (f32[8,128]{1,0:T(8,128)S(1)}, f32[8,128]{1,0:T(8,128)}, u32[]{:S(2)}) copy-start(f32[8,128]{1,0:T(8,128)} %get-tuple-element.57.refs_0_) | copy-start | bytes 12292
  96.4 27.6 %collective-permute-start.15 = (bf16[4,64,768]{2,1,0:T(8,128)(2,1)}, bf16[4,64,768]{2,1,0:T(8,128)(2,1)S(1)}, u32[]{:S(2)}, u32[]{:S(2)}) collective-permute-start(bf16[4,64,768]{2,1,0:T(8,128)(2,1)} %join_2.1), channel_id=1, source_target_pairs={{0,4},{1,5},{2,6},{3,7},{4,0},{5,1},{6,2},{7,3},{8,12},{9,13},{10,... | collective-permute-start | bytes 1179656 | tf_op jit(solution)/shard_map/ppermute | solution.py:360
  97.4 0.7 copy-start.7
  100.2 23.7 %collective-permute-start.17 = (bf16[4,64,768]{2,1,0:T(8,128)(2,1)}, bf16[4,64,768]{2,1,0:T(8,128)(2,1)S(1)}, u32[]{:S(2)}, u32[]{:S(2)}) collective-permute-start(bf16[4,64,768]{2,1,0:T(8,128)(2,1)} %join_1.1), channel_id=1, source_target_pairs={{0,2},{1,3},{2,0},{3,1},{4,6},{5,7},{6,4},{7,5},{8,10},{9,11},{10,... | collective-permute-start | bytes 1179656 | tf_op jit(solution)/shard_map/ppermute | solution.py:360
  101.7 6.8 %collective-permute-start.20 = (f32[8,128]{1,0:T(8,128)S(1)}, f32[8,128]{1,0:T(8,128)S(1)}, u32[]{:S(2)}, u32[]{:S(2)}) collective-permute-start(f32[8,128]{1,0:T(8,128)S(1)} %copy-done.15), channel_id=1, source_target_pairs={{0,24},{8,0},{16,8},{24,16},{1,25},{9,1},{17,9},{25,17},{2,26},{10... | collective-permute-start | bytes 12296 | tf_op jit(solution)/shard_map/ppermute | solution.py:386
  108.5 13.4 %copy-start.16 = (f32[8,128]{1,0:T(8,128)}, f32[8,128]{1,0:T(8,128)S(1)}, u32[]{:S(2)}) copy-start(f32[8,128]{1,0:T(8,128)S(1)} %collective-permute-done.20.refs_3_) | copy-start | bytes 12292
  108.5 4.9 %collective-permute-start.19 = (f32[8,128]{1,0:T(8,128)S(1)}, f32[8,128]{1,0:T(8,128)S(1)}, u32[]{:S(2)}, u32[]{:S(2)}) collective-permute-start(f32[8,128]{1,0:T(8,128)S(1)} %copy-done.15), channel_id=1, source_target_pairs={{0,16},{8,24},{16,0},{24,8},{1,17},{9,25},{17,1},{25,9},{2,18},{10... | collective-permute-start | bytes 12296 | tf_op jit(solution)/shard_map/ppermute | solution.py:386
  113.4 8.6 %copy-start.17 = (f32[8,128]{1,0:T(8,128)}, f32[8,128]{1,0:T(8,128)S(1)}, u32[]{:S(2)}) copy-start(f32[8,128]{1,0:T(8,128)S(1)} %collective-permute-done.19.refs_2_) | copy-start | bytes 12292
  113.4 8.6 %collective-permute-start.18 = (f32[8,128]{1,0:T(8,128)S(1)}, f32[8,128]{1,0:T(8,128)S(1)}, u32[]{:S(2)}, u32[]{:S(2)}) collective-permute-start(f32[8,128]{1,0:T(8,128)S(1)} %copy-done.15), channel_id=1, source_target_pairs={{0,8},{8,16},{16,24},{24,0},{1,9},{9,17},{17,25},{25,1},{2,10},{10... | collective-permute-start | bytes 12296 | tf_op jit(solution)/shard_map/ppermute | solution.py:386
  122.0 0.6 copy-start.18
  123.9 0.8 copy-start.10
  123.9 0.9 copy-start.11
  124.0 1.0 copy-start.12
  124.0 1.1 copy-start.13

commit v2 on v1

v2 whole, which is shorter than its diff:
```python
import functools
import math

import jax
import jax.numpy as jnp
from jax import lax
from jax.experimental import pallas as pl
from jax.experimental.pallas import tpu as pltpu
from jax.sharding import PartitionSpec as P

sharpness = 4.0
loss_scale = 65536.0
far_below = -1e30
F32 = jnp.float32
BF16 = jnp.bfloat16
LANES = 128
ROWS = 8

NT = (((1,), (1,)), ((), ()))
NN = (((1,), (0,)), ((), ()))
TN = (((0,), (0,)), ((), ()))


def spec(space=pltpu.VMEM):
    return pl.BlockSpec(memory_space=space)


def near(*arrays):
    return tuple(pltpu.with_memory_space_constraint(x, pltpu.VMEM) for x in arrays)


def tiny():
    return pl.CostEstimate(flops=1, bytes_accessed=1, transcendentals=0)


def params(mib):
    return pltpu.CompilerParams(vmem_limit_bytes=mib << 20)


def fill_meta(cands, counts, nse, per, total, meta):
    row = lax.axis_index("img")
    me = lax.axis_index("cap")
    slots = cands.shape[0]
    sub = lax.broadcasted_iota(jnp.int32, (ROWS, LANES), 0)
    lane = lax.broadcasted_iota(jnp.int32, (ROWS, LANES), 1)
    column = lane // per
    first = sub < per
    for g in range(total // 2):
        even, odd = me ^ (2 * g), me ^ (2 * g + 1)
        live = jnp.zeros((ROWS, LANES), F32)
        for s in range(slots):
            here = jnp.where(s < counts[row, even], cands[s, row, even], -1)
            there = jnp.where(s < counts[row, odd], cands[s, row, odd], -1)
            live = jnp.where(column == jnp.where(first, here, there), 1.0, live)
        meta[g] = jnp.where(sub < 2 * per, live, 0.0)
    for part in range(total // ROWS):
        live = jnp.zeros((ROWS, LANES), F32)
        for s in range(slots):
            target = jnp.where(s < counts[row, me], cands[s, row, me], -1)
            live = jnp.where((me ^ (sub + ROWS * part)) == target, 1.0, live)
        meta[total // 2 + part] = live
    meta[meta.shape[0] - 1] = jnp.exp(jnp.full((ROWS, LANES), nse[0], F32))


def block_is_live(meta, total, offset):
    return meta[total // 2 + offset // ROWS, offset % ROWS, 0] > 0.0


def forward_kernel(offset, pieces, total, *refs):
    if offset:
        meta, patches, prior, *words = refs[: 3 + pieces]
    else:
        cands, counts, nse, patches, *words = refs[: 4 + pieces]
    weights_out, scores_out = refs[-4 - (not offset) :][:2]
    low, high = refs[-2:]
    me = lax.axis_index("cap")
    column = me ^ offset
    per, patch, width = patches.shape
    tokens = words[0].shape[1]
    lines = per * tokens
    scale = sharpness * width**-0.5 * math.log2(math.e)

    def start():
        scores_out[...] = prior[...] if offset else jnp.zeros(scores_out.shape, F32)

    start()
    if not offset:
        fill_meta(cands, counts, nse, per, total, refs[-3])

    def score():
        sub = lax.broadcasted_iota(jnp.int32, (ROWS, LANES), 0)
        lane = lax.broadcasted_iota(jnp.int32, (ROWS, LANES), 1)
        spot = lane == column * per + sub

        def place(i, over_words, over_patches):
            part = jnp.sum(over_words, axis=1, keepdims=True) * (1.0 / patch)
            part = part + over_patches * (1.0 / tokens)
            part = part * (0.5 * math.log(2.0) / sharpness)
            part = jnp.concatenate([part, jnp.zeros((ROWS - per, 1), F32)], axis=0)
            line = jnp.sum(jnp.where(spot & (sub < per), part, 0.0), axis=0, keepdims=True)
            return jnp.where(sub == i, line, 0.0)

        word_rows = jnp.concatenate(
            [w[...].reshape(w.shape[0] * tokens, width) for w in words], axis=0
        )
        low[...] = jnp.full(low.shape, 1.0, F32)
        high[...] = jnp.full(high.shape, 1.0, F32)
        tile = jnp.zeros((ROWS, LANES), F32)
        for i in range(per):
            raw = lax.dot_general(word_rows, patches[i], NT, preferred_element_type=F32)
            mass = jnp.exp2(raw * scale)
            mass3 = mass.reshape(per, tokens, patch)
            word_sum = jnp.sum(mass3, axis=1)
            patch_sum = jnp.sum(mass, axis=1, keepdims=True)
            low[...] = jnp.minimum(low[...], jnp.min(word_sum, axis=0, keepdims=True))
            high[...] = jnp.maximum(high[...], jnp.max(word_sum, axis=0, keepdims=True))
            low[...] = jnp.minimum(low[...], jnp.min(patch_sum, axis=0, keepdims=True))
            high[...] = jnp.maximum(high[...], jnp.max(patch_sum, axis=0, keepdims=True))
            word_part = (0.5 / patch) / word_sum
            patch_part = (0.5 / tokens) / patch_sum
            blended = mass3 * (word_part[:, None, :] + patch_part.reshape(per, tokens, 1))
            weights_out[i] = blended.reshape(lines, patch).astype(BF16)
            patch_logs = jnp.sum(jnp.log2(patch_sum).reshape(per, tokens, 1), axis=1)
            tile = tile + place(i, jnp.log2(word_sum), patch_logs)
        scores_out[...] += tile
        safe = (jnp.min(low[...]) > 2.0**-90) & (jnp.max(high[...]) < 2.0**120)

        @pl.when(jnp.logical_not(safe))
        def _():
            start()

            def image(i, carry):
                raw = lax.dot_general(word_rows, patches[i], NT, preferred_element_type=F32)
                lifted = raw * scale
                lifted3 = lifted.reshape(per, tokens, patch)
                word_top = jnp.max(lifted3, axis=1)
                patch_top = jnp.max(lifted, axis=1, keepdims=True)
                word_mass = jnp.exp2(lifted3 - word_top[:, None, :])
                patch_mass = jnp.exp2(lifted - patch_top).reshape(per, tokens, patch)
                word_sum = jnp.sum(word_mass, axis=1)
                patch_sum = jnp.sum(patch_mass, axis=2, keepdims=True)
                word_part = (0.5 / patch) / word_sum
                patch_part = (0.5 / tokens) / patch_sum
                blended = word_mass * word_part[:, None, :] + patch_mass * patch_part
                weights_out[i] = blended.reshape(lines, patch).astype(BF16)
                patch_logs = jnp.sum(
                    patch_top.reshape(per, tokens, 1) + jnp.log2(patch_sum), axis=1
                )
                scores_out[...] += place(i, word_top + jnp.log2(word_sum), patch_logs)
                return carry

            lax.fori_loop(0, per, image, 0)

    if offset:
        pl.when(block_is_live(meta, total, offset))(score)
    else:
        score()


def forward_call(offset, total, patches, words, extra):
    per, patch, width = patches.shape
    lines = per * words[0].shape[1]
    shapes = (pltpu.VMEM((per, lines, patch), BF16), pltpu.VMEM((ROWS, LANES), F32))
    if offset:
        meta, prior = extra
        args = near(meta, patches, prior, *words)
        specs = [spec()] * len(args)
    else:
        args = (*extra, *near(patches, *words))
        specs = [spec(pltpu.SMEM)] * 3 + [spec()] * (len(args) - 3)
        shapes += (pltpu.VMEM((total // 2 + total // ROWS + 1, ROWS, LANES), F32),)
    return pl.pallas_call(
        functools.partial(forward_kernel, offset, len(words), total),
        out_shape=shapes,
        in_specs=specs,
        out_specs=(spec(),) * len(shapes),
        scratch_shapes=[pltpu.VMEM((1, patch), F32), pltpu.VMEM((1, patch), F32)],
        compiler_params=params(12),
        cost_estimate=tiny(),
        name=f"forward_{offset}",
    )(*args)


def stats_kernel(total, images, per, width, meta, *refs):
    tiles = refs[: total // 2]
    coef_out, sums_out = refs[total // 2 :]
    me = lax.axis_index("cap")
    sub = lax.broadcasted_iota(jnp.int32, (ROWS, LANES), 0)
    lane = lax.broadcasted_iota(jnp.int32, (ROWS, LANES), 1)
    first = sub < per
    image = jnp.where(first, sub, sub - per)
    softness = meta[meta.shape[0] - 1]
    kept, lives, marks = [], [], []
    peak = jnp.full((1, LANES), far_below, F32)
    for g in range(total // 2):
        even, odd = me ^ (2 * g), me ^ (2 * g + 1)
        live = meta[g] > 0.0
        masked = jnp.where(live, tiles[g][...] * softness, far_below)
        kept.append(masked)
        lives.append(live)
        marks.append(live & (lane == jnp.where(first, even, odd) * per + image))
        peak = jnp.maximum(peak, jnp.max(masked, axis=0, keepdims=True))
    mass = jnp.zeros((1, LANES), F32)
    for masked, live in zip(kept, lives):
        mass = mass + jnp.sum(
            jnp.where(live, jnp.exp(masked - peak), 0.0), axis=0, keepdims=True
        )
    col_ok = lane[:1] < total * per
    col_lse = jnp.where(col_ok, peak + jnp.log(jnp.where(col_ok, mass, 1.0)), 0.0)
    loss = jnp.where(sub == 0, col_lse, 0.0)
    temp = jnp.zeros((ROWS, LANES), F32)
    pulls = []
    for masked, live, mark in zip(kept, lives, marks):
        top = jnp.max(masked, axis=1, keepdims=True)
        part = jnp.sum(jnp.where(live, jnp.exp(masked - top), 0.0), axis=1, keepdims=True)
        row_lse = top + jnp.log(jnp.where(sub[:, :1] < 2 * per, part, 1.0))
        pull = jnp.where(
            live,
            (0.5 / images)
            * (jnp.exp(masked - row_lse) + jnp.exp(masked - col_lse) - jnp.where(mark, 2.0, 0.0)),
            0.0,
        )
        pulls.append(pull)
        temp = temp + jnp.where(live, pull * masked, 0.0)
        loss = loss + jnp.where((lane == 0) & (sub < 2 * per), row_lse, 0.0)
        loss = loss - jnp.where(mark, 2.0 * masked, 0.0)
    loss_total = jnp.sum(loss) * (0.5 / images)
    temp_total = jnp.sum(temp)
    sums_out[...] = jnp.where(sub == 0, loss_total, temp_total)
    factor = pulls[0] * softness * (loss_scale * width**-0.5)
    for k in range(total):
        spot = (lane == (me ^ k) * per + sub) & first
        for i in range(per):
            line = jnp.broadcast_to(factor[i : i + 1], (ROWS, LANES))
            value = jnp.sum(jnp.where(spot, line, 0.0), axis=1, keepdims=True)
            coef_out[k, i] = jnp.broadcast_to(value, (ROWS, LANES))


def stats_call(images, per, width, meta, tiles):
    total = 2 * len(tiles)
    return pl.pallas_call(
        functools.partial(stats_kernel, total, images, per, width),
        out_shape=(
            pltpu.VMEM((total, per, ROWS, LANES), F32),
            pltpu.VMEM((ROWS, LANES), F32),
        ),
        in_specs=[spec()] * (1 + len(tiles)),
        out_specs=(spec(), spec()),
        compiler_params=params(4),
        cost_estimate=tiny(),
        name="stats",
    )(*near(meta, *tiles))


def pair_kernel(per, own, other, out):
    sub = lax.broadcasted_iota(jnp.int32, (ROWS, LANES), 0)
    moved = jnp.concatenate([other[...]] * 2, axis=0)[ROWS - per : 2 * ROWS - per]
    out[...] = jnp.where(sub < per, own[...], moved)


def pair_call(per, own, other):
    return pl.pallas_call(
        functools.partial(pair_kernel, per),
        out_shape=pltpu.VMEM((ROWS, LANES), F32),
        in_specs=[spec()] * 2,
        out_specs=spec(),
        compiler_params=params(4),
        cost_estimate=tiny(),
        name="pair",
    )(*near(own, other))


def scaled(weights, coef, i, per):
    lines, patch = weights.shape[1:]
    block = weights[i].astype(F32).reshape(per, lines // per, patch)
    factor = jnp.tile(coef[i, :per][:, None, :], (1, 1, patch // LANES))
    return (block * factor).reshape(lines, patch).astype(BF16)


def word_kernel(group, total, meta, patches, coef, weights_a, weights_b, low_out, high_out, out_b):
    per, patch, width = patches.shape
    half = low_out.shape[0]
    for n, weights in enumerate((weights_a, weights_b)):
        offset = 2 * group + n
        shape = (per, weights.shape[1] // per, width)

        def put(value):
            if n:
                out_b[...] = value.astype(out_b.dtype)
            else:
                low_out[...] = value[:half]
                high_out[...] = value[half:]

        def run():
            wide = jnp.concatenate(
                [scaled(weights, coef.at[offset], i, per) for i in range(per)], axis=1
            )
            rows = patches[...].reshape(per * patch, width)
            put(lax.dot_general(wide, rows, NN, preferred_element_type=F32).reshape(shape))

        if offset:
            live = block_is_live(meta, total, offset)
            pl.when(live)(run)
            pl.when(jnp.logical_not(live))(lambda: put(jnp.zeros(shape, F32)))
        else:
            run()


def word_call(group, total, meta, patches, coef, weights_a, weights_b):
    per, patch, width = patches.shape
    shape = (per, weights_a.shape[1] // per, width)
    part = (per // 2, *shape[1:])
    return pl.pallas_call(
        functools.partial(word_kernel, group, total),
        out_shape=(pltpu.VMEM(part, F32), pltpu.VMEM(part, F32), pltpu.VMEM(shape, BF16)),
        in_specs=[spec()] * 5,
        out_specs=(spec(),) * 3,
        compiler_params=params(12),
        cost_estimate=tiny(),
        name=f"word_{group}",
    )(*near(meta, patches, coef, weights_a, weights_b))


def patch_kernel(total, split, meta, coef, *refs):
    weights, words, out, acc = refs[:total], refs[total:-2], refs[-2], refs[-1]
    per, patch, width = out.shape
    for k in range(total):
        pieces, words = words[: split[k]], words[split[k] :]

        def add(k=k, pieces=pieces):
            word_rows = jnp.concatenate(
                [w[...].reshape(w.shape[0] * w.shape[1], width) for w in pieces], axis=0
            )
            for i in range(per):
                part = lax.dot_general(
                    scaled(weights[k], coef.at[k], i, per),
                    word_rows,
                    TN,
                    preferred_element_type=F32,
                )
                if k:
                    acc[i] += part
                else:
                    acc[i] = part

        if k:
            pl.when(block_is_live(meta, total, k))(add)
        else:
            add()
    out[...] = acc[...].astype(BF16)


def patch_call(meta, coef, weights, words, shape):
    total = len(weights)
    flat = [piece for pieces in words for piece in pieces]
    return pl.pallas_call(
        functools.partial(patch_kernel, total, tuple(len(p) for p in words)),
        out_shape=jax.ShapeDtypeStruct(shape, BF16),
        in_specs=[spec()] * (2 + total + len(flat)),
        out_specs=spec(),
        scratch_shapes=[pltpu.VMEM(shape, F32)],
        compiler_params=params(16),
        cost_estimate=tiny(),
        name="patch",
    )(*near(meta, coef, *weights, *flat))


def half_kernel(start, x, out):
    out[...] = x[start : start + out.shape[0]]


def half_call(start, x):
    count = x.shape[0] // 2
    return pl.pallas_call(
        functools.partial(half_kernel, start),
        out_shape=pltpu.VMEM((count, *x.shape[1:]), x.dtype),
        in_specs=[spec()],
        out_specs=spec(),
        compiler_params=params(4),
        cost_estimate=tiny(),
        name=f"half_{start}",
    )(*near(x))


def join_kernel(low, high, sibling, low_out, high_out):
    half = low.shape[0]
    low_out[...] = (low[...] + sibling[:half].astype(F32)).astype(low_out.dtype)
    high_out[...] = (high[...] + sibling[half:].astype(F32)).astype(high_out.dtype)


def join_call(name, low, high, sibling, low_type, high_type):
    return pl.pallas_call(
        join_kernel,
        out_shape=(pltpu.VMEM(low.shape, low_type), pltpu.VMEM(high.shape, high_type)),
        in_specs=[spec()] * 3,
        out_specs=(spec(),) * 2,
        compiler_params=params(4),
        cost_estimate=tiny(),
        name=name,
    )(*near(low, high, sibling))


def add_kernel(*refs):
    total = refs[0][...].astype(F32)
    for ref in refs[1:-1]:
        total = total + ref[...].astype(F32)
    refs[-1][...] = total.astype(refs[-1].dtype)


def add_call(name, dtype, *arrays):
    return pl.pallas_call(
        add_kernel,
        out_shape=pltpu.VMEM(arrays[0].shape, dtype),
        in_specs=[spec()] * len(arrays),
        out_specs=spec(),
        compiler_params=params(4),
        cost_estimate=tiny(),
        name=name,
    )(*near(*arrays))


def finish_kernel(count, *refs):
    out = refs[-1]
    half = out.shape[0] // 2
    for n, part in enumerate((refs[:count], refs[count:-1])):
        total = part[0][...]
        for ref in part[1:]:
            total = total + ref[...].astype(F32)
        out[half * n : half * (n + 1)] = total.astype(BF16)


def finish_call(lows, highs, shape):
    return pl.pallas_call(
        functools.partial(finish_kernel, len(lows)),
        out_shape=jax.ShapeDtypeStruct(shape, BF16),
        in_specs=[spec()] * (len(lows) + len(highs)),
        out_specs=spec(),
        compiler_params=params(8),
        cost_estimate=tiny(),
        name="finish",
    )(*near(*lows, *highs))


def scalar_kernel(mine, other, loss_out, temp_out):
    total = mine[...] + other[...]
    loss_out[0] = total[0, 0]
    temp_out[0] = total[1, 0]


def scalar_call(mine, other):
    one = jax.ShapeDtypeStruct((1,), F32)
    return pl.pallas_call(
        scalar_kernel,
        out_shape=(one, one),
        in_specs=[spec()] * 2,
        out_specs=(spec(pltpu.SMEM), spec(pltpu.SMEM)),
        compiler_params=params(4),
        cost_estimate=tiny(),
        name="scalars",
    )(*near(mine, other))


def body(patches, words, natural_sharpness_exponent, candidates, counts):
    total = lax.axis_size("cap")
    rows = lax.axis_size("img")
    per, patch, width = patches.shape
    images = per * total * rows
    groups = total // 2
    half = per // 2
    bits = [1 << n for n in range(groups.bit_length() - 1)]
    barrier = lax.optimization_barrier

    def low_bit(g):
        return g & -g

    def high_bit(g):
        return 1 << (g.bit_length() - 1)

    def hop(x, offset):
        return lax.ppermute(x, "cap", [(i, i ^ offset) for i in range(total)])

    words_at = [None] * total
    words_at[0] = (words,)
    for b in bits:
        words_at[2 * b] = (hop(words, 2 * b),)
    words_at[1] = (hop(words, 1),)

    meta = None
    weights, scores = [], []

    def forward(k):
        nonlocal meta
        if k:
            extra = (meta, scores[-1])
        else:
            extra = (jnp.transpose(candidates, (2, 0, 1)), counts, natural_sharpness_exponent)
        made = forward_call(k, total, patches, words_at[k], extra)
        if not k:
            meta = made[2]
        weights.append(made[0])
        scores.append(made[1])

    forward(0)
    forward(1)
    direct = [words_at[2 * b][0] for b in bits]
    *direct, _ = barrier((*direct, scores[-1]))
    for b, x in zip(bits, direct):
        words_at[2 * b] = (x,)

    def part(g, side):
        pieces = words_at[2 * g]
        return pieces[side] if len(pieces) == 2 else half_call(side * half, pieces[0])

    for g in range(1, groups):
        if words_at[2 * g] is None:
            words_at[2 * g] = (
                hop(part(g ^ high_bit(g), 0), 2 * high_bit(g)),
                hop(part(g ^ low_bit(g), 1), 2 * low_bit(g)),
            )
    for b in bits:
        words_at[2 * b + 1] = (hop(words_at[2 * b][0], 1),)
    sequence = bits + [g for g in range(1, groups) if g not in bits]
    order = [0, 1] + [2 * g + n for g in sequence for n in (0, 1)]
    done = 2
    for g in sequence:
        if words_at[2 * g + 1] is None:
            *pieces, _ = barrier((*words_at[2 * g], scores[-2]))
            words_at[2 * g] = tuple(pieces)
            words_at[2 * g + 1] = tuple(hop(x, 1) for x in pieces)
        forward(2 * g)
        forward(2 * g + 1)
    by_offset = dict(zip(order, weights))
    weights = [by_offset[k] for k in range(total)]
    scores = scores[-1]

    pair = pair_call(per, scores, hop(scores, 1))
    tiles = [pair] + [hop(pair, 2 * g) for g in range(1, groups)]
    coef, sums = stats_call(images, per, width, meta, tiles)

    lows = [[] for _ in range(groups)]
    highs = [[] for _ in range(groups)]
    top = bits[-1] if bits else 0
    order = sorted(range(1, groups), key=lambda g: -bin(g).count("1")) + [0]
    waiting = []

    def settle(g, low, high, sibling):
        low, high = join_call(
            f"join_{g}",
            low,
            high,
            sibling,
            BF16 if g & 1 else F32,
            BF16 if g & top else F32,
        )
        lows[g].append(low)
        highs[g].append(high)
        return low

    def send(side, g, b):
        store = (lows, highs)[side]
        terms = store[g]
        value = terms[0] if len(terms) == 1 else add_call(f"mix_{side}_{g}", BF16, *terms)
        store[g ^ b].append(hop(value, 2 * b))

    word_coef = coef
    for g in order:
        low, high, theirs = word_call(
            g, total, meta, patches, word_coef, weights[2 * g], weights[2 * g + 1]
        )
        sibling = hop(theirs, 1)
        if waiting:
            joined = settle(*waiting.pop())
            word_coef, _ = barrier((word_coef, joined))
        waiting.append((g, low, high, sibling))
    settle(*waiting.pop())
    for b in bits:
        for g in sorted(range(1, groups), reverse=True):
            if low_bit(g) == b:
                send(0, g, b)
    for b in reversed(bits):
        for g in sorted(range(1, groups), reverse=True):
            if high_bit(g) == b:
                send(1, g, b)

    step = 1
    while 2 * step < rows:
        other = lax.ppermute(sums, "img", [(i, i ^ step) for i in range(rows)])
        sums = add_call(f"sums_{step}", F32, sums, other)
        step *= 2
    other = lax.ppermute(sums, "img", [(i, i ^ step) for i in range(rows)])
    loss, temp = scalar_call(sums, other)

    patch_grad = patch_call(meta, coef, weights, words_at, patches.shape)
    word_grad = finish_call(lows[0], highs[0], words.shape)
    return patch_grad, word_grad, loss, temp


def solution(mesh):
    placed = (P(("img", "cap"), None, None), P(("img", "cap"), None, None), P(), P(), P())
    return jax.shard_map(
        body,
        mesh=mesh,
        in_specs=placed,
        out_specs=(P(("img", "cap"), None, None), P(("img", "cap"), None, None), P(), P()),
        check_vma=False,
    )
```

time: 129 us -> 67.8 us (0.53); the launches traced: 128 us -> 67.8 us
  Pallas kernels: 58.1 us -> 14.2 us
  waiting for transfers between devices: 25.6 us -> 15.1 us
  local copies, waits for them, and re-layouts: 11.4 us -> 3.79 us
  starting transfers between devices: 31 us -> 33.2 us
    pallas_call x19 -> x26, Pallas kernels: 58.1 us -> 14.2 us  [the longest x8 6.22 us: forward_call(): pl.pallas_call(functools.partial(forward_kernel, offset, len(words), tota...]
    ppermute x18 -> x23, waiting for transfers between devices: 20.5 us -> 13.5 us  [hop(): return lax.ppermute(x, 'cap', [(i, i ^ offset) for i in range(total)])]
    unnamed x40 -> x12, local copies, waits for them, and re-layouts: 9 us -> 3.79 us
    ppermute x3 -> x2, waiting for transfers between devices: 5.08 us -> 1.59 us  [body(): other = lax.ppermute(sums, 'img', [(i, i ^ step) for i in range(rows)])]
    ppermute x18 -> x23, starting transfers between devices: 22.8 us -> 26.1 us  [hop(): return lax.ppermute(x, 'cap', [(i, i ^ offset) for i in range(total)])]
    slice x3 -> x0, local copies, waits for them, and re-layouts: 1.79 us -> none  [body(): tiles += [other[:ROWS], other[ROWS:]]]
    ppermute x3 -> x2, starting transfers between devices: 8.25 us -> 7.08 us  [body(): other = lax.ppermute(sums, 'img', [(i, i ^ step) for i in range(rows)])]
  transfers between devices with their start and end apart: 21 -> 25, of which waited for: 7 -> 13; matrix products, arithmetic and copies ran while one was open for 3% -> 0% of each run, Pallas kernels for 37% -> 19%
where the time goes in v2:
time: 67.8 us
  starting transfers between devices  33.2 us (49%)
  waiting for transfers between devices  15.1 us (22%)
  Pallas kernels  14.2 us (21%)
  local copies, waits for them, and re-layouts  3.79 us (6%)
  between operations  1.54 us (2%)
    ppermute x23, starting transfers between devices, hop(): return lax.ppermute(x, 'cap', [(i, i ^ offset) for i in range(total)])  26.1 us
    ppermute x23, waiting for transfers between devices, hop(): return lax.ppermute(x, 'cap', [(i, i ^ offset) for i in range(total)])  13.5 us
    ppermute x2, starting transfers between devices, body(): other = lax.ppermute(sums, 'img', [(i, i ^ step) for i in range(rows)])  7.08 us
    pallas_call x8, Pallas kernels, forward_call(): pl.pallas_call(functools.partial(forward_kernel, offset, len(words), tota...  6.22 us
    unnamed x12, local copies, waits for them, and re-layouts  3.79 us
    pallas_call x1, Pallas kernels, patch_call(): pl.pallas_call(functools.partial(patch_kernel, total, tuple((len(p) for p...  3.39 us
    pallas_call x4, Pallas kernels, word_call(): pl.pallas_call(functools.partial(word_kernel, group, total), out_shape=(p...  2.4 us
    ppermute x2, waiting for transfers between devices, body(): other = lax.ppermute(sums, 'img', [(i, i ^ step) for i in range(rows)])  1.59 us
  transfers between devices with their start and end apart: 25, of which 13 were waited for; matrix products, arithmetic and copies ran while one was open for 0% of the time, Pallas kernels for 19%

profile of v2, /device:TPU:0, one launch (start us, length us, event | category | flops | bytes accessed | tf_op | source)
XLA Modules:
  0.0 67.8 jit_solution(6507688929591410535)
XLA Ops:
  0.6 0.5 collective-permute-start
  1.1 2.6 %collective-permute-start.1 = (bf16[4,64,768]{2,1,0:T(8,128)(2,1)}, bf16[4,64,768]{2,1,0:T(8,128)(2,1)S(1)}, u32[]{:S(2)}, u32[]{:S(2)}) collective-permute-start(bf16[4,64,768]{2,1,0:T(8,128)(2,1)} %refs_8_.1), channel_id=1, source_target_pairs={{0,2},{1,3},{2,0},{3,1},{4,6},{5,7},{6,4},{7,5},{8,10},{9,11},{10,... | collective-permute-start | bytes 1179656 | tf_op jit(solution)/shard_map/ppermute | solution.py:480
  3.7 1.5 %collective-permute-start.2 = (bf16[4,64,768]{2,1,0:T(8,128)(2,1)}, bf16[4,64,768]{2,1,0:T(8,128)(2,1)S(1)}, u32[]{:S(2)}, u32[]{:S(2)}) collective-permute-start(bf16[4,64,768]{2,1,0:T(8,128)(2,1)} %refs_8_.1), channel_id=1, source_target_pairs={{0,4},{1,5},{2,6},{3,7},{4,0},{5,1},{6,2},{7,3},{8,12},{9,13},{10,... | collective-permute-start | bytes 1179656 | tf_op jit(solution)/shard_map/ppermute | solution.py:480
  5.9 1.4 %copy-done = bf16[4,256,768]{2,1,0:T(8,128)(2,1)S(1)} copy-done((bf16[4,256,768]{2,1,0:T(8,128)(2,1)S(1)}, bf16[4,256,768]{2,1,0:T(8,128)(2,1)}, u32[]{:S(2)}) %copy-start) | copy-done | bytes 1572888
  7.3 1.0 %copy-done.2 = bf16[4,64,768]{2,1,0:T(8,128)(2,1)S(1)} copy-done((bf16[4,64,768]{2,1,0:T(8,128)(2,1)S(1)}, bf16[4,64,768]{2,1,0:T(8,128)(2,1)}, u32[]{:S(2)}) %copy-start.2) | copy-done | bytes 393240
  8.3 0.7 %copy-done.4 = s32[4,8,6]{1,0,2:T(4,128)S(1)} copy-done((s32[4,8,6]{1,0,2:T(4,128)S(1)}, s32[4,8,6]{1,0,2:T(4,128)}, u32[]{:S(2)}) %copy-start.4) | copy-done | bytes 792
  9.0 0.7 %copy-done.5 = s32[4,8]{1,0:T(4,128)S(1)} copy-done((s32[4,8]{1,0:T(4,128)S(1)}, s32[4,8]{1,0:T(4,128)}, u32[]{:S(2)}) %copy-start.5) | copy-done | bytes 152
  9.7 4.1 %forward_0.1 = (bf16[4,256,256]{2,1,0:T(8,128)(2,1)S(1)}, f32[8,128]{1,0:T(8,128)S(1)}, f32[6,8,128]{2,1,0:T(8,128)S(1)}) custom-call(s32[6,4,8]{2,1,0:T(4,128)S(1)} %bitcast.1, s32[4,8]{1,0:T(4,128)S(1)} %copy-done.5, f32[1]{0:T(128)S(6)} %copy.9.refs_2_, bf16[4,256,768]{2,1,0:T(8,128)(2,1)S(1)} %copy-done, bf16[4,64,768]{2,1,0:T(8,128)(2,1)S(1)} %copy-done.2), custom_call_target="tpu_custom_call" | custom-call | flops 1 | bytes 1 | tf_op jit(solution)/shard_map/forward_0/pallas_call | solution.py:172
  13.8 0.9 %forward_1.1 = (bf16[4,256,256]{2,1,0:T(8,128)(2,1)S(1)}, f32[8,128]{1,0:T(8,128)S(1)}) custom-call(f32[6,8,128]{2,1,0:T(8,128)S(1)} %get-tuple-element.51.refs_0_.meta, bf16[4,256,768]{2,1,0:T(8,128)(2,1)S(1)} %copy-done.1, f32[8,128]{1,0:T(8,128)S(1)} %get-tuple-element.52.refs_2_, bf16[4,64,768]{2,1,0:T(8,128)(2,1)S(1)} %collective-permute-done.refs_3_.refs_9_), custom_call_target="tpu_custom_call" | custom-call | flops 1 | bytes 1 | tf_op jit(solution)/shard_map/forward_1/pallas_call | solution.py:172
  14.8 0.3 collective-permute-done.2.refs_3_.x.refs_12_
  15.1 2.1 %collective-permute-start.3 = (bf16[4,64,768]{2,1,0:T(8,128)(2,1)S(1)}, bf16[4,64,768]{2,1,0:T(8,128)(2,1)S(1)}, u32[]{:S(2)}, u32[]{:S(2)}) collective-permute-start(bf16[4,64,768]{2,1,0:T(8,128)(2,1)S(1)} %collective-permute-done.1.refs_3_.x.refs_10_), channel_id=1, source_target_pairs={{0,1},{1,0},{2,3},{3,2},{4,5},{5,4},{6,7},{7,6},{8,9},{9,8},{10,11... | collective-permute-start | bytes 1179656 | tf_op jit(solution)/shard_map/ppermute | solution.py:480
  17.3 0.7 %collective-permute-start.5 = (bf16[2,64,768]{2,1,0:T(8,128)(2,1)S(1)}, bf16[2,64,768]{2,1,0:T(8,128)(2,1)S(1)}, u32[]{:S(2)}, u32[]{:S(2)}) collective-permute-start(bf16[2,64,768]{2,1,0:T(8,128)(2,1)S(1)} %half_0.1), channel_id=1, source_target_pairs={{0,4},{1,5},{2,6},{3,7},{4,0},{5,1},{6,2},{7,3},{8,12},{9,13},{10,... | collective-permute-start | bytes 589832 | tf_op jit(solution)/shard_map/ppermute | solution.py:480
  18.0 0.2 collective-permute-start.4
  18.3 0.3 collective-permute-done.3.refs_3_.refs_11_
  18.5 0.9 %forward_3.1 = (bf16[4,256,256]{2,1,0:T(8,128)(2,1)S(1)}, f32[8,128]{1,0:T(8,128)S(1)}) custom-call(f32[6,8,128]{2,1,0:T(8,128)S(1)} %get-tuple-element.51.refs_0_.meta, bf16[4,256,768]{2,1,0:T(8,128)(2,1)S(1)} %copy-done.1, f32[8,128]{1,0:T(8,128)S(1)} %get-tuple-element.55.refs_2_, bf16[4,64,768]{2,1,0:T(8,128)(2,1)S(1)} %collective-permute-done.3.refs_3_.refs_11_), custom_call_target="tpu_custom_call" | custom-call | flops 1 | bytes 1 | tf_op jit(solution)/shard_map/forward_3/pallas_call | solution.py:172
  19.5 4.6 %collective-permute-done.6.refs_4_.refs_15_ = bf16[2,64,768]{2,1,0:T(8,128)(2,1)S(1)} collective-permute-done((bf16[2,64,768]{2,1,0:T(8,128)(2,1)S(1)}, bf16[2,64,768]{2,1,0:T(8,128)(2,1)S(1)}, u32[]{:S(2)}, u32[]{:S(2)}) %collective-permute-start.6) | collective-permute-done | bytes 196640 | tf_op jit(solution)/shard_map/ppermute | solution.py:480
  24.1 0.1 collective-permute-done.5.refs_3_.refs_14_
  24.2 0.5 collective-permute-start.8
  24.8 0.8 %collective-permute-done.7.refs_3_.refs_16_ = bf16[2,64,768]{2,1,0:T(8,128)(2,1)S(1)} collective-permute-done((bf16[2,64,768]{2,1,0:T(8,128)(2,1)S(1)}, bf16[2,64,768]{2,1,0:T(8,128)(2,1)S(1)}, u32[]{:S(2)}, u32[]{:S(2)}) %collective-permute-start.7) | collective-permute-done | bytes 196640 | tf_op jit(solution)/shard_map/ppermute | solution.py:480
  25.6 0.3 collective-permute-done.8.refs_4_.refs_17_
  26.0 2.3 %collective-permute-start.9 = (f32[8,128]{1,0:T(8,128)S(1)}, f32[8,128]{1,0:T(8,128)S(1)}, u32[]{:S(2)}, u32[]{:S(2)}) collective-permute-start(f32[8,128]{1,0:T(8,128)S(1)} %get-tuple-element.63.own), channel_id=1, source_target_pairs={{0,1},{1,0},{2,3},{3,2},{4,5},{5,4},{6,7},{7,6},{8,9},{9,8},{10,11... | collective-permute-start | bytes 12296 | tf_op jit(solution)/shard_map/ppermute | solution.py:480
  28.3 0.8 %collective-permute-done.9.other = f32[8,128]{1,0:T(8,128)S(1)} collective-permute-done((f32[8,128]{1,0:T(8,128)S(1)}, f32[8,128]{1,0:T(8,128)S(1)}, u32[]{:S(2)}, u32[]{:S(2)}) %collective-permute-start.9) | collective-permute-done | bytes 4128 | tf_op jit(solution)/shard_map/ppermute | solution.py:480
  29.1 1.3 %collective-permute-start.12 = (f32[8,128]{1,0:T(8,128)S(1)}, f32[8,128]{1,0:T(8,128)S(1)}, u32[]{:S(2)}, u32[]{:S(2)}) collective-permute-start(f32[8,128]{1,0:T(8,128)S(1)} %pair.1.refs_0_), channel_id=1, source_target_pairs={{0,6},{1,7},{2,4},{3,5},{4,2},{5,3},{6,0},{7,1},{8,14},{9,15},{10,... | collective-permute-start | bytes 12296 | tf_op jit(solution)/shard_map/ppermute | solution.py:480
  30.4 3.6 %collective-permute-start.11 = (f32[8,128]{1,0:T(8,128)S(1)}, f32[8,128]{1,0:T(8,128)S(1)}, u32[]{:S(2)}, u32[]{:S(2)}) collective-permute-start(f32[8,128]{1,0:T(8,128)S(1)} %pair.1.refs_0_), channel_id=1, source_target_pairs={{0,4},{1,5},{2,6},{3,7},{4,0},{5,1},{6,2},{7,3},{8,12},{9,13},{10,... | collective-permute-start | bytes 12296 | tf_op jit(solution)/shard_map/ppermute | solution.py:480
  34.0 1.4 %collective-permute-start.10 = (f32[8,128]{1,0:T(8,128)S(1)}, f32[8,128]{1,0:T(8,128)S(1)}, u32[]{:S(2)}, u32[]{:S(2)}) collective-permute-start(f32[8,128]{1,0:T(8,128)S(1)} %pair.1.refs_0_), channel_id=1, source_target_pairs={{0,2},{1,3},{2,0},{3,1},{4,6},{5,7},{6,4},{7,5},{8,10},{9,11},{10,... | collective-permute-start | bytes 12296 | tf_op jit(solution)/shard_map/ppermute | solution.py:480
  35.4 0.2 collective-permute-done.11.refs_2_
  35.6 2.0 %collective-permute-done.10.refs_1_ = f32[8,128]{1,0:T(8,128)S(1)} collective-permute-done((f32[8,128]{1,0:T(8,128)S(1)}, f32[8,128]{1,0:T(8,128)S(1)}, u32[]{:S(2)}, u32[]{:S(2)}) %collective-permute-start.10) | collective-permute-done | bytes 4128 | tf_op jit(solution)/shard_map/ppermute | solution.py:480
  37.6 0.3 stats.1
  37.9 0.2 word_3.1
  38.2 0.9 %word_1.1 = (f32[2,64,768]{2,1,0:T(8,128)S(1)}, f32[2,64,768]{2,1,0:T(8,128)S(1)}, bf16[4,64,768]{2,1,0:T(8,128)(2,1)S(1)}) custom-call(f32[6,8,128]{2,1,0:T(8,128)S(1)} %get-tuple-element.51.refs_0_.meta, bf16[4,256,768]{2,1,0:T(8,128)(2,1)S(1)} %copy-done.1, f32[8,4,8,128]{3,2,1,0:T(8,128)S(1)} %get-tuple-element.82.coef, ...), custom_call_target="tpu_custom_call" | custom-call | flops 1 | bytes 1 | tf_op jit(solution)/shard_map/word_1/pallas_call | solution.py:313
  39.2 0.7 %collective-permute-done.13.sibling = bf16[4,64,768]{2,1,0:T(8,128)(2,1)S(1)} collective-permute-done((bf16[4,64,768]{2,1,0:T(8,128)(2,1)S(1)}, bf16[4,64,768]{2,1,0:T(8,128)(2,1)S(1)}, u32[]{:S(2)}, u32[]{:S(2)}) %collective-permute-start.13) | collective-permute-done | bytes 393248 | tf_op jit(solution)/shard_map/ppermute | solution.py:480
  40.0 0.2 word_2.1
  40.1 0.8 %collective-permute-start.17 = (bf16[4,64,768]{2,1,0:T(8,128)(2,1)S(1)}, bf16[4,64,768]{2,1,0:T(8,128)(2,1)S(1)}, u32[]{:S(2)}, u32[]{:S(2)}) collective-permute-start(bf16[4,64,768]{2,1,0:T(8,128)(2,1)S(1)} %get-tuple-element.89), channel_id=1, source_target_pairs={{0,1},{1,0},{2,3},{3,2},{4,5},{5,4},{6,7},{7,6},{8,9},{9,8},{10,11... | collective-permute-start | bytes 1179656 | tf_op jit(solution)/shard_map/ppermute | solution.py:480
  40.9 1.9 %collective-permute-start.21 = (bf16[2,64,768]{2,1,0:T(8,128)(2,1)S(1)}, bf16[2,64,768]{2,1,0:T(8,128)(2,1)S(1)}, u32[]{:S(2)}, u32[]{:S(2)}) collective-permute-start(bf16[2,64,768]{2,1,0:T(8,128)(2,1)S(1)} %get-tuple-element.94), channel_id=1, source_target_pairs={{0,4},{1,5},{2,6},{3,7},{4,0},{5,1},{6,2},{7,3},{8,12},{9,13},{10,... | collective-permute-start | bytes 589832 | tf_op jit(solution)/shard_map/ppermute | solution.py:480
  42.9 1.2 %word_0.1 = (f32[2,64,768]{2,1,0:T(8,128)S(1)}, f32[2,64,768]{2,1,0:T(8,128)S(1)}, bf16[4,64,768]{2,1,0:T(8,128)(2,1)S(1)}) custom-call(f32[6,8,128]{2,1,0:T(8,128)S(1)} %get-tuple-element.51.refs_0_.meta, bf16[4,256,768]{2,1,0:T(8,128)(2,1)S(1)} %copy-done.1, f32[8,4,8,128]{3,2,1,0:T(8,128)S(1)} %get-tuple-element.82.coef, ...), custom_call_target="tpu_custom_call" | custom-call | flops 1 | bytes 1 | tf_op jit(solution)/shard_map/word_0/pallas_call | solution.py:313
  44.1 0.2 collective-permute-start.15
  44.3 2.1 %collective-permute-start.18 = (bf16[2,64,768]{2,1,0:T(8,128)(2,1)S(1)}, bf16[2,64,768]{2,1,0:T(8,128)(2,1)S(1)}, u32[]{:S(2)}, u32[]{:S(2)}) collective-permute-start(bf16[2,64,768]{2,1,0:T(8,128)(2,1)S(1)} %get-tuple-element.76), channel_id=1, source_target_pairs={{0,2},{1,3},{2,0},{3,1},{4,6},{5,7},{6,4},{7,5},{8,10},{9,11},{10,... | collective-permute-start | bytes 589832 | tf_op jit(solution)/shard_map/ppermute | solution.py:480
  46.4 2.7 %collective-permute-start.23 = (f32[8,128]{1,0:T(8,128)S(1)}, f32[8,128]{1,0:T(8,128)S(1)}, u32[]{:S(2)}, u32[]{:S(2)}) collective-permute-start(f32[8,128]{1,0:T(8,128)S(1)} %get-tuple-element.95.refs_0_), channel_id=1, source_target_pairs={{0,8},{8,0},{16,24},{24,16},{1,9},{9,1},{17,25},{25,17},{2,10},{10... | collective-permute-start | bytes 12296 | tf_op jit(solution)/shard_map/ppermute | solution.py:587
  49.2 1.6 %collective-permute-done.23.refs_1_ = f32[8,128]{1,0:T(8,128)S(1)} collective-permute-done((f32[8,128]{1,0:T(8,128)S(1)}, f32[8,128]{1,0:T(8,128)S(1)}, u32[]{:S(2)}, u32[]{:S(2)}) %collective-permute-start.23) | collective-permute-done | bytes 4128 | tf_op jit(solution)/shard_map/ppermute | solution.py:587
  50.7 4.4 %collective-permute-start.24 = (f32[8,128]{1,0:T(8,128)S(1)}, f32[8,128]{1,0:T(8,128)S(1)}, u32[]{:S(2)}, u32[]{:S(2)}) collective-permute-start(f32[8,128]{1,0:T(8,128)S(1)} %sums_1.1.mine), channel_id=1, source_target_pairs={{0,16},{8,24},{16,0},{24,8},{1,17},{9,25},{17,1},{25,9},{2,18},{10... | collective-permute-start | bytes 12296 | tf_op jit(solution)/shard_map/ppermute | solution.py:590
  55.1 0.3 collective-permute-start.16
  55.5 1.7 %collective-permute-start.22 = (bf16[2,64,768]{2,1,0:T(8,128)(2,1)S(1)}, bf16[2,64,768]{2,1,0:T(8,128)(2,1)S(1)}, u32[]{:S(2)}, u32[]{:S(2)}) collective-permute-start(bf16[2,64,768]{2,1,0:T(8,128)(2,1)S(1)} %mix_1_1.1), channel_id=1, source_target_pairs={{0,2},{1,3},{2,0},{3,1},{4,6},{5,7},{6,4},{7,5},{8,10},{9,11},{10,... | collective-permute-start | bytes 589832 | tf_op jit(solution)/shard_map/ppermute | solution.py:480
  57.5 2.0 %collective-permute-start.20 = (bf16[2,64,768]{2,1,0:T(8,128)(2,1)S(1)}, bf16[2,64,768]{2,1,0:T(8,128)(2,1)S(1)}, u32[]{:S(2)}, u32[]{:S(2)}) collective-permute-start(bf16[2,64,768]{2,1,0:T(8,128)(2,1)S(1)} %get-tuple-element.92), channel_id=1, source_target_pairs={{0,4},{1,5},{2,6},{3,7},{4,0},{5,1},{6,2},{7,3},{8,12},{9,13},{10,... | collective-permute-start | bytes 589832 | tf_op jit(solution)/shard_map/ppermute | solution.py:480
  59.5 3.4 %patch.1 = bf16[4,256,768]{2,1,0:T(8,128)(2,1)} custom-call(f32[6,8,128]{2,1,0:T(8,128)S(1)} %get-tuple-element.51.refs_0_.meta, f32[8,4,8,128]{3,2,1,0:T(8,128)S(1)} %get-tuple-element.82.coef, bf16[4,256,256]{2,1,0:T(8,128)(2,1)S(1)} %get-tuple-element.65.refs_0_.weights_a, bf16[4,256,256]{2,1,0:T(8,128)(2,1)S(1)} %get-tuple-element.66.refs_1_.weights_b, ...), custom_call_target="tpu_custom_call" | custom-call | flops 1 | bytes 1 | tf_op jit(solution)/shard_map/patch/pallas_call | solution.py:356
  62.9 0.6 scalars.1
  63.5 1.6 %collective-permute-done.22.refs_5_ = bf16[2,64,768]{2,1,0:T(8,128)(2,1)S(1)} collective-permute-done((bf16[2,64,768]{2,1,0:T(8,128)(2,1)S(1)}, bf16[2,64,768]{2,1,0:T(8,128)(2,1)S(1)}, u32[]{:S(2)}, u32[]{:S(2)}) %collective-permute-start.22) | collective-permute-done | bytes 196640 | tf_op jit(solution)/shard_map/ppermute | solution.py:480
  65.2 1.8 %collective-permute-done.20.refs_4_ = bf16[2,64,768]{2,1,0:T(8,128)(2,1)S(1)} collective-permute-done((bf16[2,64,768]{2,1,0:T(8,128)(2,1)S(1)}, bf16[2,64,768]{2,1,0:T(8,128)(2,1)S(1)}, u32[]{:S(2)}, u32[]{:S(2)}) %collective-permute-start.20) | collective-permute-done | bytes 196640 | tf_op jit(solution)/shard_map/ppermute | solution.py:480
  66.9 0.9 %finish.1 = bf16[4,64,768]{2,1,0:T(8,128)(2,1)} custom-call(f32[2,64,768]{2,1,0:T(8,128)S(1)} %get-tuple-element.86.refs_0_, bf16[2,64,768]{2,1,0:T(8,128)(2,1)S(1)} %collective-permute-done.16.refs_1_, bf16[2,64,768]{2,1,0:T(8,128)(2,1)S(1)} %collective-permute-done.19.refs_2_, f32[2,64,768]{2,1,0:T(8,128)S(1)} %get-tuple-element.91.refs_3_, ...), custom_call_target="tpu_custom_call" | custom-call | flops 1 | bytes 1 | tf_op jit(solution)/shard_map/finish/pallas_call | solution.py:433
  (40 shorter events, 1.0 us)
Async XLA Ops:
  0.6 13.2 %collective-permute-start = (bf16[4,64,768]{2,1,0:T(8,128)(2,1)}, bf16[4,64,768]{2,1,0:T(8,128)(2,1)S(1)}, u32[]{:S(2)}, u32[]{:S(2)}) collective-permute-start(bf16[4,64,768]{2,1,0:T(8,128)(2,1)} %refs_8_.1), channel_id=1, source_target_pairs={{0,1},{1,0},{2,3},{3,2},{4,5},{5,4},{6,7},{7,6},{8,9},{9,8},{10,11... | collective-permute-start | bytes 1179656 | tf_op jit(solution)/shard_map/ppermute | solution.py:480
  1.1 13.6 %collective-permute-start.1 = (bf16[4,64,768]{2,1,0:T(8,128)(2,1)}, bf16[4,64,768]{2,1,0:T(8,128)(2,1)S(1)}, u32[]{:S(2)}, u32[]{:S(2)}) collective-permute-start(bf16[4,64,768]{2,1,0:T(8,128)(2,1)} %refs_8_.1), channel_id=1, source_target_pairs={{0,2},{1,3},{2,0},{3,1},{4,6},{5,7},{6,4},{7,5},{8,10},{9,11},{10,... | collective-permute-start | bytes 1179656 | tf_op jit(solution)/shard_map/ppermute | solution.py:480
  3.7 11.4 %collective-permute-start.2 = (bf16[4,64,768]{2,1,0:T(8,128)(2,1)}, bf16[4,64,768]{2,1,0:T(8,128)(2,1)S(1)}, u32[]{:S(2)}, u32[]{:S(2)}) collective-permute-start(bf16[4,64,768]{2,1,0:T(8,128)(2,1)} %refs_8_.1), channel_id=1, source_target_pairs={{0,4},{1,5},{2,6},{3,7},{4,0},{5,1},{6,2},{7,3},{8,12},{9,13},{10,... | collective-permute-start | bytes 1179656 | tf_op jit(solution)/shard_map/ppermute | solution.py:480
  5.9 1.4 %copy-start = (bf16[4,256,768]{2,1,0:T(8,128)(2,1)S(1)}, bf16[4,256,768]{2,1,0:T(8,128)(2,1)}, u32[]{:S(2)}) copy-start(bf16[4,256,768]{2,1,0:T(8,128)(2,1)} %patches.7) | copy-start | bytes 4718596
  7.3 1.0 %copy-start.2 = (bf16[4,64,768]{2,1,0:T(8,128)(2,1)S(1)}, bf16[4,64,768]{2,1,0:T(8,128)(2,1)}, u32[]{:S(2)}) copy-start(bf16[4,64,768]{2,1,0:T(8,128)(2,1)} %refs_8_.1) | copy-start | bytes 1179652
  8.3 0.7 %copy-start.4 = (s32[4,8,6]{1,0,2:T(4,128)S(1)}, s32[4,8,6]{1,0,2:T(4,128)}, u32[]{:S(2)}) copy-start(s32[4,8,6]{1,0,2:T(4,128)} %param.8) | copy-start | bytes 2308
  9.0 0.7 %copy-start.5 = (s32[4,8]{1,0:T(4,128)S(1)}, s32[4,8]{1,0:T(4,128)}, u32[]{:S(2)}) copy-start(s32[4,8]{1,0:T(4,128)} %refs_1_.8) | copy-start | bytes 388
  9.7 4.1 %copy-start.1 = (bf16[4,256,768]{2,1,0:T(8,128)(2,1)S(1)}, bf16[4,256,768]{2,1,0:T(8,128)(2,1)}, u32[]{:S(2)}) copy-start(bf16[4,256,768]{2,1,0:T(8,128)(2,1)} %patches.7) | copy-start | bytes 4718596
  15.1 3.4 %collective-permute-start.3 = (bf16[4,64,768]{2,1,0:T(8,128)(2,1)S(1)}, bf16[4,64,768]{2,1,0:T(8,128)(2,1)S(1)}, u32[]{:S(2)}, u32[]{:S(2)}) collective-permute-start(bf16[4,64,768]{2,1,0:T(8,128)(2,1)S(1)} %collective-permute-done.1.refs_3_.x.refs_10_), channel_id=1, source_target_pairs={{0,1},{1,0},{2,3},{3,2},{4,5},{5,4},{6,7},{7,6},{8,9},{9,8},{10,11... | collective-permute-start | bytes 1179656 | tf_op jit(solution)/shard_map/ppermute | solution.py:480
  17.2 6.9 %collective-permute-start.6 = (bf16[2,64,768]{2,1,0:T(8,128)(2,1)S(1)}, bf16[2,64,768]{2,1,0:T(8,128)(2,1)S(1)}, u32[]{:S(2)}, u32[]{:S(2)}) collective-permute-start(bf16[2,64,768]{2,1,0:T(8,128)(2,1)S(1)} %half_2.1), channel_id=1, source_target_pairs={{0,2},{1,3},{2,0},{3,1},{4,6},{5,7},{6,4},{7,5},{8,10},{9,11},{10,... | collective-permute-start | bytes 589832 | tf_op jit(solution)/shard_map/ppermute | solution.py:480
  17.3 6.9 %collective-permute-start.5 = (bf16[2,64,768]{2,1,0:T(8,128)(2,1)S(1)}, bf16[2,64,768]{2,1,0:T(8,128)(2,1)S(1)}, u32[]{:S(2)}, u32[]{:S(2)}) collective-permute-start(bf16[2,64,768]{2,1,0:T(8,128)(2,1)S(1)} %half_0.1), channel_id=1, source_target_pairs={{0,4},{1,5},{2,6},{3,7},{4,0},{5,1},{6,2},{7,3},{8,12},{9,13},{10,... | collective-permute-start | bytes 589832 | tf_op jit(solution)/shard_map/ppermute | solution.py:480
  18.0 6.7 %collective-permute-start.4 = (bf16[4,64,768]{2,1,0:T(8,128)(2,1)S(1)}, bf16[4,64,768]{2,1,0:T(8,128)(2,1)S(1)}, u32[]{:S(2)}, u32[]{:S(2)}) collective-permute-start(bf16[4,64,768]{2,1,0:T(8,128)(2,1)S(1)} %collective-permute-done.2.refs_3_.x.refs_12_), channel_id=1, source_target_pairs={{0,1},{1,0},{2,3},{3,2},{4,5},{5,4},{6,7},{7,6},{8,9},{9,8},{10,11... | collective-permute-start | bytes 1179656 | tf_op jit(solution)/shard_map/ppermute | solution.py:480
  24.2 1.4 %collective-permute-start.7 = (bf16[2,64,768]{2,1,0:T(8,128)(2,1)S(1)}, bf16[2,64,768]{2,1,0:T(8,128)(2,1)S(1)}, u32[]{:S(2)}, u32[]{:S(2)}) collective-permute-start(bf16[2,64,768]{2,1,0:T(8,128)(2,1)S(1)} %collective-permute-done.5.refs_3_.refs_14_), channel_id=1, source_target_pairs={{0,1},{1,0},{2,3},{3,2},{4,5},{5,4},{6,7},{7,6},{8,9},{9,8},{10,11... | collective-permute-start | bytes 589832 | tf_op jit(solution)/shard_map/ppermute | solution.py:480
  24.2 1.7 %collective-permute-start.8 = (bf16[2,64,768]{2,1,0:T(8,128)(2,1)S(1)}, bf16[2,64,768]{2,1,0:T(8,128)(2,1)S(1)}, u32[]{:S(2)}, u32[]{:S(2)}) collective-permute-start(bf16[2,64,768]{2,1,0:T(8,128)(2,1)S(1)} %collective-permute-done.6.refs_4_.refs_15_), channel_id=1, source_target_pairs={{0,1},{1,0},{2,3},{3,2},{4,5},{5,4},{6,7},{7,6},{8,9},{9,8},{10,11... | collective-permute-start | bytes 589832 | tf_op jit(solution)/shard_map/ppermute | solution.py:480
  26.0 3.2 %collective-permute-start.9 = (f32[8,128]{1,0:T(8,128)S(1)}, f32[8,128]{1,0:T(8,128)S(1)}, u32[]{:S(2)}, u32[]{:S(2)}) collective-permute-start(f32[8,128]{1,0:T(8,128)S(1)} %get-tuple-element.63.own), channel_id=1, source_target_pairs={{0,1},{1,0},{2,3},{3,2},{4,5},{5,4},{6,7},{7,6},{8,9},{9,8},{10,11... | collective-permute-start | bytes 12296 | tf_op jit(solution)/shard_map/ppermute | solution.py:480
  29.1 6.3 %collective-permute-start.12 = (f32[8,128]{1,0:T(8,128)S(1)}, f32[8,128]{1,0:T(8,128)S(1)}, u32[]{:S(2)}, u32[]{:S(2)}) collective-permute-start(f32[8,128]{1,0:T(8,128)S(1)} %pair.1.refs_0_), channel_id=1, source_target_pairs={{0,6},{1,7},{2,4},{3,5},{4,2},{5,3},{6,0},{7,1},{8,14},{9,15},{10,... | collective-permute-start | bytes 12296 | tf_op jit(solution)/shard_map/ppermute | solution.py:480
  30.4 5.2 %collective-permute-start.11 = (f32[8,128]{1,0:T(8,128)S(1)}, f32[8,128]{1,0:T(8,128)S(1)}, u32[]{:S(2)}, u32[]{:S(2)}) collective-permute-start(f32[8,128]{1,0:T(8,128)S(1)} %pair.1.refs_0_), channel_id=1, source_target_pairs={{0,4},{1,5},{2,6},{3,7},{4,0},{5,1},{6,2},{7,3},{8,12},{9,13},{10,... | collective-permute-start | bytes 12296 | tf_op jit(solution)/shard_map/ppermute | solution.py:480
  34.0 3.6 %collective-permute-start.10 = (f32[8,128]{1,0:T(8,128)S(1)}, f32[8,128]{1,0:T(8,128)S(1)}, u32[]{:S(2)}, u32[]{:S(2)}) collective-permute-start(f32[8,128]{1,0:T(8,128)S(1)} %pair.1.refs_0_), channel_id=1, source_target_pairs={{0,2},{1,3},{2,0},{3,1},{4,6},{5,7},{6,4},{7,5},{8,10},{9,11},{10,... | collective-permute-start | bytes 12296 | tf_op jit(solution)/shard_map/ppermute | solution.py:480
  38.1 1.8 %collective-permute-start.13 = (bf16[4,64,768]{2,1,0:T(8,128)(2,1)S(1)}, bf16[4,64,768]{2,1,0:T(8,128)(2,1)S(1)}, u32[]{:S(2)}, u32[]{:S(2)}) collective-permute-start(bf16[4,64,768]{2,1,0:T(8,128)(2,1)S(1)} %get-tuple-element.75), channel_id=1, source_target_pairs={{0,1},{1,0},{2,3},{3,2},{4,5},{5,4},{6,7},{7,6},{8,9},{9,8},{10,11... | collective-permute-start | bytes 1179656 | tf_op jit(solution)/shard_map/ppermute | solution.py:480
  39.1 3.7 %collective-permute-start.14 = (bf16[4,64,768]{2,1,0:T(8,128)(2,1)S(1)}, bf16[4,64,768]{2,1,0:T(8,128)(2,1)S(1)}, u32[]{:S(2)}, u32[]{:S(2)}) collective-permute-start(bf16[4,64,768]{2,1,0:T(8,128)(2,1)S(1)} %get-tuple-element.80), channel_id=1, source_target_pairs={{0,1},{1,0},{2,3},{3,2},{4,5},{5,4},{6,7},{7,6},{8,9},{9,8},{10,11... | collective-permute-start | bytes 1179656 | tf_op jit(solution)/shard_map/ppermute | solution.py:480
  40.1 15.4 %collective-permute-start.17 = (bf16[4,64,768]{2,1,0:T(8,128)(2,1)S(1)}, bf16[4,64,768]{2,1,0:T(8,128)(2,1)S(1)}, u32[]{:S(2)}, u32[]{:S(2)}) collective-permute-start(bf16[4,64,768]{2,1,0:T(8,128)(2,1)S(1)} %get-tuple-element.89), channel_id=1, source_target_pairs={{0,1},{1,0},{2,3},{3,2},{4,5},{5,4},{6,7},{7,6},{8,9},{9,8},{10,11... | collective-permute-start | bytes 1179656 | tf_op jit(solution)/shard_map/ppermute | solution.py:480
  40.9 14.2 %collective-permute-start.21 = (bf16[2,64,768]{2,1,0:T(8,128)(2,1)S(1)}, bf16[2,64,768]{2,1,0:T(8,128)(2,1)S(1)}, u32[]{:S(2)}, u32[]{:S(2)}) collective-permute-start(bf16[2,64,768]{2,1,0:T(8,128)(2,1)S(1)} %get-tuple-element.94), channel_id=1, source_target_pairs={{0,4},{1,5},{2,6},{3,7},{4,0},{5,1},{6,2},{7,3},{8,12},{9,13},{10,... | collective-permute-start | bytes 589832 | tf_op jit(solution)/shard_map/ppermute | solution.py:480
  44.1 15.4 %copy-start.3 = (bf16[4,64,768]{2,1,0:T(8,128)(2,1)S(1)}, bf16[4,64,768]{2,1,0:T(8,128)(2,1)}, u32[]{:S(2)}) copy-start(bf16[4,64,768]{2,1,0:T(8,128)(2,1)} %refs_8_.1) | copy-start | bytes 1179652
  44.1 19.4 %collective-permute-start.15 = (bf16[4,64,768]{2,1,0:T(8,128)(2,1)S(1)}, bf16[4,64,768]{2,1,0:T(8,128)(2,1)S(1)}, u32[]{:S(2)}, u32[]{:S(2)}) collective-permute-start(bf16[4,64,768]{2,1,0:T(8,128)(2,1)S(1)} %get-tuple-element.85), channel_id=1, source_target_pairs={{0,1},{1,0},{2,3},{3,2},{4,5},{5,4},{6,7},{7,6},{8,9},{9,8},{10,11... | collective-permute-start | bytes 1179656 | tf_op jit(solution)/shard_map/ppermute | solution.py:480
  44.3 13.0 %collective-permute-start.18 = (bf16[2,64,768]{2,1,0:T(8,128)(2,1)S(1)}, bf16[2,64,768]{2,1,0:T(8,128)(2,1)S(1)}, u32[]{:S(2)}, u32[]{:S(2)}) collective-permute-start(bf16[2,64,768]{2,1,0:T(8,128)(2,1)S(1)} %get-tuple-element.76), channel_id=1, source_target_pairs={{0,2},{1,3},{2,0},{3,1},{4,6},{5,7},{6,4},{7,5},{8,10},{9,11},{10,... | collective-permute-start | bytes 589832 | tf_op jit(solution)/shard_map/ppermute | solution.py:480
  46.4 4.3 %collective-permute-start.23 = (f32[8,128]{1,0:T(8,128)S(1)}, f32[8,128]{1,0:T(8,128)S(1)}, u32[]{:S(2)}, u32[]{:S(2)}) collective-permute-start(f32[8,128]{1,0:T(8,128)S(1)} %get-tuple-element.95.refs_0_), channel_id=1, source_target_pairs={{0,8},{8,0},{16,24},{24,16},{1,9},{9,1},{17,25},{25,17},{2,10},{10... | collective-permute-start | bytes 12296 | tf_op jit(solution)/shard_map/ppermute | solution.py:587
  50.7 6.7 %collective-permute-start.24 = (f32[8,128]{1,0:T(8,128)S(1)}, f32[8,128]{1,0:T(8,128)S(1)}, u32[]{:S(2)}, u32[]{:S(2)}) collective-permute-start(f32[8,128]{1,0:T(8,128)S(1)} %sums_1.1.mine), channel_id=1, source_target_pairs={{0,16},{8,24},{16,0},{24,8},{1,17},{9,25},{17,1},{25,9},{2,18},{10... | collective-permute-start | bytes 12296 | tf_op jit(solution)/shard_map/ppermute | solution.py:590
  55.1 8.4 %collective-permute-start.16 = (bf16[2,64,768]{2,1,0:T(8,128)(2,1)S(1)}, bf16[2,64,768]{2,1,0:T(8,128)(2,1)S(1)}, u32[]{:S(2)}, u32[]{:S(2)}) collective-permute-start(bf16[2,64,768]{2,1,0:T(8,128)(2,1)S(1)} %get-tuple-element.81), channel_id=1, source_target_pairs={{0,2},{1,3},{2,0},{3,1},{4,6},{5,7},{6,4},{7,5},{8,10},{9,11},{10,... | collective-permute-start | bytes 589832 | tf_op jit(solution)/shard_map/ppermute | solution.py:480
  55.5 9.7 %collective-permute-start.22 = (bf16[2,64,768]{2,1,0:T(8,128)(2,1)S(1)}, bf16[2,64,768]{2,1,0:T(8,128)(2,1)S(1)}, u32[]{:S(2)}, u32[]{:S(2)}) collective-permute-start(bf16[2,64,768]{2,1,0:T(8,128)(2,1)S(1)} %mix_1_1.1), channel_id=1, source_target_pairs={{0,2},{1,3},{2,0},{3,1},{4,6},{5,7},{6,4},{7,5},{8,10},{9,11},{10,... | collective-permute-start | bytes 589832 | tf_op jit(solution)/shard_map/ppermute | solution.py:480
  57.4 7.8 %collective-permute-start.19 = (bf16[2,64,768]{2,1,0:T(8,128)(2,1)S(1)}, bf16[2,64,768]{2,1,0:T(8,128)(2,1)S(1)}, u32[]{:S(2)}, u32[]{:S(2)}) collective-permute-start(bf16[2,64,768]{2,1,0:T(8,128)(2,1)S(1)} %mix_0_2.1), channel_id=1, source_target_pairs={{0,4},{1,5},{2,6},{3,7},{4,0},{5,1},{6,2},{7,3},{8,12},{9,13},{10,... | collective-permute-start | bytes 589832 | tf_op jit(solution)/shard_map/ppermute | solution.py:480
  57.5 9.5 %collective-permute-start.20 = (bf16[2,64,768]{2,1,0:T(8,128)(2,1)S(1)}, bf16[2,64,768]{2,1,0:T(8,128)(2,1)S(1)}, u32[]{:S(2)}, u32[]{:S(2)}) collective-permute-start(bf16[2,64,768]{2,1,0:T(8,128)(2,1)S(1)} %get-tuple-element.92), channel_id=1, source_target_pairs={{0,4},{1,5},{2,6},{3,7},{4,0},{5,1},{6,2},{7,3},{8,12},{9,13},{10,... | collective-permute-start | bytes 589832 | tf_op jit(solution)/shard_map/ppermute | solution.py:480

commit v3 on v2

--- a/solution.py
+++ b/solution.py
@@ -66,12 +66,13 @@
     return meta[total // 2 + offset // ROWS, offset % ROWS, 0] > 0.0
 
 
-def forward_kernel(offset, pieces, total, *refs):
+def forward_kernel(offset, pieces, total, product, *refs):
     if offset:
         meta, patches, prior, *words = refs[: 3 + pieces]
     else:
         cands, counts, nse, patches, *words = refs[: 4 + pieces]
-    weights_out, scores_out = refs[-4 - (not offset) :][:2]
+    outs = list(refs[(3 if offset else 4) + pieces : -2])
+    weights_out, scores_out = outs[:2]
     low, high = refs[-2:]
     me = lax.axis_index("cap")
     column = me ^ offset
@@ -85,7 +86,7 @@
 
     start()
     if not offset:
-        fill_meta(cands, counts, nse, per, total, refs[-3])
+        fill_meta(cands, counts, nse, per, total, outs[-1])
 
     def score():
         sub = lax.broadcasted_iota(jnp.int32, (ROWS, LANES), 0)
@@ -151,16 +152,30 @@
 
             lax.fori_loop(0, per, image, 0)
 
+        if product:
+            for i in range(per):
+                outs[2][i] = lax.dot_general(
+                    weights_out[i], patches[i], NN, preferred_element_type=F32
+                )
+
     if offset:
-        pl.when(block_is_live(meta, total, offset))(score)
+        live = block_is_live(meta, total, offset)
+        pl.when(live)(score)
+
+        @pl.when(jnp.logical_not(live))
+        def _():
+            weights_out[...] = jnp.zeros(weights_out.shape, weights_out.dtype)
+
     else:
         score()
 
 
-def forward_call(offset, total, patches, words, extra):
+def forward_call(offset, total, product, patches, words, extra):
     per, patch, width = patches.shape
     lines = per * words[0].shape[1]
     shapes = (pltpu.VMEM((per, lines, patch), BF16), pltpu.VMEM((ROWS, LANES), F32))
+    if product:
+        shapes += (pltpu.VMEM((per, lines, width), F32),)
     if offset:
         meta, prior = extra
         args = near(meta, patches, prior, *words)
@@ -170,7 +185,7 @@
         specs = [spec(pltpu.SMEM)] * 3 + [spec()] * (len(args) - 3)
         shapes += (pltpu.VMEM((total // 2 + total // ROWS + 1, ROWS, LANES), F32),)
     return pl.pallas_call(
-        functools.partial(forward_kernel, offset, len(words), total),
+        functools.partial(forward_kernel, offset, len(words), total, product),
         out_shape=shapes,
         in_specs=specs,
         out_specs=(spec(),) * len(shapes),
@@ -277,12 +292,12 @@
     return (block * factor).reshape(lines, patch).astype(BF16)
 
 
-def word_kernel(group, total, meta, patches, coef, weights_a, weights_b, low_out, high_out, out_b):
-    per, patch, width = patches.shape
-    half = low_out.shape[0]
-    for n, weights in enumerate((weights_a, weights_b)):
+def word_kernel(group, total, patches, meta, coef, source_a, source_b, low_out, high_out, out_b):
+    half, tokens, width = low_out.shape
+    per = 2 * half
+    for n, source in enumerate((source_a, source_b)):
         offset = 2 * group + n
-        shape = (per, weights.shape[1] // per, width)
+        shape = (per, tokens, width)
 
         def put(value):
             if n:
@@ -292,10 +307,17 @@
                 high_out[...] = value[half:]
 
         def run():
+            if patches is None:
+                value = jnp.zeros(shape, F32)
+                for i in range(per):
+                    factor = jnp.tile(coef[offset, i, :per][:, None, :], (1, 1, width // LANES))
+                    value = value + source[i].reshape(shape) * factor
+                put(value)
+                return
             wide = jnp.concatenate(
-                [scaled(weights, coef.at[offset], i, per) for i in range(per)], axis=1
+                [scaled(source, coef.at[offset], i, per) for i in range(per)], axis=1
             )
-            rows = patches[...].reshape(per * patch, width)
+            rows = patches[...].reshape(-1, width)
             put(lax.dot_general(wide, rows, NN, preferred_element_type=F32).reshape(shape))
 
         if offset:
@@ -306,63 +328,67 @@
             run()
 
 
-def word_call(group, total, meta, patches, coef, weights_a, weights_b):
-    per, patch, width = patches.shape
-    shape = (per, weights_a.shape[1] // per, width)
-    part = (per // 2, *shape[1:])
-    return pl.pallas_call(
-        functools.partial(word_kernel, group, total),
+def word_products(group, total, meta, coef, *refs):
+    word_kernel(group, total, None, meta, coef, *refs)
+
+
+def word_blends(group, total, patches, meta, coef, *refs):
+    word_kernel(group, total, patches, meta, coef, *refs)
+
+
+def word_call(group, total, shape, meta, coef, source_a, source_b, patches=()):
+    part = (shape[0] // 2, *shape[1:])
+    return pl.pallas_call(
+        functools.partial(word_blends if patches else word_products, group, total),
         out_shape=(pltpu.VMEM(part, F32), pltpu.VMEM(part, F32), pltpu.VMEM(shape, BF16)),
-        in_specs=[spec()] * 5,
+        in_specs=[spec()] * (4 + len(patches)),
         out_specs=(spec(),) * 3,
         compiler_params=params(12),
         cost_estimate=tiny(),
         name=f"word_{group}",
-    )(*near(meta, patches, coef, weights_a, weights_b))
-
-
-def patch_kernel(total, split, meta, coef, *refs):
-    weights, words, out, acc = refs[:total], refs[total:-2], refs[-2], refs[-1]
-    per, patch, width = out.shape
-    for k in range(total):
-        pieces, words = words[: split[k]], words[split[k] :]
-
-        def add(k=k, pieces=pieces):
-            word_rows = jnp.concatenate(
-                [w[...].reshape(w.shape[0] * w.shape[1], width) for w in pieces], axis=0
-            )
-            for i in range(per):
-                part = lax.dot_general(
-                    scaled(weights[k], coef.at[k], i, per),
-                    word_rows,
-                    TN,
-                    preferred_element_type=F32,
-                )
-                if k:
-                    acc[i] += part
-                else:
-                    acc[i] = part
-
-        if k:
-            pl.when(block_is_live(meta, total, k))(add)
-        else:
-            add()
-    out[...] = acc[...].astype(BF16)
-
-
-def patch_call(meta, coef, weights, words, shape):
+    )(*near(*patches, meta, coef, source_a, source_b))
+
+
+def patch_kernel(total, start, split, coef, *refs):
+    out, result, sems = refs[-3:]
+    weights, words = refs[:total], refs[total : total + sum(split)]
+    count, patch, width = result.shape
+    per = out.shape[0]
+
+    def save(i):
+        return pltpu.make_async_copy(result.at[i], out.at[start + i], sems.at[i])
+
+    word_rows = jnp.concatenate(
+        [w[...].reshape(w.shape[0] * w.shape[1], width) for w in words], axis=0
+    )
+    for i in range(count):
+        tall = jnp.concatenate(
+            [scaled(weights[k], coef.at[k], start + i, per) for k in range(total)], axis=0
+        )
+        result[i] = lax.dot_general(tall, word_rows, TN, preferred_element_type=F32).astype(BF16)
+        save(i).start()
+    for i in range(count):
+        save(i).wait()
+
+
+def patch_call(coef, weights, words, shape, start, count, prior=()):
     total = len(weights)
     flat = [piece for pieces in words for piece in pieces]
-    return pl.pallas_call(
-        functools.partial(patch_kernel, total, tuple(len(p) for p in words)),
+    args = (*near(coef, *weights, *flat), *prior)
+    return pl.pallas_call(
+        functools.partial(patch_kernel, total, start, tuple(len(p) for p in words)),
         out_shape=jax.ShapeDtypeStruct(shape, BF16),
-        in_specs=[spec()] * (2 + total + len(flat)),
-        out_specs=spec(),
-        scratch_shapes=[pltpu.VMEM(shape, F32)],
+        in_specs=[spec()] * (1 + total + len(flat)) + [spec(pl.ANY)] * len(prior),
+        out_specs=spec(pl.ANY),
+        scratch_shapes=[
+            pltpu.VMEM((count, *shape[1:]), BF16),
+            pltpu.SemaphoreType.DMA((count,)),
+        ],
+        input_output_aliases={len(args) - 1: 0} if prior else {},
         compiler_params=params(16),
         cost_estimate=tiny(),
-        name="patch",
-    )(*near(meta, coef, *weights, *flat))
+        name=f"patch_{start}",
+    )(*args)
 
 
 def half_kernel(start, x, out):
@@ -419,26 +445,30 @@
     )(*near(*arrays))
 
 
-def finish_kernel(count, *refs):
+def total_kernel(lows, highs, *refs):
     out = refs[-1]
     half = out.shape[0] // 2
-    for n, part in enumerate((refs[:count], refs[count:-1])):
-        total = part[0][...]
+    wholes = refs[lows + highs : -1]
+    for n, part in enumerate((refs[:lows], refs[lows : lows + highs])):
+        here = slice(half * n, half * (n + 1))
+        total = part[0][...].astype(F32)
         for ref in part[1:]:
             total = total + ref[...].astype(F32)
-        out[half * n : half * (n + 1)] = total.astype(BF16)
-
-
-def finish_call(lows, highs, shape):
-    return pl.pallas_call(
-        functools.partial(finish_kernel, len(lows)),
-        out_shape=jax.ShapeDtypeStruct(shape, BF16),
-        in_specs=[spec()] * (len(lows) + len(highs)),
+        for ref in wholes:
+            total = total + ref[here].astype(F32)
+        out[here] = total.astype(out.dtype)
+
+
+def total_call(name, lows, highs, wholes, out):
+    return pl.pallas_call(
+        functools.partial(total_kernel, len(lows), len(highs)),
+        out_shape=out,
+        in_specs=[spec()] * (len(lows) + len(highs) + len(wholes)),
         out_specs=spec(),
         compiler_params=params(8),
         cost_estimate=tiny(),
-        name="finish",
-    )(*near(*lows, *highs))
+        name=name,
+    )(*near(*lows, *highs, *wholes))
 
 
 def scalar_kernel(mine, other, loss_out, temp_out):
@@ -486,7 +516,7 @@
     words_at[1] = (hop(words, 1),)
 
     meta = None
-    weights, scores = [], []
+    weights, scores, products = [], [], {}
 
     def forward(k):
         nonlocal meta
@@ -494,18 +524,19 @@
             extra = (meta, scores[-1])
         else:
             extra = (jnp.transpose(candidates, (2, 0, 1)), counts, natural_sharpness_exponent)
-        made = forward_call(k, total, patches, words_at[k], extra)
+        product = k < 2 or k // 2 in bits
+        made = forward_call(k, total, product, patches, words_at[k], extra)
         if not k:
-            meta = made[2]
+            meta = made[-1]
         weights.append(made[0])
         scores.append(made[1])
+        if product:
+            products[k] = made[2]
 
     forward(0)
     forward(1)
-    direct = [words_at[2 * b][0] for b in bits]
-    *direct, _ = barrier((*direct, scores[-1]))
-    for b, x in zip(bits, direct):
-        words_at[2 * b] = (x,)
+    for b in bits:
+        words_at[2 * b] = barrier((words_at[2 * b][0], scores[-1]))[:1]
 
     def part(g, side):
         pieces = words_at[2 * g]
@@ -524,7 +555,7 @@
     done = 2
     for g in sequence:
         if words_at[2 * g + 1] is None:
-            *pieces, _ = barrier((*words_at[2 * g], scores[-2]))
+            *pieces, _ = barrier((*words_at[2 * g], scores[-1]))
             words_at[2 * g] = tuple(pieces)
             words_at[2 * g + 1] = tuple(hop(x, 1) for x in pieces)
         forward(2 * g)
@@ -539,59 +570,75 @@
 
     lows = [[] for _ in range(groups)]
     highs = [[] for _ in range(groups)]
-    top = bits[-1] if bits else 0
-    order = sorted(range(1, groups), key=lambda g: -bin(g).count("1")) + [0]
-    waiting = []
-
-    def settle(g, low, high, sibling):
+    wholes = [[] for _ in range(groups)]
+    mixed = []
+
+    def word(g, coef):
+        if 2 * g in products:
+            sources = (products[2 * g], products[2 * g + 1])
+        else:
+            sources = (weights[2 * g], weights[2 * g + 1], (patches,))
+        low, high, theirs = word_call(g, total, words.shape, meta, coef, *sources)
+        lows[g].append(low)
+        highs[g].append(high)
+        wholes[g].append(hop(theirs, 1))
+
+    far = [g for g in range(1, groups) if g not in bits]
+    for g in sorted(far, key=lambda g: -bin(g).count("1")) + bits:
+        word(g, coef)
+    for g in far:
         low, high = join_call(
             f"join_{g}",
-            low,
-            high,
-            sibling,
+            lows[g].pop(),
+            highs[g].pop(),
+            wholes[g].pop(),
             BF16 if g & 1 else F32,
-            BF16 if g & top else F32,
+            BF16 if g & bits[-1] else F32,
         )
         lows[g].append(low)
         highs[g].append(high)
-        return low
-
-    def send(side, g, b):
-        store = (lows, highs)[side]
-        terms = store[g]
-        value = terms[0] if len(terms) == 1 else add_call(f"mix_{side}_{g}", BF16, *terms)
-        store[g ^ b].append(hop(value, 2 * b))
-
-    word_coef = coef
-    for g in order:
-        low, high, theirs = word_call(
-            g, total, meta, patches, word_coef, weights[2 * g], weights[2 * g + 1]
-        )
-        sibling = hop(theirs, 1)
-        if waiting:
-            joined = settle(*waiting.pop())
-            word_coef, _ = barrier((word_coef, joined))
-        waiting.append((g, low, high, sibling))
-    settle(*waiting.pop())
-    for b in bits:
-        for g in sorted(range(1, groups), reverse=True):
-            if low_bit(g) == b:
-                send(0, g, b)
-    for b in reversed(bits):
-        for g in sorted(range(1, groups), reverse=True):
-            if high_bit(g) == b:
-                send(1, g, b)
+    near_coef = barrier((coef, *(lows[far[-1]] if far else [])))[0]
+    word(0, near_coef)
 
     step = 1
     while 2 * step < rows:
         other = lax.ppermute(sums, "img", [(i, i ^ step) for i in range(rows)])
         sums = add_call(f"sums_{step}", F32, sums, other)
         step *= 2
+
+    def pass_on(store, g, b, name):
+        terms = store[g]
+        value = terms[0] if len(terms) == 1 else add_call(name, BF16, *terms)
+        store[g ^ b].append(hop(value, 2 * b))
+
+    for b in bits:
+        for g in reversed(far):
+            if low_bit(g) == b:
+                pass_on(lows, g, b, f"low_{g}")
+    for b in reversed(bits):
+        for g in reversed(far):
+            if high_bit(g) == b:
+                pass_on(highs, g, b, f"high_{g}")
+    block = pltpu.VMEM(words.shape, BF16)
+    for b in reversed(bits):
+        first, *rest = lows[b]
+        first, _ = barrier((first, sums))
+        value = total_call(f"mix_{b}", [first, *rest], highs[b], wholes[b], block)
+        mixed.append(value)
+        wholes[0].append(hop(value, 2 * b))
+
+    late_coef, *_ = barrier((coef, *mixed))
+    patch_grad = patch_call(late_coef, weights, words_at, patches.shape, 0, per // 2)
+    sums, patch_grad = barrier((sums, patch_grad))
     other = lax.ppermute(sums, "img", [(i, i ^ step) for i in range(rows)])
+    patch_grad = patch_call(
+        late_coef, weights, words_at, patches.shape, per // 2, per - per // 2, (patch_grad,)
+    )
+    word_grad = total_call(
+        "finish", lows[0], highs[0], wholes[0], jax.ShapeDtypeStruct(words.shape, BF16)
+    )
+    other, word_grad = barrier((other, word_grad))
     loss, temp = scalar_call(sums, other)
-
-    patch_grad = patch_call(meta, coef, weights, words_at, patches.shape)
-    word_grad = finish_call(lows[0], highs[0], words.shape)
     return patch_grad, word_grad, loss, temp
 
 

time: 67.8 us -> 71.3 us (1.052)
  Pallas kernels: 14.2 us -> 21.7 us
  starting transfers between devices: 33.2 us -> 27.4 us
  local copies, waits for them, and re-layouts: 3.79 us -> 5.2 us
    ppermute x2, starting transfers between devices: 7.08 us -> 0.07 us  [body(): other = lax.ppermute(sums, 'img', [(i, i ^ step) for i in range(rows)])]
    pallas_call x8, Pallas kernels: 6.22 us -> 13.2 us  [forward_call(): pl.pallas_call(functools.partial(forward_kernel, offset, len(words), tota...]
    ppermute x2, waiting for transfers between devices: 1.59 us -> 3.61 us  [body(): other = lax.ppermute(sums, 'img', [(i, i ^ step) for i in range(rows)])]
    ppermute x23 -> x21, waiting for transfers between devices: 13.5 us -> 11.7 us  [hop(): return lax.ppermute(x, 'cap', [(i, i ^ offset) for i in range(total)])]
    unnamed x12, local copies, waits for them, and re-layouts: 3.79 us -> 5.2 us
    ppermute x23 -> x21, starting transfers between devices: 26.1 us -> 27.3 us  [hop(): return lax.ppermute(x, 'cap', [(i, i ^ offset) for i in range(total)])]
    pallas_call x6 -> x9, Pallas kernels: 6.67 us -> 7.55 us  [the longest x2 5.2 us: patch_call(): pl.pallas_call(functools.partial(patch_kernel, total, start, tuple((len(p...]
  transfers between devices with their start and end apart: 25 -> 23, of which waited for: 13 -> 13; matrix products, arithmetic and copies ran while one was open for 0% -> 0% of each run, Pallas kernels for 19% -> 29%
where the time goes in v3:
time: 71.3 us; the launch traced here: 71.4 us
  starting transfers between devices  27.4 us (38%)
  Pallas kernels  21.7 us (30%)
  waiting for transfers between devices  15.3 us (21%)
  local copies, waits for them, and re-layouts  5.2 us (7%)
  between operations  1.73 us (2%)
    ppermute x21, starting transfers between devices, hop(): return lax.ppermute(x, 'cap', [(i, i ^ offset) for i in range(total)])  27.3 us
    pallas_call x8, Pallas kernels, forward_call(): pl.pallas_call(functools.partial(forward_kernel, offset, len(words), tota...  13.2 us
    ppermute x21, waiting for transfers between devices, hop(): return lax.ppermute(x, 'cap', [(i, i ^ offset) for i in range(total)])  11.7 us
    pallas_call x2, Pallas kernels, patch_call(): pl.pallas_call(functools.partial(patch_kernel, total, start, tuple((len(p...  5.2 us
    unnamed x12, local copies, waits for them, and re-layouts  5.2 us
    ppermute x2, waiting for transfers between devices, body(): other = lax.ppermute(sums, 'img', [(i, i ^ step) for i in range(rows)])  3.61 us
  transfers between devices with their start and end apart: 23, of which 13 were waited for; matrix products, arithmetic and copies ran while one was open for 0% of the time, Pallas kernels for 29%

profile of v3, /device:TPU:0, one launch (start us, length us, event | category | flops | bytes accessed | tf_op | source)
XLA Modules:
  0.0 71.4 jit_solution(17872790561513611460)
XLA Ops:
  0.6 0.5 collective-permute-start
  1.1 2.6 %collective-permute-start.1 = (bf16[4,64,768]{2,1,0:T(8,128)(2,1)}, bf16[4,64,768]{2,1,0:T(8,128)(2,1)S(1)}, u32[]{:S(2)}, u32[]{:S(2)}) collective-permute-start(bf16[4,64,768]{2,1,0:T(8,128)(2,1)} %refs_8_.3), channel_id=1, source_target_pairs={{0,2},{1,3},{2,0},{3,1},{4,6},{5,7},{6,4},{7,5},{8,10},{9,11},{10,... | collective-permute-start | bytes 1179656 | tf_op jit(solution)/shard_map/ppermute | solution.py:510
  3.7 1.5 %collective-permute-start.3 = (bf16[4,64,768]{2,1,0:T(8,128)(2,1)}, bf16[4,64,768]{2,1,0:T(8,128)(2,1)S(1)}, u32[]{:S(2)}, u32[]{:S(2)}) collective-permute-start(bf16[4,64,768]{2,1,0:T(8,128)(2,1)} %refs_8_.3), channel_id=1, source_target_pairs={{0,4},{1,5},{2,6},{3,7},{4,0},{5,1},{6,2},{7,3},{8,12},{9,13},{10,... | collective-permute-start | bytes 1179656 | tf_op jit(solution)/shard_map/ppermute | solution.py:510
  5.9 1.4 %copy-done = bf16[4,256,768]{2,1,0:T(8,128)(2,1)S(1)} copy-done((bf16[4,256,768]{2,1,0:T(8,128)(2,1)S(1)}, bf16[4,256,768]{2,1,0:T(8,128)(2,1)}, u32[]{:S(2)}) %copy-start) | copy-done | bytes 1572888
  7.3 1.0 %copy-done.2 = bf16[4,64,768]{2,1,0:T(8,128)(2,1)S(1)} copy-done((bf16[4,64,768]{2,1,0:T(8,128)(2,1)S(1)}, bf16[4,64,768]{2,1,0:T(8,128)(2,1)}, u32[]{:S(2)}) %copy-start.2) | copy-done | bytes 393240
  8.3 0.7 copy-done.4
  9.0 0.7 copy-done.5
  9.7 4.7 %forward_0.1 = (bf16[4,256,256]{2,1,0:T(8,128)(2,1)S(1)}, f32[8,128]{1,0:T(8,128)S(1)}, f32[4,256,768]{2,1,0:T(8,128)S(1)}, f32[6,8,128]{2,1,0:T(8,128)S(1)}) custom-call(s32[6,4,8]{2,1,0:T(4,128)S(1)} %bitcast.1, s32[4,8]{1,0:T(4,128)S(1)} %copy-done.5, f32[1]{0:T(128)S(6)} %copy.11.refs_2_, bf16[4,256,768]{2,1,0:T(8,128)(2,1)S(1)} %copy-done, ...), custom_call_target="tpu_custom_call" | custom-call | flops 1 | bytes 1 | tf_op jit(solution)/shard_map/forward_0/pallas_call | solution.py:187
  14.4 1.4 %copy-done.1 = bf16[4,256,768]{2,1,0:T(8,128)(2,1)S(1)} copy-done((bf16[4,256,768]{2,1,0:T(8,128)(2,1)S(1)}, bf16[4,256,768]{2,1,0:T(8,128)(2,1)}, u32[]{:S(2)}) %copy-start.1) | copy-done | bytes 1572888
  15.8 4.0 %forward_1.1 = (bf16[4,256,256]{2,1,0:T(8,128)(2,1)S(1)}, f32[8,128]{1,0:T(8,128)S(1)}, f32[4,256,768]{2,1,0:T(8,128)S(1)}) custom-call(f32[6,8,128]{2,1,0:T(8,128)S(1)} %get-tuple-element.57.refs_0_.meta, bf16[4,256,768]{2,1,0:T(8,128)(2,1)S(1)} %copy-done.1, f32[8,128]{1,0:T(8,128)S(1)} %get-tuple-element.58.refs_2_, ...), custom_call_target="tpu_custom_call" | custom-call | flops 1 | bytes 1 | tf_op jit(solution)/shard_map/forward_1/pallas_call | solution.py:187
  19.9 0.5 collective-permute-start.4
  20.7 0.9 %collective-permute-done.2.refs_3_.refs_11_ = bf16[4,64,768]{2,1,0:T(8,128)(2,1)S(1)} collective-permute-done((bf16[4,64,768]{2,1,0:T(8,128)(2,1)S(1)}, bf16[4,64,768]{2,1,0:T(8,128)(2,1)S(1)}, u32[]{:S(2)}, u32[]{:S(2)}) %collective-permute-start.2) | collective-permute-done | bytes 393248 | tf_op jit(solution)/shard_map/ppermute | solution.py:510
  21.6 4.0 %forward_3.1 = (bf16[4,256,256]{2,1,0:T(8,128)(2,1)S(1)}, f32[8,128]{1,0:T(8,128)S(1)}, f32[4,256,768]{2,1,0:T(8,128)S(1)}) custom-call(f32[6,8,128]{2,1,0:T(8,128)S(1)} %get-tuple-element.57.refs_0_.meta, bf16[4,256,768]{2,1,0:T(8,128)(2,1)S(1)} %copy-done.1, f32[8,128]{1,0:T(8,128)S(1)} %get-tuple-element.61.refs_2_, ...), custom_call_target="tpu_custom_call" | custom-call | flops 1 | bytes 1 | tf_op jit(solution)/shard_map/forward_3/pallas_call | solution.py:187
  25.7 1.6 %collective-permute-done.6.refs_4_.refs_15_ = bf16[2,64,768]{2,1,0:T(8,128)(2,1)S(1)} collective-permute-done((bf16[2,64,768]{2,1,0:T(8,128)(2,1)S(1)}, bf16[2,64,768]{2,1,0:T(8,128)(2,1)S(1)}, u32[]{:S(2)}, u32[]{:S(2)}) %collective-permute-start.6) | collective-permute-done | bytes 196640 | tf_op jit(solution)/shard_map/ppermute | solution.py:510
  27.4 0.1 collective-permute-done.5.refs_3_.refs_14_
  27.5 2.4 %collective-permute-start.7 = (bf16[2,64,768]{2,1,0:T(8,128)(2,1)S(1)}, bf16[2,64,768]{2,1,0:T(8,128)(2,1)S(1)}, u32[]{:S(2)}, u32[]{:S(2)}) collective-permute-start(bf16[2,64,768]{2,1,0:T(8,128)(2,1)S(1)} %collective-permute-done.5.refs_3_.refs_14_), channel_id=1, source_target_pairs={{0,1},{1,0},{2,3},{3,2},{4,5},{5,4},{6,7},{7,6},{8,9},{9,8},{10,11... | collective-permute-start | bytes 589832 | tf_op jit(solution)/shard_map/ppermute | solution.py:510
  30.0 0.9 %collective-permute-done.7.refs_3_.refs_16_ = bf16[2,64,768]{2,1,0:T(8,128)(2,1)S(1)} collective-permute-done((bf16[2,64,768]{2,1,0:T(8,128)(2,1)S(1)}, bf16[2,64,768]{2,1,0:T(8,128)(2,1)S(1)}, u32[]{:S(2)}, u32[]{:S(2)}) %collective-permute-start.7) | collective-permute-done | bytes 196640 | tf_op jit(solution)/shard_map/ppermute | solution.py:510
  30.9 0.4 collective-permute-done.8.refs_4_.refs_17_
  31.3 0.3 forward_7.1
  31.6 0.3 collective-permute-start.9
  31.9 0.9 %collective-permute-done.9.other = f32[8,128]{1,0:T(8,128)S(1)} collective-permute-done((f32[8,128]{1,0:T(8,128)S(1)}, f32[8,128]{1,0:T(8,128)S(1)}, u32[]{:S(2)}, u32[]{:S(2)}) %collective-permute-start.9) | collective-permute-done | bytes 4128 | tf_op jit(solution)/shard_map/ppermute | solution.py:510
  32.8 11.2 %collective-permute-start.12 = (f32[8,128]{1,0:T(8,128)S(1)}, f32[8,128]{1,0:T(8,128)S(1)}, u32[]{:S(2)}, u32[]{:S(2)}) collective-permute-start(f32[8,128]{1,0:T(8,128)S(1)} %pair.1.refs_0_), channel_id=1, source_target_pairs={{0,6},{1,7},{2,4},{3,5},{4,2},{5,3},{6,0},{7,1},{8,14},{9,15},{10,... | collective-permute-start | bytes 12296 | tf_op jit(solution)/shard_map/ppermute | solution.py:510
  44.0 0.3 collective-permute-start.11
  44.3 0.7 collective-permute-start.10
  45.0 0.6 collective-permute-done.12.refs_3_
  45.6 2.0 %collective-permute-done.11.refs_2_ = f32[8,128]{1,0:T(8,128)S(1)} collective-permute-done((f32[8,128]{1,0:T(8,128)S(1)}, f32[8,128]{1,0:T(8,128)S(1)}, u32[]{:S(2)}, u32[]{:S(2)}) %collective-permute-start.11) | collective-permute-done | bytes 4128 | tf_op jit(solution)/shard_map/ppermute | solution.py:510
  47.6 0.3 collective-permute-done.10.refs_1_
  47.9 0.3 stats.1
  48.2 0.2 word_3.1
  48.5 0.2 word_2.1
  48.7 0.7 collective-permute-start.16
  49.4 0.3 word_1.1
  49.7 0.1 collective-permute-start.18
  49.8 0.4 collective-permute-done.14.sibling
  50.3 0.7 %collective-permute-start.15 = (bf16[2,64,768]{2,1,0:T(8,128)(2,1)S(1)}, bf16[2,64,768]{2,1,0:T(8,128)(2,1)S(1)}, u32[]{:S(2)}, u32[]{:S(2)}) collective-permute-start(bf16[2,64,768]{2,1,0:T(8,128)(2,1)S(1)} %get-tuple-element.81), channel_id=1, source_target_pairs={{0,2},{1,3},{2,0},{3,1},{4,6},{5,7},{6,4},{7,5},{8,10},{9,11},{10,... | collective-permute-start | bytes 589832 | tf_op jit(solution)/shard_map/ppermute | solution.py:510
  51.0 2.5 %collective-permute-start.17 = (bf16[2,64,768]{2,1,0:T(8,128)(2,1)S(1)}, bf16[2,64,768]{2,1,0:T(8,128)(2,1)S(1)}, u32[]{:S(2)}, u32[]{:S(2)}) collective-permute-start(bf16[2,64,768]{2,1,0:T(8,128)(2,1)S(1)} %get-tuple-element.89), channel_id=1, source_target_pairs={{0,4},{1,5},{2,6},{3,7},{4,0},{5,1},{6,2},{7,3},{8,12},{9,13},{10,... | collective-permute-start | bytes 589832 | tf_op jit(solution)/shard_map/ppermute | solution.py:510
  53.5 3.6 %collective-permute-done.13.refs_1_ = f32[8,128]{1,0:T(8,128)S(1)} collective-permute-done((f32[8,128]{1,0:T(8,128)S(1)}, f32[8,128]{1,0:T(8,128)S(1)}, u32[]{:S(2)}, u32[]{:S(2)}) %collective-permute-start.13) | collective-permute-done | bytes 4128 | tf_op jit(solution)/shard_map/ppermute | solution.py:605
  57.1 0.6 word_0.1
  57.9 0.1 mix_2.1
  58.0 1.3 %collective-permute-start.21 = (bf16[4,64,768]{2,1,0:T(8,128)(2,1)S(1)}, bf16[4,64,768]{2,1,0:T(8,128)(2,1)S(1)}, u32[]{:S(2)}, u32[]{:S(2)}) collective-permute-start(bf16[4,64,768]{2,1,0:T(8,128)(2,1)S(1)} %mix_2.1), channel_id=1, source_target_pairs={{0,4},{1,5},{2,6},{3,7},{4,0},{5,1},{6,2},{7,3},{8,12},{9,13},{10,... | collective-permute-start | bytes 1179656 | tf_op jit(solution)/shard_map/ppermute | solution.py:510
  59.2 0.1 mix_1.1
  59.3 1.6 %collective-permute-start.22 = (bf16[4,64,768]{2,1,0:T(8,128)(2,1)S(1)}, bf16[4,64,768]{2,1,0:T(8,128)(2,1)S(1)}, u32[]{:S(2)}, u32[]{:S(2)}) collective-permute-start(bf16[4,64,768]{2,1,0:T(8,128)(2,1)S(1)} %mix_1.1), channel_id=1, source_target_pairs={{0,2},{1,3},{2,0},{3,1},{4,6},{5,7},{6,4},{7,5},{8,10},{9,11},{10,... | collective-permute-start | bytes 1179656 | tf_op jit(solution)/shard_map/ppermute | solution.py:510
  60.9 2.6 %patch_0.1.refs_18_ = bf16[4,256,768]{2,1,0:T(8,128)(2,1)} custom-call(f32[8,4,8,128]{3,2,1,0:T(8,128)S(1)} %get-tuple-element.100.coef, bf16[4,256,256]{2,1,0:T(8,128)(2,1)S(1)} %get-tuple-element.92.refs_0_, bf16[4,256,256]{2,1,0:T(8,128)(2,1)S(1)} %get-tuple-element.93.refs_1_, bf16[4,256,256]{2,1,0:T(8,128)(2,1)S(1)} %get-tuple-element.94.refs_2_, ...), custom_call_target="tpu_custom_call" | custom-call | flops 1 | bytes 1 | tf_op jit(solution)/shard_map/patch_0/pallas_call | solution.py:378
  63.6 2.6 %patch_2.1 = bf16[4,256,768]{2,1,0:T(8,128)(2,1)} custom-call(f32[8,4,8,128]{3,2,1,0:T(8,128)S(1)} %get-tuple-element.100.coef, bf16[4,256,256]{2,1,0:T(8,128)(2,1)S(1)} %get-tuple-element.92.refs_0_, bf16[4,256,256]{2,1,0:T(8,128)(2,1)S(1)} %get-tuple-element.93.refs_1_, ...), custom_call_target="tpu_custom_call", output_to_operand_aliasing={{}: (19, {})} | custom-call | flops 1 | bytes 1 | tf_op jit(solution)/shard_map/patch_2/pallas_call | solution.py:378
  66.2 3.3 %collective-permute-done.21.refs_3_ = bf16[4,64,768]{2,1,0:T(8,128)(2,1)S(1)} collective-permute-done((bf16[4,64,768]{2,1,0:T(8,128)(2,1)S(1)}, bf16[4,64,768]{2,1,0:T(8,128)(2,1)S(1)}, u32[]{:S(2)}, u32[]{:S(2)}) %collective-permute-start.21) | collective-permute-done | bytes 393248 | tf_op jit(solution)/shard_map/ppermute | solution.py:510
  69.5 0.2 collective-permute-done.22.refs_4_
  69.7 0.9 %finish.1 = bf16[4,64,768]{2,1,0:T(8,128)(2,1)} custom-call(f32[2,64,768]{2,1,0:T(8,128)S(1)} %get-tuple-element.103.refs_0_, f32[2,64,768]{2,1,0:T(8,128)S(1)} %get-tuple-element.104.refs_1_, bf16[4,64,768]{2,1,0:T(8,128)(2,1)S(1)} %collective-permute-done.20.refs_2_, bf16[4,64,768]{2,1,0:T(8,128)(2,1)S(1)} %collective-permute-done.21.refs_3_, ...), custom_call_target="tpu_custom_call" | custom-call | flops 1 | bytes 1 | tf_op jit(solution)/shard_map/finish/pallas_call | solution.py:463
  70.7 0.6 scalars.1
  (34 shorter events, 1.0 us)
Async XLA Ops:
  0.6 13.8 %collective-permute-start = (bf16[4,64,768]{2,1,0:T(8,128)(2,1)}, bf16[4,64,768]{2,1,0:T(8,128)(2,1)S(1)}, u32[]{:S(2)}, u32[]{:S(2)}) collective-permute-start(bf16[4,64,768]{2,1,0:T(8,128)(2,1)} %refs_8_.3), channel_id=1, source_target_pairs={{0,1},{1,0},{2,3},{3,2},{4,5},{5,4},{6,7},{7,6},{8,9},{9,8},{10,11... | collective-permute-start | bytes 1179656 | tf_op jit(solution)/shard_map/ppermute | solution.py:510
  1.1 18.6 %collective-permute-start.1 = (bf16[4,64,768]{2,1,0:T(8,128)(2,1)}, bf16[4,64,768]{2,1,0:T(8,128)(2,1)S(1)}, u32[]{:S(2)}, u32[]{:S(2)}) collective-permute-start(bf16[4,64,768]{2,1,0:T(8,128)(2,1)} %refs_8_.3), channel_id=1, source_target_pairs={{0,2},{1,3},{2,0},{3,1},{4,6},{5,7},{6,4},{7,5},{8,10},{9,11},{10,... | collective-permute-start | bytes 1179656 | tf_op jit(solution)/shard_map/ppermute | solution.py:510
  3.7 16.2 %collective-permute-start.3 = (bf16[4,64,768]{2,1,0:T(8,128)(2,1)}, bf16[4,64,768]{2,1,0:T(8,128)(2,1)S(1)}, u32[]{:S(2)}, u32[]{:S(2)}) collective-permute-start(bf16[4,64,768]{2,1,0:T(8,128)(2,1)} %refs_8_.3), channel_id=1, source_target_pairs={{0,4},{1,5},{2,6},{3,7},{4,0},{5,1},{6,2},{7,3},{8,12},{9,13},{10,... | collective-permute-start | bytes 1179656 | tf_op jit(solution)/shard_map/ppermute | solution.py:510
  5.9 1.4 %copy-start = (bf16[4,256,768]{2,1,0:T(8,128)(2,1)S(1)}, bf16[4,256,768]{2,1,0:T(8,128)(2,1)}, u32[]{:S(2)}) copy-start(bf16[4,256,768]{2,1,0:T(8,128)(2,1)} %patches.1) | copy-start | bytes 4718596
  7.3 1.0 %copy-start.2 = (bf16[4,64,768]{2,1,0:T(8,128)(2,1)S(1)}, bf16[4,64,768]{2,1,0:T(8,128)(2,1)}, u32[]{:S(2)}) copy-start(bf16[4,64,768]{2,1,0:T(8,128)(2,1)} %refs_8_.3) | copy-start | bytes 1179652
  8.3 0.7 copy-start.4
  9.0 0.7 copy-start.5
  14.4 1.4 %copy-start.1 = (bf16[4,256,768]{2,1,0:T(8,128)(2,1)S(1)}, bf16[4,256,768]{2,1,0:T(8,128)(2,1)}, u32[]{:S(2)}) copy-start(bf16[4,256,768]{2,1,0:T(8,128)(2,1)} %patches.1) | copy-start | bytes 4718596
  19.8 1.8 %collective-permute-start.2 = (bf16[4,64,768]{2,1,0:T(8,128)(2,1)S(1)}, bf16[4,64,768]{2,1,0:T(8,128)(2,1)S(1)}, u32[]{:S(2)}, u32[]{:S(2)}) collective-permute-start(bf16[4,64,768]{2,1,0:T(8,128)(2,1)S(1)} %collective-permute-done.1.refs_3_.x.refs_10_), channel_id=1, source_target_pairs={{0,1},{1,0},{2,3},{3,2},{4,5},{5,4},{6,7},{7,6},{8,9},{9,8},{10,11... | collective-permute-start | bytes 1179656 | tf_op jit(solution)/shard_map/ppermute | solution.py:510
  19.9 5.8 %collective-permute-start.4 = (bf16[4,64,768]{2,1,0:T(8,128)(2,1)S(1)}, bf16[4,64,768]{2,1,0:T(8,128)(2,1)S(1)}, u32[]{:S(2)}, u32[]{:S(2)}) collective-permute-start(bf16[4,64,768]{2,1,0:T(8,128)(2,1)S(1)} %collective-permute-done.3.refs_3_.x.refs_12_), channel_id=1, source_target_pairs={{0,1},{1,0},{2,3},{3,2},{4,5},{5,4},{6,7},{7,6},{8,9},{9,8},{10,11... | collective-permute-start | bytes 1179656 | tf_op jit(solution)/shard_map/ppermute | solution.py:510
  20.4 7.0 %collective-permute-start.6 = (bf16[2,64,768]{2,1,0:T(8,128)(2,1)S(1)}, bf16[2,64,768]{2,1,0:T(8,128)(2,1)S(1)}, u32[]{:S(2)}, u32[]{:S(2)}) collective-permute-start(bf16[2,64,768]{2,1,0:T(8,128)(2,1)S(1)} %half_2.1), channel_id=1, source_target_pairs={{0,2},{1,3},{2,0},{3,1},{4,6},{5,7},{6,4},{7,5},{8,10},{9,11},{10,... | collective-permute-start | bytes 589832 | tf_op jit(solution)/shard_map/ppermute | solution.py:510
  20.5 7.0 %collective-permute-start.5 = (bf16[2,64,768]{2,1,0:T(8,128)(2,1)S(1)}, bf16[2,64,768]{2,1,0:T(8,128)(2,1)S(1)}, u32[]{:S(2)}, u32[]{:S(2)}) collective-permute-start(bf16[2,64,768]{2,1,0:T(8,128)(2,1)S(1)} %half_0.1), channel_id=1, source_target_pairs={{0,4},{1,5},{2,6},{3,7},{4,0},{5,1},{6,2},{7,3},{8,12},{9,13},{10,... | collective-permute-start | bytes 589832 | tf_op jit(solution)/shard_map/ppermute | solution.py:510
  27.5 3.5 %collective-permute-start.7 = (bf16[2,64,768]{2,1,0:T(8,128)(2,1)S(1)}, bf16[2,64,768]{2,1,0:T(8,128)(2,1)S(1)}, u32[]{:S(2)}, u32[]{:S(2)}) collective-permute-start(bf16[2,64,768]{2,1,0:T(8,128)(2,1)S(1)} %collective-permute-done.5.refs_3_.refs_14_), channel_id=1, source_target_pairs={{0,1},{1,0},{2,3},{3,2},{4,5},{5,4},{6,7},{7,6},{8,9},{9,8},{10,11... | collective-permute-start | bytes 589832 | tf_op jit(solution)/shard_map/ppermute | solution.py:510
  29.9 1.4 %collective-permute-start.8 = (bf16[2,64,768]{2,1,0:T(8,128)(2,1)S(1)}, bf16[2,64,768]{2,1,0:T(8,128)(2,1)S(1)}, u32[]{:S(2)}, u32[]{:S(2)}) collective-permute-start(bf16[2,64,768]{2,1,0:T(8,128)(2,1)S(1)} %collective-permute-done.6.refs_4_.refs_15_), channel_id=1, source_target_pairs={{0,1},{1,0},{2,3},{3,2},{4,5},{5,4},{6,7},{7,6},{8,9},{9,8},{10,11... | collective-permute-start | bytes 589832 | tf_op jit(solution)/shard_map/ppermute | solution.py:510
  31.6 1.2 %collective-permute-start.9 = (f32[8,128]{1,0:T(8,128)S(1)}, f32[8,128]{1,0:T(8,128)S(1)}, u32[]{:S(2)}, u32[]{:S(2)}) collective-permute-start(f32[8,128]{1,0:T(8,128)S(1)} %get-tuple-element.69.own), channel_id=1, source_target_pairs={{0,1},{1,0},{2,3},{3,2},{4,5},{5,4},{6,7},{7,6},{8,9},{9,8},{10,11... | collective-permute-start | bytes 12296 | tf_op jit(solution)/shard_map/ppermute | solution.py:510
  32.8 12.8 %collective-permute-start.12 = (f32[8,128]{1,0:T(8,128)S(1)}, f32[8,128]{1,0:T(8,128)S(1)}, u32[]{:S(2)}, u32[]{:S(2)}) collective-permute-start(f32[8,128]{1,0:T(8,128)S(1)} %pair.1.refs_0_), channel_id=1, source_target_pairs={{0,6},{1,7},{2,4},{3,5},{4,2},{5,3},{6,0},{7,1},{8,14},{9,15},{10,... | collective-permute-start | bytes 12296 | tf_op jit(solution)/shard_map/ppermute | solution.py:510
  44.0 3.6 %collective-permute-start.11 = (f32[8,128]{1,0:T(8,128)S(1)}, f32[8,128]{1,0:T(8,128)S(1)}, u32[]{:S(2)}, u32[]{:S(2)}) collective-permute-start(f32[8,128]{1,0:T(8,128)S(1)} %pair.1.refs_0_), channel_id=1, source_target_pairs={{0,4},{1,5},{2,6},{3,7},{4,0},{5,1},{6,2},{7,3},{8,12},{9,13},{10,... | collective-permute-start | bytes 12296 | tf_op jit(solution)/shard_map/ppermute | solution.py:510
  44.3 3.6 %collective-permute-start.10 = (f32[8,128]{1,0:T(8,128)S(1)}, f32[8,128]{1,0:T(8,128)S(1)}, u32[]{:S(2)}, u32[]{:S(2)}) collective-permute-start(f32[8,128]{1,0:T(8,128)S(1)} %pair.1.refs_0_), channel_id=1, source_target_pairs={{0,2},{1,3},{2,0},{3,1},{4,6},{5,7},{6,4},{7,5},{8,10},{9,11},{10,... | collective-permute-start | bytes 12296 | tf_op jit(solution)/shard_map/ppermute | solution.py:510
  48.4 1.8 %collective-permute-start.14 = (bf16[4,64,768]{2,1,0:T(8,128)(2,1)S(1)}, bf16[4,64,768]{2,1,0:T(8,128)(2,1)S(1)}, u32[]{:S(2)}, u32[]{:S(2)}) collective-permute-start(bf16[4,64,768]{2,1,0:T(8,128)(2,1)S(1)} %get-tuple-element.80), channel_id=1, source_target_pairs={{0,1},{1,0},{2,3},{3,2},{4,5},{5,4},{6,7},{7,6},{8,9},{9,8},{10,11... | collective-permute-start | bytes 1179656 | tf_op jit(solution)/shard_map/ppermute | solution.py:510
  48.7 9.2 %collective-permute-start.16 = (bf16[4,64,768]{2,1,0:T(8,128)(2,1)S(1)}, bf16[4,64,768]{2,1,0:T(8,128)(2,1)S(1)}, u32[]{:S(2)}, u32[]{:S(2)}) collective-permute-start(bf16[4,64,768]{2,1,0:T(8,128)(2,1)S(1)} %get-tuple-element.83), channel_id=1, source_target_pairs={{0,1},{1,0},{2,3},{3,2},{4,5},{5,4},{6,7},{7,6},{8,9},{9,8},{10,11... | collective-permute-start | bytes 1179656 | tf_op jit(solution)/shard_map/ppermute | solution.py:510
  49.7 9.6 %collective-permute-start.18 = (bf16[4,64,768]{2,1,0:T(8,128)(2,1)S(1)}, bf16[4,64,768]{2,1,0:T(8,128)(2,1)S(1)}, u32[]{:S(2)}, u32[]{:S(2)}) collective-permute-start(bf16[4,64,768]{2,1,0:T(8,128)(2,1)S(1)} %get-tuple-element.90), channel_id=1, source_target_pairs={{0,1},{1,0},{2,3},{3,2},{4,5},{5,4},{6,7},{7,6},{8,9},{9,8},{10,11... | collective-permute-start | bytes 1179656 | tf_op jit(solution)/shard_map/ppermute | solution.py:510
  50.3 7.6 %collective-permute-start.15 = (bf16[2,64,768]{2,1,0:T(8,128)(2,1)S(1)}, bf16[2,64,768]{2,1,0:T(8,128)(2,1)S(1)}, u32[]{:S(2)}, u32[]{:S(2)}) collective-permute-start(bf16[2,64,768]{2,1,0:T(8,128)(2,1)S(1)} %get-tuple-element.81), channel_id=1, source_target_pairs={{0,2},{1,3},{2,0},{3,1},{4,6},{5,7},{6,4},{7,5},{8,10},{9,11},{10,... | collective-permute-start | bytes 589832 | tf_op jit(solution)/shard_map/ppermute | solution.py:510
  51.0 8.2 %collective-permute-start.17 = (bf16[2,64,768]{2,1,0:T(8,128)(2,1)S(1)}, bf16[2,64,768]{2,1,0:T(8,128)(2,1)S(1)}, u32[]{:S(2)}, u32[]{:S(2)}) collective-permute-start(bf16[2,64,768]{2,1,0:T(8,128)(2,1)S(1)} %get-tuple-element.89), channel_id=1, source_target_pairs={{0,4},{1,5},{2,6},{3,7},{4,0},{5,1},{6,2},{7,3},{8,12},{9,13},{10,... | collective-permute-start | bytes 589832 | tf_op jit(solution)/shard_map/ppermute | solution.py:510
  53.5 3.6 %collective-permute-start.13 = (f32[8,128]{1,0:T(8,128)S(1)}, f32[8,128]{1,0:T(8,128)S(1)}, u32[]{:S(2)}, u32[]{:S(2)}) collective-permute-start(f32[8,128]{1,0:T(8,128)S(1)} %get-tuple-element.74.refs_0_), channel_id=1, source_target_pairs={{0,8},{8,0},{16,24},{24,16},{1,9},{9,1},{17,25},{25,17},{2,10},{10... | collective-permute-start | bytes 12296 | tf_op jit(solution)/shard_map/ppermute | solution.py:605
  57.8 3.2 %copy-start.3 = (bf16[4,64,768]{2,1,0:T(8,128)(2,1)S(1)}, bf16[4,64,768]{2,1,0:T(8,128)(2,1)}, u32[]{:S(2)}) copy-start(bf16[4,64,768]{2,1,0:T(8,128)(2,1)} %refs_8_.3) | copy-start | bytes 1179652
  57.8 8.4 %collective-permute-start.20 = (bf16[4,64,768]{2,1,0:T(8,128)(2,1)S(1)}, bf16[4,64,768]{2,1,0:T(8,128)(2,1)S(1)}, u32[]{:S(2)}, u32[]{:S(2)}) collective-permute-start(bf16[4,64,768]{2,1,0:T(8,128)(2,1)S(1)} %get-tuple-element.105), channel_id=1, source_target_pairs={{0,1},{1,0},{2,3},{3,2},{4,5},{5,4},{6,7},{7,6},{8,9},{9,8},{10,11... | collective-permute-start | bytes 1179656 | tf_op jit(solution)/shard_map/ppermute | solution.py:510
  58.0 11.6 %collective-permute-start.21 = (bf16[4,64,768]{2,1,0:T(8,128)(2,1)S(1)}, bf16[4,64,768]{2,1,0:T(8,128)(2,1)S(1)}, u32[]{:S(2)}, u32[]{:S(2)}) collective-permute-start(bf16[4,64,768]{2,1,0:T(8,128)(2,1)S(1)} %mix_2.1), channel_id=1, source_target_pairs={{0,4},{1,5},{2,6},{3,7},{4,0},{5,1},{6,2},{7,3},{8,12},{9,13},{10,... | collective-permute-start | bytes 1179656 | tf_op jit(solution)/shard_map/ppermute | solution.py:510
  59.3 10.4 %collective-permute-start.22 = (bf16[4,64,768]{2,1,0:T(8,128)(2,1)S(1)}, bf16[4,64,768]{2,1,0:T(8,128)(2,1)S(1)}, u32[]{:S(2)}, u32[]{:S(2)}) collective-permute-start(bf16[4,64,768]{2,1,0:T(8,128)(2,1)S(1)} %mix_1.1), channel_id=1, source_target_pairs={{0,2},{1,3},{2,0},{3,1},{4,6},{5,7},{6,4},{7,5},{8,10},{9,11},{10,... | collective-permute-start | bytes 1179656 | tf_op jit(solution)/shard_map/ppermute | solution.py:510
  63.5 7.1 %collective-permute-start.19 = (f32[8,128]{1,0:T(8,128)S(1)}, f32[8,128]{1,0:T(8,128)S(1)}, u32[]{:S(2)}, u32[]{:S(2)}) collective-permute-start(f32[8,128]{1,0:T(8,128)S(1)} %sums_1.1.mine), channel_id=1, source_target_pairs={{0,16},{8,24},{16,0},{24,8},{1,17},{9,25},{17,1},{25,9},{2,18},{10... | collective-permute-start | bytes 12296 | tf_op jit(solution)/shard_map/ppermute | solution.py:633
